TPU v7x, 1024 devices: a whole 4x4x32 slice. The times are simulated.
1024 devices in a mesh: group: 8 (over y, core), dx: 16 (over z_hi, x), dy: 8 (over z_lo).
Axes of the slice: x: 4, y: 4, z: 32 (z_hi: 4, z_lo: 8; z = z_hi * 8 + z_lo), core: 2. Of those that a mesh axis runs over, the one named last changes fastest.
Arguments:
- tracers: float32 [64, 32, 128, 1024], P('group', None, 'dx', 'dy'), may hold values from -4 to 4
- reaction: float32 [64, 8], P('group'), may hold values from -0.2 to 0.2
- velocity: float32 [3, 32, 128, 1024], P(None, 'group', 'dx', 'dy'), may hold values from -6 to 6
- thickness: float32 [32, 128, 1024], P('group', 'dx', 'dy'), may hold values from 0.4 to 1
- sea_mask: int32 [128, 1024], P('dx', 'dy'), may hold values 0 or 1
- bottom: int32 [128, 1024], P('dx', 'dy'), may hold values from 1 to 32
- diffusivity: float32 [32, 128, 1024], P(None, 'dx', 'dy'), may hold values from 0.05 to 5
Outputs:
- tracers_out: float32 [64, 32, 128, 1024], P('group', None, 'dx', 'dy')
All inputs are finite; a program needn't handle non-finite values. No bound on the sum of `sea_mask` on one device may be relied on, other than what follows from the above.
Results may differ from a plain program's by a relative error of at most 0.0003.
Values sent between devices are 32-bit elements; how exact they have to be, the bound alone decides.
No kernel may reach another device: no remote copies, remote signals or barrier semaphores. Data moves between devices by JAX's collectives and lax.ppermute only.
A program may use at most 64 MiB of HBM per device.

v0:
```python
import jax
import jax.numpy as jnp
from jax import lax
from jax.sharding import PartitionSpec as P

TSTEPS = 2


def with_halo(block, sides, width):
    for axis, dim in sides:
        count = lax.axis_size(axis)
        forward = [(i, i + 1) for i in range(count - 1)]
        backward = [(target, source) for source, target in forward]
        low = lax.ppermute(
            lax.slice_in_dim(block, block.shape[dim] - width, None, axis=dim), axis, forward
        )
        high = lax.ppermute(lax.slice_in_dim(block, 0, width, axis=dim), axis, backward)
        block = jnp.concatenate([low, block, high], axis=dim)
    return block


def take_run(values, offset, length, along_dim):
    return lax.slice_in_dim(values, offset, offset + length, axis=values.ndim + along_dim)


def face_fluxes(padded, courant, along_dim, length):
    outer_lo = take_run(padded, 0, length + 3, along_dim)
    inner_lo = take_run(padded, 1, length + 3, along_dim)
    inner_hi = take_run(padded, 2, length + 3, along_dim)
    outer_hi = take_run(padded, 3, length + 3, along_dim)
    edge_vals = 7.0 / 12.0 * (inner_lo + inner_hi) - 1.0 / 12.0 * (outer_lo + outer_hi)
    edge_vals = jnp.minimum(
        jnp.maximum(edge_vals, jnp.minimum(inner_lo, inner_hi)), jnp.maximum(inner_lo, inner_hi)
    )
    centre = take_run(padded, 2, length + 2, along_dim)
    left_edge = take_run(edge_vals, 0, length + 2, along_dim)
    right_edge = take_run(edge_vals, 1, length + 2, along_dim)
    slopes = right_edge - left_edge
    curves = 6.0 * centre - 3.0 * (left_edge + right_edge)
    right_west = take_run(right_edge, 0, length + 1, along_dim)
    slope_west = take_run(slopes, 0, length + 1, along_dim)
    curve_west = take_run(curves, 0, length + 1, along_dim)
    left_east = take_run(left_edge, 1, length + 1, along_dim)
    slope_east = take_run(slopes, 1, length + 1, along_dim)
    curve_east = take_run(curves, 1, length + 1, along_dim)
    upwind = right_west - 0.5 * courant * (slope_west - (1.0 - courant * (2.0 / 3.0)) * curve_west)
    reverse = -courant
    downwind = left_east + 0.5 * reverse * (slope_east + (1.0 - reverse * (2.0 / 3.0)) * curve_east)
    return courant * jnp.where(courant > 0, upwind, downwind)


def advect(padded, flux_pad, wet_pad):
    count_x = padded.shape[-2] - 6
    count_y = padded.shape[-1] - 6
    wet_cells = wet_pad[:, 1:-1, 1:-1]
    courant_x = (
        flux_pad[0][:, 0 : count_x + 1, 1:-1]
        * wet_pad[:, 0 : count_x + 1, 1:-1]
        * wet_pad[:, 1 : count_x + 2, 1:-1]
    )
    flux_x = face_fluxes(padded[..., 3:-3], courant_x, -2, count_x)
    courant_y = (
        flux_pad[1][:, 1:-1, 0 : count_y + 1]
        * wet_pad[:, 1:-1, 0 : count_y + 1]
        * wet_pad[:, 1:-1, 1 : count_y + 2]
    )
    flux_y = face_fluxes(padded[..., 3:-3, :], courant_y, -1, count_y)
    centre = padded[..., 3:-3, 3:-3]
    wet_below = jnp.concatenate([wet_cells[1:], jnp.zeros_like(wet_cells[:1])], axis=0)
    courant_z = flux_pad[2][:, 1:-1, 1:-1] * wet_cells * wet_below
    cells_below = jnp.concatenate(
        [centre[..., 1:, :, :], jnp.zeros_like(centre[..., :1, :, :])], axis=-3
    )
    flux_z = courant_z * jnp.where(courant_z > 0, centre, cells_below)
    flux_above = jnp.concatenate(
        [jnp.zeros_like(flux_z[..., :1, :, :]), flux_z[..., :-1, :, :]], axis=-3
    )
    return centre - (
        flux_x[..., 1:, :]
        - flux_x[..., :-1, :]
        + (flux_y[..., 1:] - flux_y[..., :-1])
        + (flux_z - flux_above)
    )


def mixing_factors(diffusivity, wet_cells):
    wet_below = jnp.concatenate([wet_cells[1:], jnp.zeros_like(wet_cells[:1])], axis=0)
    coupling = diffusivity * wet_cells * wet_below
    inverses = []
    ratios = []
    lowers = []
    for level_idx in range(coupling.shape[0]):
        upper_c = coupling[level_idx]
        if level_idx > 0:
            lower_c = coupling[level_idx - 1]
            diagonal = 1.0 + lower_c + upper_c + lower_c * ratios[-1]
        else:
            lower_c = jnp.zeros_like(upper_c)
            diagonal = 1.0 + upper_c
        inverse = 1.0 / diagonal
        inverses.append(inverse)
        ratios.append(-upper_c * inverse)
        lowers.append(lower_c)
    return (inverses, ratios, lowers)


def solve(right_side, factors):
    inverses, ratios, lowers = factors
    forward = []
    for level_idx in range(len(inverses)):
        if level_idx > 0:
            forward.append(
                (right_side[..., level_idx, :, :] + lowers[level_idx] * forward[-1])
                * inverses[level_idx]
            )
        else:
            forward.append(right_side[..., 0, :, :] * inverses[0])
    result = [forward[-1]]
    for level_idx in range(len(inverses) - 2, -1, -1):
        result.append(forward[level_idx] - ratios[level_idx] * result[-1])
    return jnp.stack(result[::-1], axis=-3)


def react(group_tracers, group_rates):
    return group_tracers + group_tracers * jnp.einsum(
        "ab,bzxy->azxy", group_rates, group_tracers, precision=lax.Precision.HIGHEST
    )


def on_device(tracers, reaction, velocity, thickness, sea_mask, bottom, diffusivity):
    slab = 0.3 * jnp.tanh(velocity) * thickness[None]
    depth_cells = (sea_mask * bottom).astype(jnp.float32)[None, None]
    fluxes = lax.all_gather(slab, "group", axis=1, tiled=True)
    flux_pad, depth_pad = (
        with_halo(fluxes, (("dx", 2), ("dy", 3)), 1),
        with_halo(depth_cells, (("dx", 2), ("dy", 3)), 1),
    )
    levels = jnp.arange(diffusivity.shape[0]).astype(jnp.float32)
    wet_pad = (levels[:, None, None] < depth_pad[0]).astype(jnp.float32)
    wet_cells = wet_pad[:, 1:-1, 1:-1]
    factors = mixing_factors(diffusivity, wet_cells)
    current = tracers * wet_cells[None]
    for time_step in range(TSTEPS):
        current = react(current, reaction)
        padded = with_halo(current, (("dx", 2), ("dy", 3)), 3)
        current = solve(advect(padded, flux_pad, wet_pad), factors)
    return current


def solution(mesh):
    placed = (
        P("group", None, "dx", "dy"),
        P("group", None),
        P(None, "group", "dx", "dy"),
        P("group", "dx", "dy"),
        P("dx", "dy"),
        P("dx", "dy"),
        P(None, "dx", "dy"),
    )
    return jax.shard_map(
        on_device,
        mesh=mesh,
        in_specs=placed,
        out_specs=P("group", None, "dx", "dy"),
        check_vma=False,
    )
```

profile of v0, /device:TPU:6, one launch (start us, length us, event | category | flops | bytes accessed | tf_op | source)
XLA Modules:
  0.0 336.2 jit_solution(1982477661203707622)
XLA Ops:
  0.8 15.6 %collective-permute-start = (f32[1,1,1,128]{3,2,1,0:T(1,128)S(1)}, f32[1,1,1,128]{3,2,1,0:T(1,128)S(1)}, u32[]{:S(2)}, u32[]{:S(2)}) collective-permute-start(f32[1,1,1,128]{3,2,1,0:T(1,128)S(1)} %get-tuple-element.202), channel_id=1, source_target_pairs={{0,8},{8,16},{16,24},{24,32},{32,40},{40,48},{48,56},{56,64},{64,7... | collective-permute-start | bytes 1544 | tf_op jit(solution)/shard_map/ppermute | solution.py:14
  16.4 1.9 collective-permute-start.1
  19.9 13.5 %all_gather.3 = f32[3,32,8,128]{3,2,1,0:T(8,128)S(1)} all-gather(f32[3,4,8,128]{3,2,1,0:T(8,128)S(1)} %tanh_multiply_fusion), channel_id=1, replica_groups=mesh['group'=8,'dx'=16,'dy'=8] {'group'}, dimensions={1}, use_global_device_ids=true | all-gather | bytes 442368 | tf_op jit(solution)/shard_map/all_gather | solution.py:133
  33.5 14.7 %collective-permute-start.4 = (f32[3,32,1,128]{3,2,1,0:T(1,128)S(1)}, f32[3,32,1,128]{3,2,1,0:T(1,128)S(1)}, u32[]{:S(2)}, u32[]{:S(2)}) collective-permute-start(f32[3,32,1,128]{3,2,1,0:T(1,128)S(1)} %get-tuple-element.142), channel_id=1, source_target_pairs={{0,8},{8,16},{16,24},{24,32},{32,40},{40,48},{48,56},{56,64},{64,7... | collective-permute-start | bytes 147464 | tf_op jit(solution)/shard_map/ppermute | solution.py:14
  48.2 1.9 collective-permute-start.5
  50.3 3.8 %collective-permute-start.2 = (f32[1,1,10,1]{3,2,1,0:T(8,128)S(1)}, f32[1,1,10,1]{3,2,1,0:T(8,128)S(1)}, u32[]{:S(2)}, u32[]{:S(2)}) collective-permute-start(f32[1,1,10,1]{3,2,1,0:T(8,128)S(1)} %get-tuple-element.200), channel_id=1, source_target_pairs={{0,1},{1,2},{2,3},{3,4},{4,5},{5,6},{6,7},{8,9},{9,10},{10,11},{11... | collective-permute-start | bytes 128 | tf_op jit(solution)/shard_map/ppermute | solution.py:14
  54.1 1.3 collective-permute-start.3
  55.4 4.2 %collective-permute-done.3 = f32[1,1,10,1]{3,2,1,0:T(8,128)S(1)} collective-permute-done((f32[1,1,10,1]{3,2,1,0:T(8,128)S(1)}, f32[1,1,10,1]{3,2,1,0:T(8,128)S(1)}, u32[]{:S(2)}, u32[]{:S(2)}) %collective-permute-start.3) | collective-permute-done | bytes 72 | tf_op jit(solution)/shard_map/ppermute | solution.py:17
  70.3 2.2 multiply_add_fusion.1
  76.3 1.4 copy.43
  77.7 3.8 %collective-permute-start.6 = (f32[3,32,10,1]{1,3,2,0:T(1,128)S(1)}, f32[3,32,10,1]{1,3,2,0:T(1,128)S(1)}, u32[]{:S(2)}, u32[]{:S(2)}) collective-permute-start(f32[3,32,10,1]{1,3,2,0:T(1,128)S(1)} %copy.43), channel_id=1, source_target_pairs={{0,1},{1,2},{2,3},{3,4},{4,5},{5,6},{6,7},{8,9},{9,10},{10,11},{11... | collective-permute-start | bytes 11528 | tf_op jit(solution)/shard_map/ppermute | solution.py:14
  81.9 1.3 collective-permute-start.7
  83.9 15.2 %collective-permute-start.8 = (f32[8,32,3,128]{3,0,2,1:T(8,128)}, f32[8,32,3,128]{3,0,2,1:T(8,128)S(1)}, u32[]{:S(2)}, u32[]{:S(2)}) collective-permute-start(f32[8,32,3,128]{3,0,2,1:T(8,128)} %get-tuple-element.136), channel_id=1, source_target_pairs={{0,8},{8,16},{16,24},{24,32},{32,40},{40,48},{48,56},{56,64},{64,7... | collective-permute-start | bytes 1179656 | tf_op jit(solution)/shard_map/ppermute | solution.py:14
  99.1 1.9 collective-permute-start.9
  101.1 1.3 copy.45
  103.5 2.5 pad_maximum_fusion.16
  110.9 69.1 %collective-permute-done.9 = f32[8,32,3,128]{3,0,2,1:T(8,128)S(1)} collective-permute-done((f32[8,32,3,128]{3,0,2,1:T(8,128)}, f32[8,32,3,128]{3,0,2,1:T(8,128)S(1)}, u32[]{:S(2)}, u32[]{:S(2)}) %collective-permute-start.9) | collective-permute-done | bytes 393248 | tf_op jit(solution)/shard_map/ppermute | solution.py:17
  180.8 2.4 fusion.193
  183.1 1.6 fusion.31
  184.7 1.8 slice_subtract_fusion.3
  186.5 3.0 copy.47
  189.5 2.0 collective-permute-start.10
  191.5 3.0 copy.48
  194.4 1.5 collective-permute-start.11
  195.9 4.2 %fusion.50 = f32[8,32,9,128]{3,0,2,1:T(8,128)} fusion(f32[8,32,10,128]{3,0,2,1:T(8,128)} %get-tuple-element.133, f32[8,32,10,128]{3,0,2,1:T(8,128)} %get-tuple-element.132, f32[8,32,11,128]{3,0,2,1:T(8,128)S(1)} %fusion.31, f32[32,9,128]{2,1,0:T(8,128)} %get-tuple-element.147, f32[32,9,128]{2,1,0:T(8,128)S(1)} %copy-done.35, ...), kind=kLoop, calls=%fused_computation.88 | loop fusion | flops 2949120 | bytes 7852032 | tf_op jit(solution)/shard_map/mul | solution.py:49
  200.2 3.0 copy.49
  203.1 3.0 copy.50
  206.1 3.8 %pad_maximum_fusion = f32[8,32,14,134]{3,0,2,1:T(8,128)S(1)} fusion(f32[8,32,14,3]{3,0,2,1:T(8,128)} %copy.50, f32[8,32,3,128]{3,0,2,1:T(8,128)S(1)} %copy-done.16, f32[8,32,8,128]{3,0,2,1:T(8,128)S(1)} %copy-done.3, f32[8,32,3,128]{3,0,2,1:T(8,128)S(1)} %copy-done.14, f32[8,32,14,3]{3,0,2,1:T(8,128)} %copy.49), kind=kLoop, calls=%fused_computation | loop fusion | flops 1921024 | bytes 3842048 | tf_op jit(solution)/shard_map/concatenate | solution.py:18
  210.0 2.0 fusion.27
  213.3 2.3 fusion.18
  216.9 1.5 constant_dynamic-update-slice_fusion.31
  220.0 1.9 collective-permute-start.12
  221.9 4.1 %collective-permute-start.13 = (f32[8,32,3,128]{3,0,2,1:T(8,128)S(1)}, f32[8,32,3,128]{3,0,2,1:T(8,128)S(1)}, u32[]{:S(2)}, u32[]{:S(2)}) collective-permute-start(f32[8,32,3,128]{3,0,2,1:T(8,128)S(1)} %get-tuple-element.135), channel_id=1, source_target_pairs={{8,0},{16,8},{24,16},{32,24},{40,32},{48,40},{56,48},{64,56},{72,6... | collective-permute-start | bytes 1179656 | tf_op jit(solution)/shard_map/ppermute | solution.py:17
  226.5 3.5 %collective-permute-done.12 = f32[8,32,3,128]{3,0,2,1:T(8,128)S(1)} collective-permute-done((f32[8,32,3,128]{3,0,2,1:T(8,128)S(1)}, f32[8,32,3,128]{3,0,2,1:T(8,128)S(1)}, u32[]{:S(2)}, u32[]{:S(2)}) %collective-permute-start.12) | collective-permute-done | bytes 393248 | tf_op jit(solution)/shard_map/ppermute | solution.py:14
  230.0 68.9 %collective-permute-done.13 = f32[8,32,3,128]{3,0,2,1:T(8,128)S(1)} collective-permute-done((f32[8,32,3,128]{3,0,2,1:T(8,128)S(1)}, f32[8,32,3,128]{3,0,2,1:T(8,128)S(1)}, u32[]{:S(2)}, u32[]{:S(2)}) %collective-permute-start.13) | collective-permute-done | bytes 393248 | tf_op jit(solution)/shard_map/ppermute | solution.py:17
  299.0 2.4 fusion.192
  301.9 1.8 slice_subtract_fusion.2
  303.7 3.0 copy.53
  306.6 2.0 collective-permute-start.14
  308.6 2.9 copy.54
  311.5 1.3 collective-permute-start.15
  312.8 4.4 %fusion.42 = f32[8,32,9,128]{3,0,2,1:T(8,128)} fusion(f32[8,32,10,128]{3,0,2,1:T(8,128)} %get-tuple-element.131, f32[8,32,10,128]{3,0,2,1:T(8,128)} %get-tuple-element.130, f32[8,32,11,128]{3,0,2,1:T(8,128)S(1)} %fusion.35, f32[32,9,128]{2,1,0:T(8,128)} %get-tuple-element.147, f32[32,9,128]{2,1,0:T(8,128)} %get-tuple-element.145, ...), kind=kLoop, calls=%fused_computation.78 | loop fusion | flops 2949120 | bytes 7852032 | tf_op jit(solution)/shard_map/mul | solution.py:49
  317.2 1.8 copy.55
  320.0 2.9 copy.56
  322.9 3.3 pad_maximum_fusion.1
  326.2 2.0 fusion.13
  329.5 2.3 fusion.4
  333.1 1.5 constant_dynamic-update-slice_fusion.63
  (408 shorter events, 33.2 us)
Async XLA Ops:
  0.0 70.3 %copy-start = (f32[8,8]{1,0:T(8,128)S(1)}, f32[8,8]{1,0:T(8,128)}, u32[]{:S(2)}) copy-start(f32[8,8]{1,0:T(8,128)} %param.8) | copy-start | bytes 772
  0.0 70.3 %copy-start.38 = (f32[8,32,8,128]{3,2,1,0:T(8,128)S(1)}, f32[8,32,8,128]{3,2,1,0:T(8,128)}, u32[]{:S(2)}) copy-start(f32[8,32,8,128]{3,2,1,0:T(8,128)} %param.7) | copy-start | bytes 3145732
  0.8 49.4 %collective-permute-start = (f32[1,1,1,128]{3,2,1,0:T(1,128)S(1)}, f32[1,1,1,128]{3,2,1,0:T(1,128)S(1)}, u32[]{:S(2)}, u32[]{:S(2)}) collective-permute-start(f32[1,1,1,128]{3,2,1,0:T(1,128)S(1)} %get-tuple-element.202), channel_id=1, source_target_pairs={{0,8},{8,16},{16,24},{24,32},{32,40},{40,48},{48,56},{56,64},{64,7... | collective-permute-start | bytes 1544 | tf_op jit(solution)/shard_map/ppermute | solution.py:14
  16.4 33.7 %collective-permute-start.1 = (f32[1,1,1,128]{3,2,1,0:T(1,128)S(1)}, f32[1,1,1,128]{3,2,1,0:T(1,128)S(1)}, u32[]{:S(2)}, u32[]{:S(2)}) collective-permute-start(f32[1,1,1,128]{3,2,1,0:T(1,128)S(1)} %get-tuple-element.203), channel_id=1, source_target_pairs={{8,0},{16,8},{24,16},{32,24},{40,32},{48,40},{56,48},{64,56},{72,6... | collective-permute-start | bytes 1544 | tf_op jit(solution)/shard_map/ppermute | solution.py:17
  33.4 41.6 %copy-start.24 = (f32[3,32,8,128]{3,2,1,0:T(8,128)}, f32[3,32,8,128]{3,2,1,0:T(8,128)S(1)}, u32[]{:S(2)}) copy-start(f32[3,32,8,128]{3,2,1,0:T(8,128)S(1)} %all_gather.3) | copy-start | bytes 1179652
  33.5 41.5 %collective-permute-start.4 = (f32[3,32,1,128]{3,2,1,0:T(1,128)S(1)}, f32[3,32,1,128]{3,2,1,0:T(1,128)S(1)}, u32[]{:S(2)}, u32[]{:S(2)}) collective-permute-start(f32[3,32,1,128]{3,2,1,0:T(1,128)S(1)} %get-tuple-element.142), channel_id=1, source_target_pairs={{0,8},{8,16},{16,24},{24,32},{32,40},{40,48},{48,56},{56,64},{64,7... | collective-permute-start | bytes 147464 | tf_op jit(solution)/shard_map/ppermute | solution.py:14
  48.2 26.8 %collective-permute-start.5 = (f32[3,32,1,128]{3,2,1,0:T(1,128)S(1)}, f32[3,32,1,128]{3,2,1,0:T(1,128)S(1)}, u32[]{:S(2)}, u32[]{:S(2)}) collective-permute-start(f32[3,32,1,128]{3,2,1,0:T(1,128)S(1)} %get-tuple-element.143), channel_id=1, source_target_pairs={{8,0},{16,8},{24,16},{32,24},{40,32},{48,40},{56,48},{64,56},{72,6... | collective-permute-start | bytes 147464 | tf_op jit(solution)/shard_map/ppermute | solution.py:17
  50.3 5.2 %collective-permute-start.2 = (f32[1,1,10,1]{3,2,1,0:T(8,128)S(1)}, f32[1,1,10,1]{3,2,1,0:T(8,128)S(1)}, u32[]{:S(2)}, u32[]{:S(2)}) collective-permute-start(f32[1,1,10,1]{3,2,1,0:T(8,128)S(1)} %get-tuple-element.200), channel_id=1, source_target_pairs={{0,1},{1,2},{2,3},{3,4},{4,5},{5,6},{6,7},{8,9},{9,10},{10,11},{11... | collective-permute-start | bytes 128 | tf_op jit(solution)/shard_map/ppermute | solution.py:14
  54.1 5.5 %collective-permute-start.3 = (f32[1,1,10,1]{3,2,1,0:T(8,128)S(1)}, f32[1,1,10,1]{3,2,1,0:T(8,128)S(1)}, u32[]{:S(2)}, u32[]{:S(2)}) collective-permute-start(f32[1,1,10,1]{3,2,1,0:T(8,128)S(1)} %get-tuple-element.201), channel_id=1, source_target_pairs={{1,0},{2,1},{3,2},{4,3},{5,4},{6,5},{7,6},{9,8},{10,9},{11,10},{12... | collective-permute-start | bytes 128 | tf_op jit(solution)/shard_map/ppermute | solution.py:17
  62.2 11.3 %copy-start.77 = (f32[1,8,128]{2,1,0:T(8,128)}, f32[1,8,128]{2,1,0:T(8,128)S(1)}, u32[]{:S(2)}) copy-start(f32[1,8,128]{2,1,0:T(8,128)S(1)} %get-tuple-element.70) | copy-start | bytes 12292
  62.2 12.1 %copy-start.133 = (f32[1,8,128]{2,1,0:T(8,128)}, f32[1,8,128]{2,1,0:T(8,128)S(1)}, u32[]{:S(2)}) copy-start(f32[1,8,128]{2,1,0:T(8,128)S(1)} %get-tuple-element.71) | copy-start | bytes 12292
  62.8 10.7 %copy-start.80 = (f32[1,8,128]{2,1,0:T(8,128)}, f32[1,8,128]{2,1,0:T(8,128)S(1)}, u32[]{:S(2)}) copy-start(f32[1,8,128]{2,1,0:T(8,128)S(1)} %get-tuple-element.73) | copy-start | bytes 12292
  62.8 11.5 %copy-start.134 = (f32[1,8,128]{2,1,0:T(8,128)}, f32[1,8,128]{2,1,0:T(8,128)S(1)}, u32[]{:S(2)}) copy-start(f32[1,8,128]{2,1,0:T(8,128)S(1)} %get-tuple-element.74) | copy-start | bytes 12292
  63.4 10.1 %copy-start.83 = (f32[1,8,128]{2,1,0:T(8,128)}, f32[1,8,128]{2,1,0:T(8,128)S(1)}, u32[]{:S(2)}) copy-start(f32[1,8,128]{2,1,0:T(8,128)S(1)} %get-tuple-element.76) | copy-start | bytes 12292
  63.4 10.9 %copy-start.135 = (f32[1,8,128]{2,1,0:T(8,128)}, f32[1,8,128]{2,1,0:T(8,128)S(1)}, u32[]{:S(2)}) copy-start(f32[1,8,128]{2,1,0:T(8,128)S(1)} %get-tuple-element.77) | copy-start | bytes 12292
  64.0 9.5 %copy-start.86 = (f32[1,8,128]{2,1,0:T(8,128)}, f32[1,8,128]{2,1,0:T(8,128)S(1)}, u32[]{:S(2)}) copy-start(f32[1,8,128]{2,1,0:T(8,128)S(1)} %get-tuple-element.79) | copy-start | bytes 12292
  64.0 19.1 %copy-start.89 = (f32[1,8,128]{2,1,0:T(8,128)}, f32[1,8,128]{2,1,0:T(8,128)S(1)}, u32[]{:S(2)}) copy-start(f32[1,8,128]{2,1,0:T(8,128)S(1)} %get-tuple-element.80) | copy-start | bytes 12292
  64.7 8.9 %copy-start.92 = (f32[1,8,128]{2,1,0:T(8,128)}, f32[1,8,128]{2,1,0:T(8,128)S(1)}, u32[]{:S(2)}) copy-start(f32[1,8,128]{2,1,0:T(8,128)S(1)} %get-tuple-element.82) | copy-start | bytes 12292
  64.7 18.5 %copy-start.95 = (f32[1,8,128]{2,1,0:T(8,128)}, f32[1,8,128]{2,1,0:T(8,128)S(1)}, u32[]{:S(2)}) copy-start(f32[1,8,128]{2,1,0:T(8,128)S(1)} %get-tuple-element.83) | copy-start | bytes 12292
  65.3 8.3 %copy-start.98 = (f32[1,8,128]{2,1,0:T(8,128)}, f32[1,8,128]{2,1,0:T(8,128)S(1)}, u32[]{:S(2)}) copy-start(f32[1,8,128]{2,1,0:T(8,128)S(1)} %get-tuple-element.85) | copy-start | bytes 12292
  65.3 17.9 %copy-start.101 = (f32[1,8,128]{2,1,0:T(8,128)}, f32[1,8,128]{2,1,0:T(8,128)S(1)}, u32[]{:S(2)}) copy-start(f32[1,8,128]{2,1,0:T(8,128)S(1)} %get-tuple-element.86) | copy-start | bytes 12292
  65.9 7.6 %copy-start.104 = (f32[1,8,128]{2,1,0:T(8,128)}, f32[1,8,128]{2,1,0:T(8,128)S(1)}, u32[]{:S(2)}) copy-start(f32[1,8,128]{2,1,0:T(8,128)S(1)} %get-tuple-element.88) | copy-start | bytes 12292
  65.9 17.2 %copy-start.107 = (f32[1,8,128]{2,1,0:T(8,128)}, f32[1,8,128]{2,1,0:T(8,128)S(1)}, u32[]{:S(2)}) copy-start(f32[1,8,128]{2,1,0:T(8,128)S(1)} %get-tuple-element.89) | copy-start | bytes 12292
  66.6 7.0 %copy-start.110 = (f32[1,8,128]{2,1,0:T(8,128)}, f32[1,8,128]{2,1,0:T(8,128)S(1)}, u32[]{:S(2)}) copy-start(f32[1,8,128]{2,1,0:T(8,128)S(1)} %get-tuple-element.91) | copy-start | bytes 12292
  66.6 7.0 %copy-start.113 = (f32[1,8,128]{2,1,0:T(8,128)}, f32[1,8,128]{2,1,0:T(8,128)S(1)}, u32[]{:S(2)}) copy-start(f32[1,8,128]{2,1,0:T(8,128)S(1)} %get-tuple-element.92) | copy-start | bytes 12292
  67.2 6.4 %copy-start.116 = (f32[1,8,128]{2,1,0:T(8,128)}, f32[1,8,128]{2,1,0:T(8,128)S(1)}, u32[]{:S(2)}) copy-start(f32[1,8,128]{2,1,0:T(8,128)S(1)} %get-tuple-element.94) | copy-start | bytes 12292
  67.2 6.4 %copy-start.119 = (f32[1,8,128]{2,1,0:T(8,128)}, f32[1,8,128]{2,1,0:T(8,128)S(1)}, u32[]{:S(2)}) copy-start(f32[1,8,128]{2,1,0:T(8,128)S(1)} %get-tuple-element.95) | copy-start | bytes 12292
  72.4 11.4 %copy-start.2 = (f32[8,32,8,128]{3,0,2,1:T(8,128)}, f32[8,32,8,128]{3,0,2,1:T(8,128)S(1)}, u32[]{:S(2)}) copy-start(f32[8,32,8,128]{3,0,2,1:T(8,128)S(1)} %multiply_add_fusion.1) | copy-start | bytes 3145732
  75.2 8.0 %copy-start.131 = (f32[1,8,128]{2,1,0:T(8,128)S(1)}, f32[1,8,128]{2,1,0:T(8,128)}, u32[]{:S(2)}) copy-start(f32[1,8,128]{2,1,0:T(8,128)} %get-tuple-element.110) | copy-start | bytes 12292
  77.7 23.3 %collective-permute-start.6 = (f32[3,32,10,1]{1,3,2,0:T(1,128)S(1)}, f32[3,32,10,1]{1,3,2,0:T(1,128)S(1)}, u32[]{:S(2)}, u32[]{:S(2)}) collective-permute-start(f32[3,32,10,1]{1,3,2,0:T(1,128)S(1)} %copy.43), channel_id=1, source_target_pairs={{0,1},{1,2},{2,3},{3,4},{4,5},{5,6},{6,7},{8,9},{9,10},{10,11},{11... | collective-permute-start | bytes 11528 | tf_op jit(solution)/shard_map/ppermute | solution.py:14
  81.9 20.4 %collective-permute-start.7 = (f32[3,32,10,1]{1,3,2,0:T(1,128)S(1)}, f32[3,32,10,1]{1,3,2,0:T(1,128)S(1)}, u32[]{:S(2)}, u32[]{:S(2)}) collective-permute-start(f32[3,32,10,1]{1,3,2,0:T(1,128)S(1)} %copy.44), channel_id=1, source_target_pairs={{1,0},{2,1},{3,2},{4,3},{5,4},{6,5},{7,6},{9,8},{10,9},{11,10},{12... | collective-permute-start | bytes 11528 | tf_op jit(solution)/shard_map/ppermute | solution.py:17
  83.9 19.7 %copy-start.25 = (f32[3,32,8,128]{3,2,1,0:T(8,128)S(1)}, f32[3,32,8,128]{3,2,1,0:T(8,128)}, u32[]{:S(2)}) copy-start(f32[3,32,8,128]{3,2,1,0:T(8,128)} %copy-done.24) | copy-start | bytes 1179652
  83.9 27.0 %collective-permute-start.8 = (f32[8,32,3,128]{3,0,2,1:T(8,128)}, f32[8,32,3,128]{3,0,2,1:T(8,128)S(1)}, u32[]{:S(2)}, u32[]{:S(2)}) collective-permute-start(f32[8,32,3,128]{3,0,2,1:T(8,128)} %get-tuple-element.136), channel_id=1, source_target_pairs={{0,8},{8,16},{16,24},{24,32},{32,40},{40,48},{48,56},{56,64},{64,7... | collective-permute-start | bytes 1179656 | tf_op jit(solution)/shard_map/ppermute | solution.py:14
  99.1 80.9 %collective-permute-start.9 = (f32[8,32,3,128]{3,0,2,1:T(8,128)}, f32[8,32,3,128]{3,0,2,1:T(8,128)S(1)}, u32[]{:S(2)}, u32[]{:S(2)}) collective-permute-start(f32[8,32,3,128]{3,0,2,1:T(8,128)} %get-tuple-element.137), channel_id=1, source_target_pairs={{8,0},{16,8},{24,16},{32,24},{40,32},{48,40},{56,48},{64,56},{72,6... | collective-permute-start | bytes 1179656 | tf_op jit(solution)/shard_map/ppermute | solution.py:17
  109.8 70.3 %copy-start.19 = (f32[32,8,129]{2,1,0:T(8,128)}, f32[32,8,129]{2,1,0:T(8,128)S(1)}, u32[]{:S(2)}) copy-start(f32[32,8,129]{2,1,0:T(8,128)S(1)} %get-tuple-element.118) | copy-start | bytes 396292
  110.9 69.2 %copy-start.13 = (f32[8,32,3,128]{3,0,2,1:T(8,128)}, f32[8,32,3,128]{3,0,2,1:T(8,128)S(1)}, u32[]{:S(2)}) copy-start(f32[8,32,3,128]{3,0,2,1:T(8,128)S(1)} %collective-permute-done.8) | copy-start | bytes 1179652
  186.5 9.4 %copy-start.22 = (f32[32,9,128]{2,1,0:T(8,128)S(1)}, f32[32,9,128]{2,1,0:T(8,128)}, u32[]{:S(2)}) copy-start(f32[32,9,128]{2,1,0:T(8,128)} %copy-done.21) | copy-start | bytes 442372
  186.5 9.4 %copy-start.34 = (f32[32,9,128]{2,1,0:T(8,128)S(1)}, f32[32,9,128]{2,1,0:T(8,128)}, u32[]{:S(2)}) copy-start(f32[32,9,128]{2,1,0:T(8,128)} %get-tuple-element.144) | copy-start | bytes 442372
  186.5 9.4 %copy-start.35 = (f32[32,9,128]{2,1,0:T(8,128)S(1)}, f32[32,9,128]{2,1,0:T(8,128)}, u32[]{:S(2)}) copy-start(f32[32,9,128]{2,1,0:T(8,128)} %get-tuple-element.145) | copy-start | bytes 442372
  186.5 9.4 %copy-start.41 = (pred[32,9,128]{2,1,0:T(8,128)(4,1)S(1)}, pred[32,9,128]{2,1,0:T(8,128)(4,1)}, u32[]{:S(2)}) copy-start(pred[32,9,128]{2,1,0:T(8,128)(4,1)} %get-tuple-element.115) | copy-start | bytes 110596
  189.5 10.6 %collective-permute-start.10 = (f32[8,32,14,3]{1,0,3,2:T(8,128)}, f32[8,32,14,3]{1,0,3,2:T(8,128)}, u32[]{:S(2)}, u32[]{:S(2)}) collective-permute-start(f32[8,32,14,3]{1,0,3,2:T(8,128)} %copy.47), channel_id=1, source_target_pairs={{0,1},{1,2},{2,3},{3,4},{4,5},{5,6},{6,7},{8,9},{9,10},{10,11},{11... | collective-permute-start | bytes 129032 | tf_op jit(solution)/shard_map/ppermute | solution.py:14
  194.4 8.7 %collective-permute-start.11 = (f32[8,32,14,3]{1,0,3,2:T(8,128)}, f32[8,32,14,3]{1,0,3,2:T(8,128)}, u32[]{:S(2)}, u32[]{:S(2)}) collective-permute-start(f32[8,32,14,3]{1,0,3,2:T(8,128)} %copy.48), channel_id=1, source_target_pairs={{1,0},{2,1},{3,2},{4,3},{5,4},{6,5},{7,6},{9,8},{10,9},{11,10},{12... | collective-permute-start | bytes 129032 | tf_op jit(solution)/shard_map/ppermute | solution.py:17
  220.0 10.0 %collective-permute-start.12 = (f32[8,32,3,128]{3,0,2,1:T(8,128)S(1)}, f32[8,32,3,128]{3,0,2,1:T(8,128)S(1)}, u32[]{:S(2)}, u32[]{:S(2)}) collective-permute-start(f32[8,32,3,128]{3,0,2,1:T(8,128)S(1)} %get-tuple-element.134), channel_id=1, source_target_pairs={{0,8},{8,16},{16,24},{24,32},{32,40},{40,48},{48,56},{56,64},{64,7... | collective-permute-start | bytes 1179656 | tf_op jit(solution)/shard_map/ppermute | solution.py:14
  221.9 77.0 %collective-permute-start.13 = (f32[8,32,3,128]{3,0,2,1:T(8,128)S(1)}, f32[8,32,3,128]{3,0,2,1:T(8,128)S(1)}, u32[]{:S(2)}, u32[]{:S(2)}) collective-permute-start(f32[8,32,3,128]{3,0,2,1:T(8,128)S(1)} %get-tuple-element.135), channel_id=1, source_target_pairs={{8,0},{16,8},{24,16},{32,24},{40,32},{48,40},{56,48},{64,56},{72,6... | collective-permute-start | bytes 1179656 | tf_op jit(solution)/shard_map/ppermute | solution.py:17
  303.6 9.2 %copy-start.23 = (f32[32,9,128]{2,1,0:T(8,128)S(1)}, f32[32,9,128]{2,1,0:T(8,128)}, u32[]{:S(2)}) copy-start(f32[32,9,128]{2,1,0:T(8,128)} %copy-done.21) | copy-start | bytes 442372
  303.6 9.2 %copy-start.42 = (pred[32,9,128]{2,1,0:T(8,128)(4,1)S(1)}, pred[32,9,128]{2,1,0:T(8,128)(4,1)}, u32[]{:S(2)}) copy-start(pred[32,9,128]{2,1,0:T(8,128)(4,1)} %get-tuple-element.115) | copy-start | bytes 110596
  306.6 10.6 %collective-permute-start.14 = (f32[8,32,14,3]{1,0,3,2:T(8,128)}, f32[8,32,14,3]{1,0,3,2:T(8,128)}, u32[]{:S(2)}, u32[]{:S(2)}) collective-permute-start(f32[8,32,14,3]{1,0,3,2:T(8,128)} %copy.53), channel_id=1, source_target_pairs={{0,1},{1,2},{2,3},{3,4},{4,5},{5,6},{6,7},{8,9},{9,10},{10,11},{11... | collective-permute-start | bytes 129032 | tf_op jit(solution)/shard_map/ppermute | solution.py:14
  311.5 8.5 %collective-permute-start.15 = (f32[8,32,14,3]{1,0,3,2:T(8,128)}, f32[8,32,14,3]{1,0,3,2:T(8,128)}, u32[]{:S(2)}, u32[]{:S(2)}) collective-permute-start(f32[8,32,14,3]{1,0,3,2:T(8,128)} %copy.54), channel_id=1, source_target_pairs={{1,0},{2,1},{3,2},{4,3},{5,4},{6,5},{7,6},{9,8},{10,9},{11,10},{12... | collective-permute-start | bytes 129032 | tf_op jit(solution)/shard_map/ppermute | solution.py:17
  (108 other events, 186.6 us)
where the time goes:
time: 337 us; the launch traced here: 336 us
  waiting for transfers between devices  147 us (44%)
  starting transfers between devices  74.3 us (22%)
  other arithmetic  58.8 us (17%)
  local copies, waits for them, and re-layouts  37 us (11%)
  blocking collectives  13.5 us (4%)
    ppermute x8, waiting for transfers between devices, with_halo(): lax.ppermute(lax.slice_in_dim(block, 0, width, axis=dim), axis, backward)  143 us
    ppermute x8, starting transfers between devices, with_halo(): lax.ppermute(lax.slice_in_dim(block, block.shape[dim] - width, None, axis...  59.1 us
    ppermute x8, starting transfers between devices, with_halo(): lax.ppermute(lax.slice_in_dim(block, 0, width, axis=dim), axis, backward)  15.2 us
    slice x11, local copies, waits for them, and re-layouts, with_halo(): lax.slice_in_dim(block, block.shape[dim] - width, None, axis=dim)  14.5 us
    all_gather x1, blocking collectives, on_device(): fluxes = lax.all_gather(slab, 'group', axis=1, tiled=True)  13.5 us
    mul x4, other arithmetic, face_fluxes(): return courant * jnp.where(courant > 0, upwind, downwind)  13.2 us
    concatenate x7, other arithmetic, with_halo(): block = jnp.concatenate([low, block, high], axis=dim)  9.97 us
    mul x16, other arithmetic, solve(): result.append(forward[level_idx] - ratios[level_idx] * result[-1])  9.85 us
  transfers between devices with their start and end apart: 16, of which 5 were waited for; matrix products, arithmetic and copies ran while one was open for 14% of the time, Pallas kernels for 0%

commit v1 on v0

v1 whole, which is shorter than its diff:
```python
import functools

import jax
import jax.numpy as jnp
from jax import lax
from jax.experimental import pallas as pl
from jax.experimental.pallas import tpu as pltpu
from jax.sharding import PartitionSpec as P

INTERPRET = False
XS = 4
NZ = 32
TR = 8
LANES = 128
HALO = 6
PIECES = {"O": (0, 8), "A": (8, 8), "B": (16, 8), "C": (24, 8)}


def spot(row):
    if row < 0:
        return 12 + row
    return row if row < 8 else row + 4


def vmem(count):
    return [pl.BlockSpec(memory_space=pltpu.VMEM)] * count


def shape_of(*dims):
    return jax.ShapeDtypeStruct(dims, jnp.float32)


def call(body, outs, scalars, arrays, scratch=()):
    return pl.pallas_call(
        body,
        out_shape=outs,
        in_specs=[pl.BlockSpec(memory_space=pltpu.SMEM)] * len(scalars) + vmem(len(arrays)),
        out_specs=vmem(len(outs)),
        scratch_shapes=list(scratch),
        interpret=INTERPRET,
    )(*scalars, *arrays)


def spun(rates_ref):
    rates = rates_ref[...]
    tracer = lax.broadcasted_iota(jnp.int32, (TR, TR), 0)
    other = lax.broadcasted_iota(jnp.int32, (TR, TR), 1)
    spins = []
    for shift in range(TR):
        picked = jnp.where(other == (tracer + TR - shift) % TR, rates, 0.0)
        spins.append(jnp.broadcast_to(jnp.sum(picked, axis=1, keepdims=True), (TR, LANES)))
    return spins


def react(value, rates):
    total = rates[0] * value
    for shift in range(1, TR):
        total = total + rates[shift] * pltpu.roll(value, shift, 0)
    return value + value * total


def first_kernel(x_ref, tracers_ref, sea_ref, bottom_ref, rates_ref, hi_ref, lo_ref, *far_refs):
    depth = sea_ref[...] * bottom_ref[...]
    depths = [jnp.broadcast_to(depth[row : row + 1], (TR, LANES)) for row in range(8)]
    rates = spun(rates_ref)

    def level(k, carry):
        for row in range(8):
            value = tracers_ref[pl.ds(k * 8 + row, TR, stride=NZ * 8), :]
            value = react(jnp.where(k < depths[row], value, 0.0), rates)
            if row < HALO:
                lo_ref[k, row] = value
            if row >= 8 - HALO:
                hi_ref[k, row - (8 - HALO)] = value
        return carry

    lax.fori_loop(0, NZ, level, 0)
    for far_ref, (first, count) in zip(far_refs, PIECES.values()):

        @pl.when(x_ref[0] == XS - 1)
        def _():
            far_ref[...] = hi_ref[first : first + count]

        @pl.when(x_ref[0] != XS - 1)
        def _():
            far_ref[...] = lo_ref[first : first + count]


def pack(values, rows):
    lane = lax.broadcasted_iota(jnp.int32, (TR, LANES), 1)
    slot = lane // 8
    east = west = jnp.zeros((TR, LANES), jnp.float32)
    for value, row in zip(values, rows):
        place = 8 * (row + 3)
        here = slot == row + 3
        east = jnp.where(here, pltpu.roll(value, (place + 3) % LANES, 1), east)
        west = jnp.where(here, pltpu.roll(value, (place + 5) % LANES, 1), west)
    return east, west


def join_kernel(x_ref, hi_ref, lo_ref, west_ref, east_ref, *refs):
    pieces, (all_ref, pack_east_ref, pack_west_ref) = refs[:4], refs[4:]
    for near_ref, owner, base in ((west_ref, 0, 0), (east_ref, XS - 1, HALO + 8)):

        @pl.when(x_ref[0] == owner)
        def _():
            for piece_ref, (first, count) in zip(pieces, PIECES.values()):
                all_ref[first : first + count, base : base + HALO] = piece_ref[...]

        @pl.when(x_ref[0] != owner)
        def _():
            all_ref[:, base : base + HALO] = near_ref[...]

    all_ref[:, HALO : 2 * HALO] = lo_ref[...]
    all_ref[:, 2 * HALO : 2 * HALO + 2] = hi_ref[:, HALO - 2 : HALO]
    rows = list(range(-3, 11))

    def level(k, carry):
        packed = pack([all_ref[k, row + HALO] for row in rows], rows)
        pack_east_ref[k], pack_west_ref[k] = packed
        return carry

    lax.fori_loop(0, NZ, level, 0)


UX, AX, BX, UY, AY, BY, CZ, INV, RATIO, LOWER = range(0, 160, 16)


def coefficient_kernel(gathered_ref, out_ref):
    def level(k, carry):
        ratio_before, lower = carry
        for source, at in ((0, UX), (16, UY)):
            courant = gathered_ref[k, source : source + 16]
            size = jnp.abs(courant)
            out_ref[k, at : at + 16] = courant
            out_ref[k, at + 16 : at + 32] = 0.5 * size
            out_ref[k, at + 32 : at + 48] = 1.0 - size * (2.0 / 3.0)
        out_ref[k, CZ : CZ + 16] = gathered_ref[k, 32:48]
        upper = gathered_ref[k, 48:64]
        inverse = 1.0 / (1.0 + lower + upper + lower * ratio_before)
        ratio = -upper * inverse
        out_ref[k, INV : INV + 16] = inverse
        out_ref[k, RATIO : RATIO + 16] = ratio
        out_ref[k, LOWER : LOWER + 16] = lower
        return ratio, upper

    zero = jnp.zeros((16, LANES), jnp.float32)
    lax.fori_loop(0, NZ, level, (zero, zero))


def edge(outer_lo, inner_lo, inner_hi, outer_hi):
    value = 7.0 / 12.0 * (inner_lo + inner_hi) - 1.0 / 12.0 * (outer_lo + outer_hi)
    return jnp.minimum(
        jnp.maximum(value, jnp.minimum(inner_lo, inner_hi)), jnp.maximum(inner_lo, inner_hi)
    )


def face(courant, half, slope, low_edge, near, high_edge, low_cell, high_cell):
    positive = courant > 0
    far = jnp.where(positive, low_edge, high_edge)
    cell = jnp.where(positive, low_cell, high_cell)
    curve = 6.0 * cell - 3.0 * (near + far)
    return courant * (near - half * ((near - far) - slope * curve))


def ahead(value, count):
    return pltpu.roll(value, (LANES - count) % LANES, 1)


def along_y(q, courant, half, slope):
    q_next = ahead(q, 1)
    edges = edge(pltpu.roll(q, 1, 1), q, q_next, ahead(q, 2))
    return face(
        courant, half, slope, pltpu.roll(edges, 1, 1), edges, ahead(edges, 1), q, q_next
    )


def step_kernel(low_row, high_row, base, last, q_ref, coef_ref, gathered_ref, east_ref, west_ref,
                from_west_ref, from_east_ref, rates_ref, *refs):
    if last:
        out_ref, forward_ref, flux_ref = refs
    else:
        out_ref, pack_east_ref, pack_west_ref, forward_ref, flux_ref = refs
    rows = list(range(low_row, high_row))
    rates = spun(rates_ref)
    lane = lax.broadcasted_iota(jnp.int32, (TR, LANES), 1)
    place = lane % 8

    def coef(k, at, row):
        return jnp.broadcast_to(coef_ref[k, pl.ds(at + spot(row), 1), :], (TR, LANES))

    def strip(k, at, value):
        courant = jnp.broadcast_to(gathered_ref[k, pl.ds(at, 1), :], (TR, LANES))
        size = jnp.abs(courant)
        return along_y(value, courant, 0.5 * size, 1.0 - size * (2.0 / 3.0))

    forward_ref[...] = jnp.zeros_like(forward_ref)
    flux_ref[...] = jnp.zeros_like(flux_ref)

    def down(k, carry):
        below = jnp.minimum(k + 1, NZ - 1)
        strip_w = strip(k, 64, jnp.where(place < 3, from_west_ref[k], east_ref[k]))
        strip_e = strip(k, 65, jnp.where(place < 5, west_ref[k], from_east_ref[k]))
        edges, flux_x = {}, {}

        def q(row):
            return q_ref[k, row + base]

        def edge_at(row):
            if row not in edges:
                edges[row] = edge(q(row - 1), q(row), q(row + 1), q(row + 2))
            return edges[row]

        def flux_at(row):
            if row not in flux_x:
                flux_x[row] = face(
                    coef(k, UX, row), coef(k, AX, row), coef(k, BX, row),
                    edge_at(row - 1), edge_at(row), edge_at(row + 1), q(row), q(row + 1),
                )
            return flux_x[row]

        for index, row in enumerate(rows):
            here = q(row)
            flux_y = along_y(here, coef(k, UY, row), coef(k, AY, row), coef(k, BY, row))
            at = 8 * (row + 3)
            low_end = pltpu.roll(strip_w, (LANES - at - 3) % LANES, 1)
            high_end = pltpu.roll(strip_e, (123 - at) % LANES, 1)
            flux_y = jnp.where(lane < 2, low_end, jnp.where(lane >= 125, high_end, flux_y))
            flux_south = pltpu.roll(jnp.where(lane == 127, low_end, flux_y), 1, 1)
            courant_z = coef(k, CZ, row)
            flux_z = courant_z * jnp.where(courant_z > 0, here, q_ref[below, row + base])
            advected = here - (
                (flux_at(row) - flux_at(row - 1)) + (flux_y - flux_south)
                + (flux_z - flux_ref[index])
            )
            flux_ref[index] = flux_z
            forward_ref[k + 1, index] = (
                advected + coef(k, LOWER, row) * forward_ref[k, index]
            ) * coef(k, INV, row)
        return carry

    lax.fori_loop(0, NZ, down, 0)
    flux_ref[...] = jnp.zeros_like(flux_ref)

    def up(step, carry):
        k = NZ - 1 - step
        own = {}
        for index, row in enumerate(rows):
            value = forward_ref[k + 1, index] - coef(k, RATIO, row) * flux_ref[index]
            flux_ref[index] = value
            if last:
                out_ref[pl.ds(k * 8 + row, TR, stride=NZ * 8), :] = value
            else:
                value = react(value, rates)
                out_ref[k, index] = value
                if 0 <= row < 8:
                    own[row] = value
        if not last:
            pack_east_ref[k], pack_west_ref[k] = pack(own.values(), own.keys())
        return carry

    lax.fori_loop(0, NZ, up, 0)


def transport(tracers, reaction, velocity, thickness, sea_mask, bottom, diffusivity):
    groups, stripes, count = lax.axis_size("dy"), lax.axis_size("dx") // XS, lax.axis_size("dx")
    x_index = (lax.axis_index("dx") % XS).astype(jnp.int32).reshape(1)

    def dx_pairs(forth, back):
        pairs = []
        for stripe in range(stripes):
            for source, target, far in forth:
                if 0 <= stripe + far < stripes and (far or stripe + 1 < stripes):
                    pairs.append((stripe * XS + source, (stripe + far) * XS + target))
            for source, target, far in back:
                if 0 <= stripe - far < stripes and (far or stripe > 0):
                    pairs.append((stripe * XS + source, (stripe - far) * XS + target))
        return pairs

    def collect_pairs(forth, back):
        pairs = []
        for stripe in range(stripes):
            if stripe > 0:
                pairs += [(stripe * XS + s, stripe * XS + t) for s, t in forth]
            if stripe + 1 < stripes:
                pairs += [(stripe * XS + s, stripe * XS + t) for s, t in back]
        return pairs

    sizes = [n for _, n in PIECES.values()]
    hi, lo, *far = call(
        first_kernel,
        [shape_of(NZ, HALO, TR, LANES)] * 2 + [shape_of(n, HALO, TR, LANES) for n in sizes],
        [x_index], [tracers.reshape(-1, LANES), sea_mask, bottom, reaction],
    )
    far = dict(zip(PIECES, far))
    own_piece = far.pop("O")
    far["A"] = lax.ppermute(far["A"], "dx", dx_pairs([(3, 2, 0)], [(0, 1, 0)]))
    far["B"] = lax.ppermute(far["B"], "dx", dx_pairs([(3, 0, 0)], [(0, 3, 0)]))
    far["C"] = lax.ppermute(far["C"], "dx", dx_pairs([(3, 1, 0)], [(0, 2, 0)]))
    velocity, thickness, sea_mask, bottom, diffusivity, far = lax.optimization_barrier(
        (velocity, thickness, sea_mask, bottom, diffusivity, far)
    )
    far["O"] = lax.ppermute(own_piece, "dx", dx_pairs([(3, 3, 1)], [(0, 0, 1)]))
    far["A"] = lax.ppermute(far["A"], "dx", dx_pairs([(2, 2, 1)], [(1, 1, 1)]))
    far["B"] = lax.ppermute(far["B"], "dx", dx_pairs([(0, 0, 1)], [(3, 3, 1)]))
    far["C"] = lax.ppermute(far["C"], "dx", dx_pairs([(1, 1, 1)], [(2, 2, 1)]))
    inside = [(i, i + 1) for i in range(count - 1) if i % XS != XS - 1]
    from_west = lax.ppermute(hi, "dx", inside)
    from_east = lax.ppermute(lo, "dx", [(b, a) for a, b in inside])
    far["O"] = lax.ppermute(far["O"], "dx", collect_pairs([(3, 0)], [(0, 3)]))
    far["A"] = lax.ppermute(far["A"], "dx", collect_pairs([(2, 0)], [(1, 3)]))
    far["C"] = lax.ppermute(far["C"], "dx", collect_pairs([(1, 0)], [(2, 3)]))

    levels = thickness.shape[0]
    first_level = lax.axis_index("group") * levels
    slab = 0.3 * jnp.tanh(velocity) * thickness[None]
    mix = lax.dynamic_slice_in_dim(diffusivity, first_level, levels, axis=0)
    depth = (sea_mask * bottom).astype(jnp.float32)
    own = jnp.concatenate([slab.reshape(-1, 8, LANES), mix, depth[None]], axis=0)
    forward = [(i, i + 1) for i in range(count - 1)]
    backward = [(b, a) for a, b in forward]
    rim_west = lax.ppermute(own[:, 4:], "dx", forward)
    rim_east = lax.ppermute(own[:, :4], "dx", backward)
    blocks = jnp.concatenate([own, rim_west, rim_east], axis=1)
    flux = blocks[: 3 * levels].reshape(3, levels, 16, LANES)
    mix, depth = blocks[3 * levels : 4 * levels], blocks[-1]
    north = [(i, i + 1) for i in range(groups - 1)]
    from_south = lax.ppermute(
        jnp.concatenate([flux[1, :, :, -1], depth[None, :, -1]], axis=0), "dy", north
    )
    depth_north = lax.ppermute(depth[None, :, 0], "dy", [(b, a) for a, b in north])[0]
    flux_south, depth_south = from_south[:-1], from_south[-1]
    level = (first_level + jnp.arange(levels)).astype(jnp.float32)[:, None, None]
    next_x = jnp.concatenate(
        [depth[1:8], depth[12:13], depth[9:12], depth[0:1], depth[13:16], depth[:1] * 0.0], axis=0
    )
    next_y = jnp.concatenate([depth[:, 1:], depth_north[:, None]], axis=1)
    courant_x = jnp.where(level < jnp.minimum(depth, next_x), flux[0], 0.0)
    courant_y = jnp.where(level < jnp.minimum(depth, next_y), flux[1], 0.0)
    courant_z = jnp.where(level + 1.0 < depth, flux[2], 0.0)
    coupling = jnp.where(level + 1.0 < depth, mix, 0.0)
    south = jnp.where(level[:, :, 0] < jnp.minimum(depth_south, depth[:, 0]), flux_south, 0.0)

    def strip_of(three):
        picked = jnp.concatenate([three[:, 9:12], three[:, 0:8], three[:, 12:15]], axis=1)
        picked = jnp.pad(picked, ((0, 0), (0, 2), (2, 3)))
        return picked.reshape(levels, 1, LANES)

    ends = [
        strip_of(jnp.concatenate([south[:, :, None], courant_y[:, :, :2]], axis=2)),
        strip_of(courant_y[:, :, -3:]),
        jnp.zeros((levels, 6, LANES), jnp.float32),
    ]
    table = jnp.concatenate([courant_x, courant_y, courant_z, coupling, *ends], axis=1)
    gathered = lax.all_gather(table, "group", axis=0, tiled=True)
    (coefs,) = call(coefficient_kernel, [shape_of(NZ, 160, LANES)], [], [gathered])

    def swap(east, west):
        return (
            lax.ppermute(east, "dy", north),
            lax.ppermute(west, "dy", [(b, a) for a, b in north]),
        )

    packs = [shape_of(NZ, TR, LANES)] * 2
    joined, east, west = call(
        join_kernel, [shape_of(NZ, 20, TR, LANES)] + packs, [x_index],
        [hi, lo, from_west, from_east] + [far[name] for name in PIECES],
    )

    def scratch(rows):
        return [
            pltpu.VMEM((NZ + 1, rows, TR, LANES), jnp.float32),
            pltpu.VMEM((rows, TR, LANES), jnp.float32),
        ]

    middle, east2, west2 = call(
        functools.partial(step_kernel, -3, 11, HALO, False),
        [shape_of(NZ, 14, TR, LANES)] + packs, [],
        [joined, coefs, gathered, east, west, *swap(east, west), reaction], scratch(14),
    )
    (out,) = call(
        functools.partial(step_kernel, 0, 8, 3, True),
        [shape_of(TR * NZ * 8, LANES)], [],
        [middle, coefs, gathered, east2, west2, *swap(east2, west2), reaction], scratch(8),
    )
    return out.reshape(TR, NZ, 8, LANES)


def solution(mesh):
    placed = (
        P("group", None, "dx", "dy"),
        P("group", None),
        P(None, "group", "dx", "dy"),
        P("group", "dx", "dy"),
        P("dx", "dy"),
        P("dx", "dy"),
        P(None, "dx", "dy"),
    )
    return jax.shard_map(
        transport,
        mesh=mesh,
        in_specs=placed,
        out_specs=P("group", None, "dx", "dy"),
        check_vma=False,
    )
```

time: 337 us -> 236 us (0.70)
  other arithmetic: 58.8 us -> 2.85 us
  waiting for transfers between devices: 147 us -> 93.8 us
  Pallas kernels: 0 us -> 48 us
  local copies, waits for them, and re-layouts: 37 us -> 8.76 us
  blocking collectives: 13.5 us -> 0 us
  between operations: 2.59 us -> 13.8 us
  starting transfers between devices: 74.3 us -> 66.9 us
    ppermute x16 -> x20, waiting for transfers between devices: 147 us -> 93.8 us  [the longest x1 29.7 us: transport(): far['B'] = lax.ppermute(far['B'], 'dx', dx_pairs([(0, 0, 1)], [(3, 3, 1)]))]
    pallas_call x0 -> x5, Pallas kernels: none -> 48 us  [call(): pl.pallas_call(body, out_shape=outs, in_specs=[pl.BlockSpec(memory_space=...]
    mul x29 -> x3, other arithmetic: 29.7 us -> 1.55 us  [the longest x2 1.55 us: transport(): slab = 0.3 * jnp.tanh(velocity) * thickness[None]]
    slice x22 -> x14, local copies, waits for them, and re-layouts: 20.9 us -> 0.84 us  [the longest x2 0.18 us: strip_of(): three[:, 9:12]]
    all_gather x1 -> x0, blocking collectives: 13.5 us -> none  [on_device(): fluxes = lax.all_gather(slab, 'group', axis=1, tiled=True)]
    ppermute x6 -> x0, local copies, waits for them, and re-layouts: 13.1 us -> none  [the longest x3 7.11 us: with_halo(): lax.ppermute(lax.slice_in_dim(block, 0, width, axis=dim), axis, backward)]
    concatenate x7, other arithmetic: 9.97 us -> 0.28 us  [the longest x2 0.16 us: strip_of(): jnp.concatenate([three[:, 9:12], three[:, 0:8], three[:, 12:15]], axis=1)]
    ppermute x16 -> x20, starting transfers between devices: 74.3 us -> 66.9 us  [the longest x1 15.9 us: transport(): far['O'] = lax.ppermute(own_piece, 'dx', dx_pairs([(3, 3, 1)], [(0, 0, 1)]))]
  transfers between devices with their start and end apart: 16 -> 21, of which waited for: 5 -> 10; matrix products, arithmetic and copies ran while one was open for 14% -> 1% of each run, Pallas kernels for 0% -> 4%
where the time goes in v1:
time: 236 us; the launch traced here: 234 us
  waiting for transfers between devices  93.8 us (40%)
  starting transfers between devices  66.9 us (28%)
  Pallas kernels  48 us (20%)
  between operations  13.8 us (6%)
  local copies, waits for them, and re-layouts  8.76 us (4%)
  other arithmetic  2.85 us (1%)
    pallas_call x5, Pallas kernels, call(): pl.pallas_call(body, out_shape=outs, in_specs=[pl.BlockSpec(memory_space=...  48 us
    ppermute x1, waiting for transfers between devices, transport(): far['B'] = lax.ppermute(far['B'], 'dx', dx_pairs([(0, 0, 1)], [(3, 3, 1)]))  29.7 us
    ppermute x2, waiting for transfers between devices, swap(): lax.ppermute(west, 'dy', [(b, a) for a, b in north])  27.3 us
    ppermute x1, starting transfers between devices, transport(): far['O'] = lax.ppermute(own_piece, 'dx', dx_pairs([(3, 3, 1)], [(0, 0, 1)]))  15.9 us
    ppermute x1, waiting for transfers between devices, transport(): rim_east = lax.ppermute(own[:, :4], 'dx', backward)  15.1 us
    ppermute x1, waiting for transfers between devices, transport(): far['O'] = lax.ppermute(far['O'], 'dx', collect_pairs([(3, 0)], [(0, 3)]))  13.4 us
    ppermute x1, starting transfers between devices, transport(): far['B'] = lax.ppermute(far['B'], 'dx', dx_pairs([(3, 0, 0)], [(0, 3, 0)]))  12.9 us
    ppermute x1, starting transfers between devices, transport(): rim_west = lax.ppermute(own[:, 4:], 'dx', forward)  8.25 us
  transfers between devices with their start and end apart: 21, of which 10 were waited for; matrix products, arithmetic and copies ran while one was open for 1% of the time, Pallas kernels for 4%

profile of v1, /device:TPU:6, one launch (start us, length us, event | category | flops | bytes accessed | tf_op | source)
XLA Modules:
  0.0 234.1 jit_solution(11108594108184867860)
XLA Ops:
  6.5 4.3 %shard_map.73 = (f32[32,6,8,128]{3,2,1,0:T(8,128)}, f32[32,6,8,128]{3,2,1,0:T(8,128)}, f32[8,6,8,128]{3,2,1,0:T(8,128)}, f32[8,6,8,128]{3,2,1,0:T(8,128)}, f32[8...) custom-call(s32[1]{0:T(128)} %bitcast.x_ref, f32[2048,128]{1,0:T(8,128)} %bitcast.26, s32[8,128]{1,0:T(8,128)} %sea_ref.1, ...), custom_call_target="tpu_custom_call" | custom-call | tf_op jit(solution)/shard_map/pallas_call | solution.py:34
  10.9 2.9 %collective-permute-start.4 = (f32[8,6,8,128]{3,2,1,0:T(8,128)}, f32[8,6,8,128]{3,2,1,0:T(8,128)S(1)}, u32[]{:S(2)}, u32[]{:S(2)}) collective-permute-start(f32[8,6,8,128]{3,2,1,0:T(8,128)} %get-tuple-element.28), channel_id=1, source_target_pairs={{24,16},{56,48},{32,40},{88,80},{64,72},{96,104},{25,17},{57,49},{... | collective-permute-start | bytes 589832 | tf_op jit(solution)/shard_map/ppermute | solution.py:297
  13.7 12.9 %collective-permute-start.5 = (f32[8,6,8,128]{3,2,1,0:T(8,128)}, f32[8,6,8,128]{3,2,1,0:T(8,128)S(1)}, u32[]{:S(2)}, u32[]{:S(2)}) collective-permute-start(f32[8,6,8,128]{3,2,1,0:T(8,128)} %get-tuple-element.29), channel_id=1, source_target_pairs={{24,0},{56,32},{32,56},{88,64},{64,88},{96,120},{25,1},{57,33},{33... | collective-permute-start | bytes 589832 | tf_op jit(solution)/shard_map/ppermute | solution.py:298
  26.7 1.3 collective-permute-start.6
  28.1 2.1 collective-permute-done.5
  30.2 1.3 collective-permute-done.6
  31.5 0.8 convert_bitcast_fusion
  32.2 0.7 broadcast_multiply_fusion
  33.0 0.8 tanh_multiply_fusion
  33.8 8.3 %collective-permute-start.12 = (f32[17,4,128]{2,1,0:T(4,128)S(1)}, f32[17,4,128]{2,1,0:T(4,128)S(1)}, u32[]{:S(2)}, u32[]{:S(2)}) collective-permute-start(f32[17,4,128]{2,1,0:T(4,128)S(1)} %get-tuple-element.55), channel_id=1, source_target_pairs={{0,8},{8,16},{16,24},{24,32},{32,40},{40,48},{48,56},{56,64},{64,7... | collective-permute-start | bytes 104456 | tf_op jit(solution)/shard_map/ppermute | solution.py:322
  42.1 1.9 collective-permute-start.13
  44.0 15.1 %collective-permute-done.13 = f32[17,4,128]{2,1,0:T(4,128)S(1)} collective-permute-done((f32[17,4,128]{2,1,0:T(4,128)S(1)}, f32[17,4,128]{2,1,0:T(4,128)S(1)}, u32[]{:S(2)}, u32[]{:S(2)}) %collective-permute-start.13) | collective-permute-done | bytes 34848 | tf_op jit(solution)/shard_map/ppermute | solution.py:323
  59.2 0.2 slice_reduce_fusion
  59.5 1.3 collective-permute-start.14
  61.0 4.5 %collective-permute-start.15 = (f32[5,16]{1,0:T(8,128)S(1)}, f32[5,16]{1,0:T(8,128)S(1)}, u32[]{:S(2)}, u32[]{:S(2)}) collective-permute-start(f32[5,16]{1,0:T(8,128)S(1)} %pad_maximum_fusion.4), channel_id=1, source_target_pairs={{0,1},{1,2},{2,3},{3,4},{4,5},{5,6},{6,7},{8,9},{9,10},{10,11},{11... | collective-permute-start | bytes 968 | tf_op jit(solution)/shard_map/ppermute | solution.py:328
  66.0 0.1 copy.20
  66.4 0.1 copy.28
  66.7 0.1 collective-permute-done.15
  67.1 0.1 copy.27
  67.4 3.1 %concatenate.43 = f32[4,72,128]{2,1,0:T(8,128)} concatenate(f32[4,16,128]{2,1,0:T(8,128)S(1)} %get-tuple-element.53, f32[4,16,128]{2,1,0:T(8,128)S(1)} %get-tuple-element.54, f32[4,16,128]{2,1,0:T(8,128)S(1)} %get-tuple-element.50, f32[4,16,128]{2,1,0:T(8,128)S(1)} %get-tuple-element.49, f32[4,1,128]{2,1,0:T(1,128)S(1)} %bitcast.36, f32[4,1,128]{2,1,0:T(1,128)S(1)} %bitcast.35, ...), dimensions={1} | concatenate | bytes 294912 | tf_op jit(solution)/shard_map/concatenate | solution.py:354
  70.5 1.3 collective-permute-start
  71.8 4.6 %collective-permute-start.1 = (f32[32,6,8,128]{3,2,1,0:T(8,128)S(1)}, f32[32,6,8,128]{3,2,1,0:T(8,128)S(1)}, u32[]{:S(2)}, u32[]{:S(2)}) collective-permute-start(f32[32,6,8,128]{3,2,1,0:T(8,128)S(1)} %copy-done.1), channel_id=1, source_target_pairs={{8,0},{16,8},{24,16},{40,32},{48,40},{56,48},{72,64},{80,72},{88,8... | collective-permute-start | bytes 2359304 | tf_op jit(solution)/shard_map/ppermute | solution.py:309
  76.5 15.9 %collective-permute-start.2 = (f32[8,6,8,128]{3,2,1,0:T(8,128)S(1)}, f32[8,6,8,128]{3,2,1,0:T(8,128)S(1)}, u32[]{:S(2)}, u32[]{:S(2)}) collective-permute-start(f32[8,6,8,128]{3,2,1,0:T(8,128)S(1)} %copy-done.14), channel_id=1, source_target_pairs={{24,56},{56,88},{32,0},{88,120},{64,32},{96,64},{25,57},{57,89},{3... | collective-permute-start | bytes 589832 | tf_op jit(solution)/shard_map/ppermute | solution.py:303
  92.4 3.2 %collective-permute-done.2 = f32[8,6,8,128]{3,2,1,0:T(8,128)S(1)} collective-permute-done((f32[8,6,8,128]{3,2,1,0:T(8,128)S(1)}, f32[8,6,8,128]{3,2,1,0:T(8,128)S(1)}, u32[]{:S(2)}, u32[]{:S(2)}) %collective-permute-start.2) | collective-permute-done | bytes 196640 | tf_op jit(solution)/shard_map/ppermute | solution.py:303
  95.5 1.3 collective-permute-start.3
  96.8 0.7 collective-permute-start.7
  97.5 0.7 collective-permute-start.10
  98.2 13.4 %collective-permute-done.3.refs_0_ = f32[8,6,8,128]{3,2,1,0:T(8,128)S(1)} collective-permute-done((f32[8,6,8,128]{3,2,1,0:T(8,128)S(1)}, f32[8,6,8,128]{3,2,1,0:T(8,128)S(1)}, u32[]{:S(2)}, u32[]{:S(2)}) %collective-permute-start.3) | collective-permute-done | bytes 196640 | tf_op jit(solution)/shard_map/ppermute | solution.py:310
  111.6 1.3 collective-permute-start.9
  112.9 1.3 collective-permute-start.8
  114.2 1.3 collective-permute-start.11
  115.5 29.7 %collective-permute-done.9.refs_2_ = f32[8,6,8,128]{3,2,1,0:T(8,128)S(1)} collective-permute-done((f32[8,6,8,128]{3,2,1,0:T(8,128)S(1)}, f32[8,6,8,128]{3,2,1,0:T(8,128)S(1)}, u32[]{:S(2)}, u32[]{:S(2)}) %collective-permute-start.9) | collective-permute-done | bytes 196640 | tf_op jit(solution)/shard_map/ppermute | solution.py:305
  145.2 0.7 copy-done.5
  146.0 0.9 copy-done.2
  146.9 0.9 copy-done.3
  147.8 6.9 %shard_map.74 = (f32[32,20,8,128]{3,2,1,0:T(8,128)}, f32[32,8,128]{2,1,0:T(8,128)}, f32[32,8,128]{2,1,0:T(8,128)}) custom-call(s32[1]{0:T(128)} %bitcast.x_ref, f32[32,6,8,128]{3,2,1,0:T(8,128)} %get-tuple-element.25.hi_ref, f32[32,6,8,128]{3,2,1,0:T(8,128)} %get-tuple-element.26.lo_ref, f32[32,6,8,128]{3,2,1,0:T(8,128)} %copy-done.2, ...), custom_call_target="tpu_custom_call" | custom-call | tf_op jit(solution)/shard_map/pallas_call | solution.py:34
  154.7 1.3 collective-permute-start.16
  156.0 1.3 collective-permute-start.17
  157.3 3.2 %shard_map.75.coef_ref = f32[32,160,128]{2,1,0:T(8,128)} custom-call(f32[32,72,128]{2,1,0:T(8,128)} %all-gather.2.cloned.1.call-done.gathered_ref), custom_call_target="tpu_custom_call" | custom-call | tf_op jit(solution)/shard_map/pallas_call | solution.py:34
  160.5 3.0 %collective-permute-done.17.from_east_ref = f32[32,8,128]{2,1,0:T(8,128)S(1)} collective-permute-done((f32[32,8,128]{2,1,0:T(8,128)}, f32[32,8,128]{2,1,0:T(8,128)S(1)}, u32[]{:S(2)}, u32[]{:S(2)}) %collective-permute-start.17) | collective-permute-done | bytes 131104 | tf_op jit(solution)/shard_map/ppermute | solution.py:361
  163.5 0.7 copy-done.11
  164.1 18.8 %shard_map.76 = (f32[32,14,8,128]{3,2,1,0:T(8,128)}, f32[32,8,128]{2,1,0:T(8,128)}, f32[32,8,128]{2,1,0:T(8,128)}) custom-call(f32[32,20,8,128]{3,2,1,0:T(8,128)} %get-tuple-element.34.q_ref, f32[32,160,128]{2,1,0:T(8,128)} %shard_map.75.coef_ref, f32[32,72,128]{2,1,0:T(8,128)} %all-gather.2.cloned.1.call-done.gathered_ref, ...), custom_call_target="tpu_custom_call" | custom-call | tf_op jit(solution)/shard_map/pallas_call | solution.py:34
  183.0 1.6 collective-permute-start.18
  184.6 1.3 collective-permute-start.19
  185.9 1.6 collective-permute-done.18.from_west_ref
  187.5 24.3 %collective-permute-done.19.from_east_ref = f32[32,8,128]{2,1,0:T(8,128)S(1)} collective-permute-done((f32[32,8,128]{2,1,0:T(8,128)}, f32[32,8,128]{2,1,0:T(8,128)S(1)}, u32[]{:S(2)}, u32[]{:S(2)}) %collective-permute-start.19) | collective-permute-done | bytes 131104 | tf_op jit(solution)/shard_map/ppermute | solution.py:361
  211.9 0.6 copy-done.9
  212.5 14.7 %shard_map.77 = f32[2048,128]{1,0:T(8,128)} custom-call(f32[32,14,8,128]{3,2,1,0:T(8,128)} %get-tuple-element.42.q_ref, f32[32,160,128]{2,1,0:T(8,128)} %shard_map.75.coef_ref, f32[32,72,128]{2,1,0:T(8,128)} %all-gather.2.cloned.1.call-done.gathered_ref, f32[32,8,128]{2,1,0:T(8,128)} %get-tuple-element.43.east_ref, ...), custom_call_target="tpu_custom_call" | custom-call | tf_op jit(solution)/shard_map/pallas_call | solution.py:34
  (74 shorter events, 2.0 us)
Async XLA Ops:
  6.5 150.7 %all-gather.2.cloned.1.call-start = ((), (), s32[]{:S(2)}) async-start(), calls=%async_computation | async-start | bytes 1327104 | tf_op jit(solution)/shard_map/all_gather | solution.py:355
  10.9 59.7 %copy-start = (f32[32,6,8,128]{3,2,1,0:T(8,128)S(1)}, f32[32,6,8,128]{3,2,1,0:T(8,128)}, u32[]{:S(2)}) copy-start(f32[32,6,8,128]{3,2,1,0:T(8,128)} %get-tuple-element.25.hi_ref) | copy-start | bytes 2359300
  10.9 61.0 %copy-start.1 = (f32[32,6,8,128]{3,2,1,0:T(8,128)S(1)}, f32[32,6,8,128]{3,2,1,0:T(8,128)}, u32[]{:S(2)}) copy-start(f32[32,6,8,128]{3,2,1,0:T(8,128)} %get-tuple-element.26.lo_ref) | copy-start | bytes 2359300
  10.9 65.6 %copy-start.14 = (f32[8,6,8,128]{3,2,1,0:T(8,128)S(1)}, f32[8,6,8,128]{3,2,1,0:T(8,128)}, u32[]{:S(2)}) copy-start(f32[8,6,8,128]{3,2,1,0:T(8,128)} %get-tuple-element.27) | copy-start | bytes 589828
  10.9 17.2 %collective-permute-start.4 = (f32[8,6,8,128]{3,2,1,0:T(8,128)}, f32[8,6,8,128]{3,2,1,0:T(8,128)S(1)}, u32[]{:S(2)}, u32[]{:S(2)}) collective-permute-start(f32[8,6,8,128]{3,2,1,0:T(8,128)} %get-tuple-element.28), channel_id=1, source_target_pairs={{24,16},{56,48},{32,40},{88,80},{64,72},{96,104},{25,17},{57,49},{... | collective-permute-start | bytes 589832 | tf_op jit(solution)/shard_map/ppermute | solution.py:297
  13.7 16.4 %collective-permute-start.5 = (f32[8,6,8,128]{3,2,1,0:T(8,128)}, f32[8,6,8,128]{3,2,1,0:T(8,128)S(1)}, u32[]{:S(2)}, u32[]{:S(2)}) collective-permute-start(f32[8,6,8,128]{3,2,1,0:T(8,128)} %get-tuple-element.29), channel_id=1, source_target_pairs={{24,0},{56,32},{32,56},{88,64},{64,88},{96,120},{25,1},{57,33},{33... | collective-permute-start | bytes 589832 | tf_op jit(solution)/shard_map/ppermute | solution.py:298
  26.7 4.8 %collective-permute-start.6 = (f32[8,6,8,128]{3,2,1,0:T(8,128)}, f32[8,6,8,128]{3,2,1,0:T(8,128)S(1)}, u32[]{:S(2)}, u32[]{:S(2)}) collective-permute-start(f32[8,6,8,128]{3,2,1,0:T(8,128)} %get-tuple-element.30), channel_id=1, source_target_pairs={{24,8},{56,40},{32,48},{88,72},{64,80},{96,112},{25,9},{57,41},{33... | collective-permute-start | bytes 589832 | tf_op jit(solution)/shard_map/ppermute | solution.py:299
  28.0 2.1 copy-start.12
  31.5 27.6 %copy-start.13 = (f32[8,6,8,128]{3,2,1,0:T(8,128)}, f32[8,6,8,128]{3,2,1,0:T(8,128)S(1)}, u32[]{:S(2)}) copy-start(f32[8,6,8,128]{3,2,1,0:T(8,128)S(1)} %collective-permute-done.6) | copy-start | bytes 589828
  33.8 25.3 %collective-permute-start.12 = (f32[17,4,128]{2,1,0:T(4,128)S(1)}, f32[17,4,128]{2,1,0:T(4,128)S(1)}, u32[]{:S(2)}, u32[]{:S(2)}) collective-permute-start(f32[17,4,128]{2,1,0:T(4,128)S(1)} %get-tuple-element.55), channel_id=1, source_target_pairs={{0,8},{8,16},{16,24},{24,32},{32,40},{40,48},{48,56},{56,64},{64,7... | collective-permute-start | bytes 104456 | tf_op jit(solution)/shard_map/ppermute | solution.py:322
  42.1 17.0 %collective-permute-start.13 = (f32[17,4,128]{2,1,0:T(4,128)S(1)}, f32[17,4,128]{2,1,0:T(4,128)S(1)}, u32[]{:S(2)}, u32[]{:S(2)}) collective-permute-start(f32[17,4,128]{2,1,0:T(4,128)S(1)} %get-tuple-element.56), channel_id=1, source_target_pairs={{8,0},{16,8},{24,16},{32,24},{40,32},{48,40},{56,48},{64,56},{72,6... | collective-permute-start | bytes 104456 | tf_op jit(solution)/shard_map/ppermute | solution.py:323
  59.5 6.1 %collective-permute-start.14 = (f32[1,16]{1,0:T(1,128)S(1)}, f32[1,16]{1,0:T(1,128)S(1)}, u32[]{:S(2)}, u32[]{:S(2)}) collective-permute-start(f32[1,16]{1,0:T(1,128)S(1)} %bitcast.39), channel_id=1, source_target_pairs={{1,0},{2,1},{3,2},{4,3},{5,4},{6,5},{7,6},{9,8},{10,9},{11,10},{12... | collective-permute-start | bytes 200 | tf_op jit(solution)/shard_map/ppermute | solution.py:331
  61.0 5.9 %collective-permute-start.15 = (f32[5,16]{1,0:T(8,128)S(1)}, f32[5,16]{1,0:T(8,128)S(1)}, u32[]{:S(2)}, u32[]{:S(2)}) collective-permute-start(f32[5,16]{1,0:T(8,128)S(1)} %pad_maximum_fusion.4), channel_id=1, source_target_pairs={{0,1},{1,2},{2,3},{3,4},{4,5},{5,6},{6,7},{8,9},{9,10},{10,11},{11... | collective-permute-start | bytes 968 | tf_op jit(solution)/shard_map/ppermute | solution.py:328
  70.5 74.6 %collective-permute-start = (f32[32,6,8,128]{3,2,1,0:T(8,128)S(1)}, f32[32,6,8,128]{3,2,1,0:T(8,128)S(1)}, u32[]{:S(2)}, u32[]{:S(2)}) collective-permute-start(f32[32,6,8,128]{3,2,1,0:T(8,128)S(1)} %copy-done), channel_id=1, source_target_pairs={{0,8},{8,16},{16,24},{32,40},{40,48},{48,56},{64,72},{72,80},{80,8... | collective-permute-start | bytes 2359304 | tf_op jit(solution)/shard_map/ppermute | solution.py:308
  71.8 74.1 %collective-permute-start.1 = (f32[32,6,8,128]{3,2,1,0:T(8,128)S(1)}, f32[32,6,8,128]{3,2,1,0:T(8,128)S(1)}, u32[]{:S(2)}, u32[]{:S(2)}) collective-permute-start(f32[32,6,8,128]{3,2,1,0:T(8,128)S(1)} %copy-done.1), channel_id=1, source_target_pairs={{8,0},{16,8},{24,16},{40,32},{48,40},{56,48},{72,64},{80,72},{88,8... | collective-permute-start | bytes 2359304 | tf_op jit(solution)/shard_map/ppermute | solution.py:309
  76.5 19.1 %collective-permute-start.2 = (f32[8,6,8,128]{3,2,1,0:T(8,128)S(1)}, f32[8,6,8,128]{3,2,1,0:T(8,128)S(1)}, u32[]{:S(2)}, u32[]{:S(2)}) collective-permute-start(f32[8,6,8,128]{3,2,1,0:T(8,128)S(1)} %copy-done.14), channel_id=1, source_target_pairs={{24,56},{56,88},{32,0},{88,120},{64,32},{96,64},{25,57},{57,89},{3... | collective-permute-start | bytes 589832 | tf_op jit(solution)/shard_map/ppermute | solution.py:303
  95.5 16.0 %collective-permute-start.3 = (f32[8,6,8,128]{3,2,1,0:T(8,128)S(1)}, f32[8,6,8,128]{3,2,1,0:T(8,128)S(1)}, u32[]{:S(2)}, u32[]{:S(2)}) collective-permute-start(f32[8,6,8,128]{3,2,1,0:T(8,128)S(1)} %collective-permute-done.2), channel_id=1, source_target_pairs={{0,24},{56,32},{32,56},{88,64},{64,88},{120,96},{1,25},{57,33},{33... | collective-permute-start | bytes 589832 | tf_op jit(solution)/shard_map/ppermute | solution.py:310
  96.8 16.0 %collective-permute-start.7 = (f32[8,6,8,128]{3,2,1,0:T(8,128)}, f32[8,6,8,128]{3,2,1,0:T(8,128)S(1)}, u32[]{:S(2)}, u32[]{:S(2)}) collective-permute-start(f32[8,6,8,128]{3,2,1,0:T(8,128)} %copy-done.12), channel_id=1, source_target_pairs={{16,48},{48,80},{40,8},{80,112},{72,40},{104,72},{17,49},{49,81},{... | collective-permute-start | bytes 589832 | tf_op jit(solution)/shard_map/ppermute | solution.py:304
  97.5 16.7 %collective-permute-start.10 = (f32[8,6,8,128]{3,2,1,0:T(8,128)}, f32[8,6,8,128]{3,2,1,0:T(8,128)S(1)}, u32[]{:S(2)}, u32[]{:S(2)}) collective-permute-start(f32[8,6,8,128]{3,2,1,0:T(8,128)} %copy-done.13), channel_id=1, source_target_pairs={{8,40},{40,72},{48,16},{72,104},{80,48},{112,80},{9,41},{41,73},{4... | collective-permute-start | bytes 589832 | tf_op jit(solution)/shard_map/ppermute | solution.py:306
  111.6 34.4 %copy-start.4 = (f32[8,6,8,128]{3,2,1,0:T(8,128)}, f32[8,6,8,128]{3,2,1,0:T(8,128)S(1)}, u32[]{:S(2)}) copy-start(f32[8,6,8,128]{3,2,1,0:T(8,128)S(1)} %collective-permute-done.3.refs_0_) | copy-start | bytes 589828
  111.6 33.6 %collective-permute-start.9 = (f32[8,6,8,128]{3,2,1,0:T(8,128)S(1)}, f32[8,6,8,128]{3,2,1,0:T(8,128)S(1)}, u32[]{:S(2)}, u32[]{:S(2)}) collective-permute-start(f32[8,6,8,128]{3,2,1,0:T(8,128)S(1)} %collective-permute-done.5), channel_id=1, source_target_pairs={{0,32},{32,64},{56,24},{64,96},{88,56},{120,88},{1,33},{33,65},{57... | collective-permute-start | bytes 589832 | tf_op jit(solution)/shard_map/ppermute | solution.py:305
  112.9 32.3 %collective-permute-start.8 = (f32[8,6,8,128]{3,2,1,0:T(8,128)S(1)}, f32[8,6,8,128]{3,2,1,0:T(8,128)S(1)}, u32[]{:S(2)}, u32[]{:S(2)}) collective-permute-start(f32[8,6,8,128]{3,2,1,0:T(8,128)S(1)} %collective-permute-done.7), channel_id=1, source_target_pairs={{8,24},{48,32},{40,56},{80,64},{72,88},{112,96},{9,25},{49,33},{41... | collective-permute-start | bytes 589832 | tf_op jit(solution)/shard_map/ppermute | solution.py:311
  114.2 31.0 %collective-permute-start.11 = (f32[8,6,8,128]{3,2,1,0:T(8,128)S(1)}, f32[8,6,8,128]{3,2,1,0:T(8,128)S(1)}, u32[]{:S(2)}, u32[]{:S(2)}) collective-permute-start(f32[8,6,8,128]{3,2,1,0:T(8,128)S(1)} %collective-permute-done.10), channel_id=1, source_target_pairs={{16,24},{40,32},{48,56},{72,64},{80,88},{104,96},{17,25},{41,33},{... | collective-permute-start | bytes 589832 | tf_op jit(solution)/shard_map/ppermute | solution.py:312
  145.1 0.7 copy-start.5
  145.1 0.8 copy-start.6
  145.2 0.8 copy-start.7
  146.0 0.9 copy-start.2
  146.9 0.9 copy-start.3
  154.7 5.9 %collective-permute-start.16 = (f32[32,8,128]{2,1,0:T(8,128)}, f32[32,8,128]{2,1,0:T(8,128)S(1)}, u32[]{:S(2)}, u32[]{:S(2)}) collective-permute-start(f32[32,8,128]{2,1,0:T(8,128)} %get-tuple-element.40.east_ref), channel_id=1, source_target_pairs={{0,1},{1,2},{2,3},{3,4},{4,5},{5,6},{6,7},{8,9},{9,10},{10,11},{11... | collective-permute-start | bytes 393224 | tf_op jit(solution)/shard_map/ppermute | solution.py:360
  156.0 7.5 %collective-permute-start.17 = (f32[32,8,128]{2,1,0:T(8,128)}, f32[32,8,128]{2,1,0:T(8,128)S(1)}, u32[]{:S(2)}, u32[]{:S(2)}) collective-permute-start(f32[32,8,128]{2,1,0:T(8,128)} %get-tuple-element.41.west_ref), channel_id=1, source_target_pairs={{1,0},{2,1},{3,2},{4,3},{5,4},{6,5},{7,6},{9,8},{10,9},{11,10},{12... | collective-permute-start | bytes 393224 | tf_op jit(solution)/shard_map/ppermute | solution.py:361
  160.5 3.0 %copy-start.10 = (f32[32,8,128]{2,1,0:T(8,128)}, f32[32,8,128]{2,1,0:T(8,128)S(1)}, u32[]{:S(2)}) copy-start(f32[32,8,128]{2,1,0:T(8,128)S(1)} %collective-permute-done.16.from_west_ref) | copy-start | bytes 393220
  163.5 0.7 copy-start.11
  183.0 4.6 %collective-permute-start.18 = (f32[32,8,128]{2,1,0:T(8,128)}, f32[32,8,128]{2,1,0:T(8,128)S(1)}, u32[]{:S(2)}, u32[]{:S(2)}) collective-permute-start(f32[32,8,128]{2,1,0:T(8,128)} %get-tuple-element.43.east_ref), channel_id=1, source_target_pairs={{0,1},{1,2},{2,3},{3,4},{4,5},{5,6},{6,7},{8,9},{9,10},{10,11},{11... | collective-permute-start | bytes 393224 | tf_op jit(solution)/shard_map/ppermute | solution.py:360
  184.6 27.3 %collective-permute-start.19 = (f32[32,8,128]{2,1,0:T(8,128)}, f32[32,8,128]{2,1,0:T(8,128)S(1)}, u32[]{:S(2)}, u32[]{:S(2)}) collective-permute-start(f32[32,8,128]{2,1,0:T(8,128)} %get-tuple-element.44.west_ref), channel_id=1, source_target_pairs={{1,0},{2,1},{3,2},{4,3},{5,4},{6,5},{7,6},{9,8},{10,9},{11,10},{12... | collective-permute-start | bytes 393224 | tf_op jit(solution)/shard_map/ppermute | solution.py:361
  187.5 24.4 %copy-start.8 = (f32[32,8,128]{2,1,0:T(8,128)}, f32[32,8,128]{2,1,0:T(8,128)S(1)}, u32[]{:S(2)}) copy-start(f32[32,8,128]{2,1,0:T(8,128)S(1)} %collective-permute-done.18.from_west_ref) | copy-start | bytes 393220
  211.9 0.7 copy-start.9
Sparse Core Ops, SparseCore 0:
  70.6 42.1 all-gather.1

commit v2 on v1

--- a/solution.py
+++ b/solution.py
@@ -13,7 +13,9 @@
 TR = 8
 LANES = 128
 HALO = 6
-PIECES = {"O": (0, 8), "A": (8, 8), "B": (16, 8), "C": (24, 8)}
+VMEM_LIMIT = 24 << 20
+UNROLL = 2
+PIECES = {"O": (0, 8), "A": (8, 8), "B": (16, 9), "C": (25, 7)}
 
 
 def spot(row):
@@ -27,18 +29,50 @@
 
 
 def shape_of(*dims):
-    return jax.ShapeDtypeStruct(dims, jnp.float32)
-
-
-def call(body, outs, scalars, arrays, scratch=()):
+    if INTERPRET:
+        return jax.ShapeDtypeStruct(dims, jnp.float32)
+    return pltpu.VMEM(dims, jnp.float32)
+
+
+def stored(value):
+    return value if INTERPRET else pltpu.with_memory_space_constraint(value, pltpu.HBM)
+
+
+def kept(value):
+    return value if INTERPRET else pltpu.with_memory_space_constraint(value, pltpu.VMEM)
+
+
+def fetched(body, skip, count):
+    def wrapped(*refs):
+        *refs, arrivals = refs
+        sources, places = refs[skip : skip + count], refs[len(refs) - count :]
+        copies = [
+            pltpu.make_async_copy(source, place, arrivals.at[index])
+            for index, (source, place) in enumerate(zip(sources, places))
+        ]
+        for copy in copies:
+            copy.start()
+        for copy in copies:
+            copy.wait()
+        body(*refs[:skip], *places, *refs[skip + count : len(refs) - count])
+
+    return wrapped if count else body
+
+
+def call(body, outs, scalars, arrays, scratch=(), arguments=()):
     return pl.pallas_call(
-        body,
+        fetched(body, len(scalars), len(arguments)),
         out_shape=outs,
-        in_specs=[pl.BlockSpec(memory_space=pltpu.SMEM)] * len(scalars) + vmem(len(arrays)),
+        in_specs=[pl.BlockSpec(memory_space=pltpu.SMEM)] * len(scalars)
+        + [pl.BlockSpec(memory_space=pltpu.HBM)] * len(arguments)
+        + vmem(len(arrays)),
         out_specs=vmem(len(outs)),
-        scratch_shapes=list(scratch),
+        scratch_shapes=list(scratch)
+        + [pltpu.VMEM(value.shape, value.dtype) for value in arguments]
+        + [pltpu.SemaphoreType.DMA((len(arguments),))] * bool(arguments),
+        compiler_params=pltpu.CompilerParams(vmem_limit_bytes=VMEM_LIMIT),
         interpret=INTERPRET,
-    )(*scalars, *arrays)
+    )(*scalars, *map(stored, arguments), *map(kept, arrays))
 
 
 def spun(rates_ref):
@@ -124,19 +158,104 @@
 
 
 UX, AX, BX, UY, AY, BY, CZ, INV, RATIO, LOWER = range(0, 160, 16)
-
-
-def coefficient_kernel(gathered_ref, out_ref):
+ENDS = 160
+
+
+def own_kernel(group_ref, x_ref, sea_ref, bottom_ref, mix_ref, slab_ref, own_ref, *rim_refs):
+    levels = slab_ref.shape[1]
+    first_level = group_ref[0] * levels
+    for kind in range(3):
+        own_ref[kind * levels : (kind + 1) * levels] = slab_ref[kind]
+    own_ref[3 * levels : 4 * levels] = mix_ref[pl.ds(first_level, levels)]
+    own_ref[4 * levels] = (sea_ref[...] * bottom_ref[...]).astype(jnp.float32)
+    low_ref, high_ref, far_ref = rim_refs
+    low_ref[...] = jnp.zeros_like(low_ref)
+    high_ref[...] = jnp.zeros_like(high_ref)
+    for item in range(own_ref.shape[0]):
+        place = pl.ds(4 * (item % 2), 4)
+        low_ref[item // 2, place] = own_ref[item, 0:4]
+        high_ref[item // 2, place] = own_ref[item, 4:8]
+    far_ref[...] = jnp.where(x_ref[0] == XS - 1, high_ref[...], low_ref[...])
+
+
+def blocks_kernel(x_ref, own_ref, west_ref, east_ref, far_ref, blocks_ref, north_ref, south_ref):
+    items = own_ref.shape[0]
+    levels = items // 4
+    blocks_ref[:, 0:8] = own_ref[...]
+    for item in range(items):
+        place = pl.ds(4 * (item % 2), 4)
+        far = far_ref[item // 2, place]
+        blocks_ref[item, 8:12] = jnp.where(x_ref[0] == 0, far, west_ref[item // 2, place])
+        blocks_ref[item, 12:16] = jnp.where(x_ref[0] == XS - 1, far, east_ref[item // 2, place])
+    for index, item in enumerate([*range(levels, 2 * levels), items - 1]):
+        north_ref[index] = jnp.broadcast_to(
+            blocks_ref[item][:, LANES - 1 : LANES], (16, LANES)
+        )
+    south_ref[0] = jnp.broadcast_to(blocks_ref[items - 1][:, 0:1], (16, LANES))
+
+
+def table_kernel(group_ref, blocks_ref, south_ref, north_ref, table_ref, next_ref):
+    items = blocks_ref.shape[0]
+    levels = items // 4
+    lane = lax.broadcasted_iota(jnp.int32, (16, LANES), 1)
+    slot = lax.broadcasted_iota(jnp.int32, (8, LANES), 1) // 8
+    depth = blocks_ref[items - 1]
+    for target, source, count in ((0, 1, 7), (7, 12, 1), (8, 9, 3), (11, 0, 1), (12, 13, 3)):
+        next_ref[target : target + count] = blocks_ref[items - 1, source : source + count]
+    next_ref[15:16] = jnp.zeros((1, LANES), jnp.float32)
+    depth_x = jnp.minimum(depth, next_ref[...])
+    depth_y = jnp.minimum(
+        depth, jnp.where(lane == LANES - 1, north_ref[0], pltpu.roll(depth, LANES - 1, 1))
+    )
+    depth_south = jnp.minimum(south_ref[levels], jnp.broadcast_to(depth[:, 0:1], (16, LANES)))
+    table_ref[...] = jnp.zeros_like(table_ref)
+    for index in range(levels):
+        level = (group_ref[0] * levels + index).astype(jnp.float32)
+        courant_y = jnp.where(level < depth_y, blocks_ref[levels + index], 0.0)
+        table_ref[index, 0:16] = jnp.where(level < depth_x, blocks_ref[index], 0.0)
+        table_ref[index, 16:32] = courant_y
+        wet_below = level + 1.0 < depth
+        table_ref[index, 32:48] = jnp.where(wet_below, blocks_ref[2 * levels + index], 0.0)
+        table_ref[index, 48:64] = jnp.where(wet_below, blocks_ref[3 * levels + index], 0.0)
+        south = jnp.where(level < depth_south, south_ref[index], 0.0)
+        next_ref[...] = jnp.where(lane == LANES - 1, south, courant_y)
+        low = high = jnp.zeros((8, LANES), jnp.float32)
+        for row in range(-3, 11):
+            at = 8 * (row + 3)
+            here = slot == row + 3
+            place = pl.ds(spot(row), 1)
+            low_row = jnp.broadcast_to(next_ref[place], (8, LANES))
+            high_row = jnp.broadcast_to(table_ref[index, pl.ds(16 + spot(row), 1)], (8, LANES))
+            low = jnp.where(here, pltpu.roll(low_row, (at + 3) % LANES, 1), low)
+            high = jnp.where(here, pltpu.roll(high_row, (at + 5) % LANES, 1), high)
+        table_ref[index, 64:65] = low[0:1]
+        table_ref[index, 65:66] = high[0:1]
+
+
+def coefficient_kernel(order, group_ref, *refs):
+    pieces, out_ref = refs[:-1], refs[-1]
+    levels = pieces[0].shape[0]
+    for (flip, turn), piece_ref in zip(order, pieces):
+        owner = (group_ref[0] // 2 + turn) % (len(order) // 2) * 2 + (group_ref[0] % 2 + flip) % 2
+
+        def spread(index, carry):
+            k = owner * levels + index
+            for source, at in ((0, UX), (16, UY)):
+                courant = piece_ref[index, source : source + 16]
+                size = jnp.abs(courant)
+                out_ref[k, at : at + 16] = courant
+                out_ref[k, at + 16 : at + 32] = 0.5 * size
+                out_ref[k, at + 32 : at + 48] = 1.0 - size * (2.0 / 3.0)
+            out_ref[k, CZ : CZ + 16] = piece_ref[index, 32:48]
+            out_ref[k, INV : INV + 16] = piece_ref[index, 48:64]
+            out_ref[k, ENDS : ENDS + 8] = piece_ref[index, 64:72]
+            return carry
+
+        lax.fori_loop(0, levels, spread, 0)
+
     def level(k, carry):
         ratio_before, lower = carry
-        for source, at in ((0, UX), (16, UY)):
-            courant = gathered_ref[k, source : source + 16]
-            size = jnp.abs(courant)
-            out_ref[k, at : at + 16] = courant
-            out_ref[k, at + 16 : at + 32] = 0.5 * size
-            out_ref[k, at + 32 : at + 48] = 1.0 - size * (2.0 / 3.0)
-        out_ref[k, CZ : CZ + 16] = gathered_ref[k, 32:48]
-        upper = gathered_ref[k, 48:64]
+        upper = out_ref[k, INV : INV + 16]
         inverse = 1.0 / (1.0 + lower + upper + lower * ratio_before)
         ratio = -upper * inverse
         out_ref[k, INV : INV + 16] = inverse
@@ -175,7 +294,7 @@
     )
 
 
-def step_kernel(low_row, high_row, base, last, q_ref, coef_ref, gathered_ref, east_ref, west_ref,
+def step_kernel(low_row, high_row, base, last, q_ref, coef_ref, east_ref, west_ref,
                 from_west_ref, from_east_ref, rates_ref, *refs):
     if last:
         out_ref, forward_ref, flux_ref = refs
@@ -190,17 +309,17 @@
         return jnp.broadcast_to(coef_ref[k, pl.ds(at + spot(row), 1), :], (TR, LANES))
 
     def strip(k, at, value):
-        courant = jnp.broadcast_to(gathered_ref[k, pl.ds(at, 1), :], (TR, LANES))
+        courant = jnp.broadcast_to(coef_ref[k, pl.ds(ENDS + at, 1), :], (TR, LANES))
         size = jnp.abs(courant)
         return along_y(value, courant, 0.5 * size, 1.0 - size * (2.0 / 3.0))
 
     forward_ref[...] = jnp.zeros_like(forward_ref)
     flux_ref[...] = jnp.zeros_like(flux_ref)
 
-    def down(k, carry):
+    def down(k):
         below = jnp.minimum(k + 1, NZ - 1)
-        strip_w = strip(k, 64, jnp.where(place < 3, from_west_ref[k], east_ref[k]))
-        strip_e = strip(k, 65, jnp.where(place < 5, west_ref[k], from_east_ref[k]))
+        strip_w = strip(k, 0, jnp.where(place < 3, from_west_ref[k], east_ref[k]))
+        strip_e = strip(k, 1, jnp.where(place < 5, west_ref[k], from_east_ref[k]))
         edges, flux_x = {}, {}
 
         def q(row):
@@ -237,13 +356,15 @@
             forward_ref[k + 1, index] = (
                 advected + coef(k, LOWER, row) * forward_ref[k, index]
             ) * coef(k, INV, row)
-        return carry
-
-    lax.fori_loop(0, NZ, down, 0)
+
+    @pl.loop(0, NZ // UNROLL)
+    def _(part):
+        for index in range(UNROLL):
+            down(part * UNROLL + index)
+
     flux_ref[...] = jnp.zeros_like(flux_ref)
 
-    def up(step, carry):
-        k = NZ - 1 - step
+    def up(k):
         own = {}
         for index, row in enumerate(rows):
             value = forward_ref[k + 1, index] - coef(k, RATIO, row) * flux_ref[index]
@@ -257,13 +378,16 @@
                     own[row] = value
         if not last:
             pack_east_ref[k], pack_west_ref[k] = pack(own.values(), own.keys())
-        return carry
-
-    lax.fori_loop(0, NZ, up, 0)
+
+    @pl.loop(0, NZ // UNROLL)
+    def _(part):
+        for index in range(UNROLL):
+            up(NZ - 1 - part * UNROLL - index)
 
 
 def transport(tracers, reaction, velocity, thickness, sea_mask, bottom, diffusivity):
     groups, stripes, count = lax.axis_size("dy"), lax.axis_size("dx") // XS, lax.axis_size("dx")
+    group = lax.axis_index("group").astype(jnp.int32).reshape(1)
     x_index = (lax.axis_index("dx") % XS).astype(jnp.int32).reshape(1)
 
     def dx_pairs(forth, back):
@@ -290,76 +414,69 @@
     hi, lo, *far = call(
         first_kernel,
         [shape_of(NZ, HALO, TR, LANES)] * 2 + [shape_of(n, HALO, TR, LANES) for n in sizes],
-        [x_index], [tracers.reshape(-1, LANES), sea_mask, bottom, reaction],
+        [x_index], [], (), [tracers.reshape(-1, LANES), sea_mask, bottom, reaction],
+    )
+    velocity, thickness, sea_mask, bottom, diffusivity, far = lax.optimization_barrier(
+        (velocity, thickness, sea_mask, bottom, diffusivity, far)
     )
     far = dict(zip(PIECES, far))
-    own_piece = far.pop("O")
     far["A"] = lax.ppermute(far["A"], "dx", dx_pairs([(3, 2, 0)], [(0, 1, 0)]))
     far["B"] = lax.ppermute(far["B"], "dx", dx_pairs([(3, 0, 0)], [(0, 3, 0)]))
     far["C"] = lax.ppermute(far["C"], "dx", dx_pairs([(3, 1, 0)], [(0, 2, 0)]))
-    velocity, thickness, sea_mask, bottom, diffusivity, far = lax.optimization_barrier(
-        (velocity, thickness, sea_mask, bottom, diffusivity, far)
-    )
-    far["O"] = lax.ppermute(own_piece, "dx", dx_pairs([(3, 3, 1)], [(0, 0, 1)]))
+    far["O"] = lax.ppermute(far["O"], "dx", dx_pairs([(3, 3, 1)], [(0, 0, 1)]))
     far["A"] = lax.ppermute(far["A"], "dx", dx_pairs([(2, 2, 1)], [(1, 1, 1)]))
     far["B"] = lax.ppermute(far["B"], "dx", dx_pairs([(0, 0, 1)], [(3, 3, 1)]))
     far["C"] = lax.ppermute(far["C"], "dx", dx_pairs([(1, 1, 1)], [(2, 2, 1)]))
     inside = [(i, i + 1) for i in range(count - 1) if i % XS != XS - 1]
+    outside = [(b, a) for a, b in inside]
     from_west = lax.ppermute(hi, "dx", inside)
-    from_east = lax.ppermute(lo, "dx", [(b, a) for a, b in inside])
+    from_east = lax.ppermute(lo, "dx", outside)
     far["O"] = lax.ppermute(far["O"], "dx", collect_pairs([(3, 0)], [(0, 3)]))
     far["A"] = lax.ppermute(far["A"], "dx", collect_pairs([(2, 0)], [(1, 3)]))
     far["C"] = lax.ppermute(far["C"], "dx", collect_pairs([(1, 0)], [(2, 3)]))
 
     levels = thickness.shape[0]
-    first_level = lax.axis_index("group") * levels
+    items = 4 * levels + 1
     slab = 0.3 * jnp.tanh(velocity) * thickness[None]
-    mix = lax.dynamic_slice_in_dim(diffusivity, first_level, levels, axis=0)
-    depth = (sea_mask * bottom).astype(jnp.float32)
-    own = jnp.concatenate([slab.reshape(-1, 8, LANES), mix, depth[None]], axis=0)
-    forward = [(i, i + 1) for i in range(count - 1)]
-    backward = [(b, a) for a, b in forward]
-    rim_west = lax.ppermute(own[:, 4:], "dx", forward)
-    rim_east = lax.ppermute(own[:, :4], "dx", backward)
-    blocks = jnp.concatenate([own, rim_west, rim_east], axis=1)
-    flux = blocks[: 3 * levels].reshape(3, levels, 16, LANES)
-    mix, depth = blocks[3 * levels : 4 * levels], blocks[-1]
+    rim = shape_of((items + 1) // 2, 8, LANES)
+
+    own, rim_low, rim_high, rim_far = call(
+        own_kernel, [shape_of(items, 8, LANES)] + [rim] * 3, [group, x_index], [slab], (),
+        [sea_mask, bottom, diffusivity],
+    )
+    rim_west = lax.ppermute(rim_high, "dx", inside)
+    rim_east = lax.ppermute(rim_low, "dx", outside)
+    swapped = [(i, i + 1) for i in range(count - 1) if i % XS == XS - 1]
+    rim_far = lax.ppermute(rim_far, "dx", swapped + [(b, a) for a, b in swapped])
+    blocks, to_north, to_south = call(
+        blocks_kernel,
+        [shape_of(items, 16, LANES), shape_of(levels + 1, 16, LANES), shape_of(1, 16, LANES)],
+        [x_index], [own, rim_west, rim_east, rim_far],
+    )
     north = [(i, i + 1) for i in range(groups - 1)]
-    from_south = lax.ppermute(
-        jnp.concatenate([flux[1, :, :, -1], depth[None, :, -1]], axis=0), "dy", north
-    )
-    depth_north = lax.ppermute(depth[None, :, 0], "dy", [(b, a) for a, b in north])[0]
-    flux_south, depth_south = from_south[:-1], from_south[-1]
-    level = (first_level + jnp.arange(levels)).astype(jnp.float32)[:, None, None]
-    next_x = jnp.concatenate(
-        [depth[1:8], depth[12:13], depth[9:12], depth[0:1], depth[13:16], depth[:1] * 0.0], axis=0
-    )
-    next_y = jnp.concatenate([depth[:, 1:], depth_north[:, None]], axis=1)
-    courant_x = jnp.where(level < jnp.minimum(depth, next_x), flux[0], 0.0)
-    courant_y = jnp.where(level < jnp.minimum(depth, next_y), flux[1], 0.0)
-    courant_z = jnp.where(level + 1.0 < depth, flux[2], 0.0)
-    coupling = jnp.where(level + 1.0 < depth, mix, 0.0)
-    south = jnp.where(level[:, :, 0] < jnp.minimum(depth_south, depth[:, 0]), flux_south, 0.0)
-
-    def strip_of(three):
-        picked = jnp.concatenate([three[:, 9:12], three[:, 0:8], three[:, 12:15]], axis=1)
-        picked = jnp.pad(picked, ((0, 0), (0, 2), (2, 3)))
-        return picked.reshape(levels, 1, LANES)
-
-    ends = [
-        strip_of(jnp.concatenate([south[:, :, None], courant_y[:, :, :2]], axis=2)),
-        strip_of(courant_y[:, :, -3:]),
-        jnp.zeros((levels, 6, LANES), jnp.float32),
-    ]
-    table = jnp.concatenate([courant_x, courant_y, courant_z, coupling, *ends], axis=1)
-    gathered = lax.all_gather(table, "group", axis=0, tiled=True)
-    (coefs,) = call(coefficient_kernel, [shape_of(NZ, 160, LANES)], [], [gathered])
+    south = [(b, a) for a, b in north]
+    (table,) = call(
+        table_kernel, [shape_of(levels, 72, LANES)], [group],
+        [blocks, lax.ppermute(to_north, "dy", north), lax.ppermute(to_south, "dy", south)],
+        [pltpu.VMEM((16, LANES), jnp.float32)],
+    )
+    members = lax.axis_size("group")
+
+    def gather(value, flip, turn):
+        pairs = [((i + 2 * turn) % members ^ flip, i) for i in range(members)]
+        return lax.ppermute(value, "group", pairs)
+
+    turns = [1, 3, 2] if members == 8 else list(range(1, members // 2))
+    along = [table] + [gather(table, 0, turn) for turn in turns]
+    across = [gather(value, 1, 0) for value in along]
+    order = [(flip, turn) for flip in (0, 1) for turn in [0] + turns]
+    (coefs,) = call(
+        functools.partial(coefficient_kernel, order), [shape_of(NZ, ENDS + 8, LANES)],
+        [group], along + across,
+    )
 
     def swap(east, west):
-        return (
-            lax.ppermute(east, "dy", north),
-            lax.ppermute(west, "dy", [(b, a) for a, b in north]),
-        )
+        return lax.ppermute(east, "dy", north), lax.ppermute(west, "dy", south)
 
     packs = [shape_of(NZ, TR, LANES)] * 2
     joined, east, west = call(
@@ -376,12 +493,12 @@
     middle, east2, west2 = call(
         functools.partial(step_kernel, -3, 11, HALO, False),
         [shape_of(NZ, 14, TR, LANES)] + packs, [],
-        [joined, coefs, gathered, east, west, *swap(east, west), reaction], scratch(14),
+        [joined, coefs, east, west, *swap(east, west), reaction], scratch(14),
     )
     (out,) = call(
         functools.partial(step_kernel, 0, 8, 3, True),
-        [shape_of(TR * NZ * 8, LANES)], [],
-        [middle, coefs, gathered, east2, west2, *swap(east2, west2), reaction], scratch(8),
+        [jax.ShapeDtypeStruct((TR * NZ * 8, LANES), jnp.float32)], [],
+        [middle, coefs, east2, west2, *swap(east2, west2), reaction], scratch(8),
     )
     return out.reshape(TR, NZ, 8, LANES)
 

time: 236 us -> 206 us (0.87)
  Pallas kernels: 48 us -> 30.6 us
  between operations: 13.8 us -> 0.42 us
  starting transfers between devices: 66.9 us -> 76.3 us
  local copies, waits for them, and re-layouts: 8.76 us -> 0.01 us
  waiting for transfers between devices: 93.8 us -> 96.7 us
    ppermute x10 -> x18, starting transfers between devices: 42 us -> 64.6 us  [the longest x7 22.4 us: gather(): return lax.ppermute(value, 'group', pairs)]
    pallas_call x5 -> x8, Pallas kernels: 48 us -> 30.6 us  [call(): pl.pallas_call(fetched(body, len(scalars), len(arguments)), out_shape=out...]
    ppermute x1, waiting for transfers between devices: 29.7 us -> 42 us  [transport(): far['B'] = lax.ppermute(far['B'], 'dx', dx_pairs([(0, 0, 1)], [(3, 3, 1)]))]
    ppermute x1, starting transfers between devices: 12.9 us -> 1.3 us  [transport(): far['B'] = lax.ppermute(far['B'], 'dx', dx_pairs([(3, 0, 0)], [(0, 3, 0)]))]
    ppermute x1, waiting for transfers between devices: 0.01 us -> 10.2 us  [transport(): far['A'] = lax.ppermute(far['A'], 'dx', dx_pairs([(3, 2, 0)], [(0, 1, 0)]))]
    ppermute x1, waiting for transfers between devices: 13.4 us -> 4.85 us  [transport(): far['O'] = lax.ppermute(far['O'], 'dx', collect_pairs([(3, 0)], [(0, 3)]))]
    ppermute x10 -> x18, waiting for transfers between devices: 47.3 us -> 39.6 us  [the longest x1 21.5 us: transport(): lax.ppermute(rim_far, 'dx', swapped + [(b, a) for a, b in swapped])]
    unnamed x33 -> x2, local copies, waits for them, and re-layouts: 4.26 us -> 0.01 us
  transfers between devices with their start and end apart: 21 -> 28, of which waited for: 10 -> 11; matrix products, arithmetic and copies ran while one was open for 1% -> 1% of each run, Pallas kernels for 4% -> 3%
where the time goes in v2:
time: 206 us; the launch traced here: 205 us
  waiting for transfers between devices  96.7 us (47%)
  starting transfers between devices  76.3 us (37%)
  Pallas kernels  30.6 us (15%)
    ppermute x1, waiting for transfers between devices, transport(): far['B'] = lax.ppermute(far['B'], 'dx', dx_pairs([(0, 0, 1)], [(3, 3, 1)]))  42 us
    pallas_call x8, Pallas kernels, call(): pl.pallas_call(fetched(body, len(scalars), len(arguments)), out_shape=out...  30.6 us
    ppermute x7, starting transfers between devices, gather(): return lax.ppermute(value, 'group', pairs)  22.4 us
    ppermute x1, waiting for transfers between devices, transport(): lax.ppermute(rim_far, 'dx', swapped + [(b, a) for a, b in swapped])  21.5 us
    ppermute x1, starting transfers between devices, transport(): far['O'] = lax.ppermute(far['O'], 'dx', dx_pairs([(3, 3, 1)], [(0, 0, 1)]))  15.7 us
    ppermute x4, waiting for transfers between devices, swap(): return (lax.ppermute(east, 'dy', north), lax.ppermute(west, 'dy', south))  10.8 us
    ppermute x1, waiting for transfers between devices, transport(): far['A'] = lax.ppermute(far['A'], 'dx', dx_pairs([(3, 2, 0)], [(0, 1, 0)]))  10.2 us
    ppermute x1, starting transfers between devices, transport(): lax.ppermute(rim_far, 'dx', swapped + [(b, a) for a, b in swapped])  8.1 us
  transfers between devices with their start and end apart: 28, of which 11 were waited for; matrix products, arithmetic and copies ran while one was open for 1% of the time, Pallas kernels for 3%

profile of v2, /device:TPU:6, one launch (start us, length us, event | category | flops | bytes accessed | tf_op | source)
XLA Modules:
  0.0 205.5 jit_solution(2801713004460458345)
XLA Ops:
  0.0 3.0 %shard_map.73 = (f32[32,6,8,128]{3,2,1,0:T(8,128)S(1)}, f32[32,6,8,128]{3,2,1,0:T(8,128)S(1)}, f32[8,6,8,128]{3,2,1,0:T(8,128)S(1)}, f32[8,6,8,128]{3,2,1,0:T(8,...) custom-call(s32[1]{0:T(128)} %bitcast.refs_0_.x_ref.refs_1_, f32[2048,128]{1,0:T(8,128)} %bitcast.4, ...), custom_call_target="tpu_custom_call" | custom-call | tf_op jit(solution)/shard_map/pallas_call | solution.py:63
  3.0 15.7 %collective-permute-start.2 = (f32[8,6,8,128]{3,2,1,0:T(8,128)S(1)}, f32[8,6,8,128]{3,2,1,0:T(8,128)S(1)}, u32[]{:S(2)}, u32[]{:S(2)}) collective-permute-start(f32[8,6,8,128]{3,2,1,0:T(8,128)S(1)} %get-tuple-element.39), channel_id=1, source_target_pairs={{24,56},{56,88},{32,0},{88,120},{64,32},{96,64},{25,57},{57,89},{3... | collective-permute-start | bytes 589832 | tf_op jit(solution)/shard_map/ppermute | solution.py:426
  18.8 1.3 collective-permute-start.9
  20.1 0.7 broadcast_multiply_fusion
  20.8 0.8 tanh_multiply_fusion.refs_5_
  21.6 1.0 shard_map.75
  22.6 1.3 collective-permute-start.12
  23.9 4.5 %collective-permute-start.13 = (f32[9,8,128]{2,1,0:T(8,128)S(1)}, f32[9,8,128]{2,1,0:T(8,128)S(1)}, u32[]{:S(2)}, u32[]{:S(2)}) collective-permute-start(f32[9,8,128]{2,1,0:T(8,128)S(1)} %get-tuple-element.51), channel_id=1, source_target_pairs={{8,0},{16,8},{24,16},{40,32},{48,40},{56,48},{72,64},{80,72},{88,8... | collective-permute-start | bytes 110600 | tf_op jit(solution)/shard_map/ppermute | solution.py:448
  28.5 8.1 %collective-permute-start.14 = (f32[9,8,128]{2,1,0:T(8,128)S(1)}, f32[9,8,128]{2,1,0:T(8,128)S(1)}, u32[]{:S(2)}, u32[]{:S(2)}) collective-permute-start(f32[9,8,128]{2,1,0:T(8,128)S(1)} %get-tuple-element.52), channel_id=1, source_target_pairs={{24,32},{56,64},{88,96},{32,24},{64,56},{96,88},{25,33},{57,65},{8... | collective-permute-start | bytes 110600 | tf_op jit(solution)/shard_map/ppermute | solution.py:450
  36.6 21.5 %collective-permute-done.14.far_ref = f32[9,8,128]{2,1,0:T(8,128)S(1)} collective-permute-done((f32[9,8,128]{2,1,0:T(8,128)S(1)}, f32[9,8,128]{2,1,0:T(8,128)S(1)}, u32[]{:S(2)}, u32[]{:S(2)}) %collective-permute-start.14) | collective-permute-done | bytes 36896 | tf_op jit(solution)/shard_map/ppermute | solution.py:450
  58.2 1.3 collective-permute-start.15
  59.4 1.3 collective-permute-start
  60.7 1.3 collective-permute-start.16
  62.0 4.2 %collective-permute-done.16.north_ref = f32[1,16,128]{2,1,0:T(8,128)S(1)} collective-permute-done((f32[1,16,128]{2,1,0:T(8,128)S(1)}, f32[1,16,128]{2,1,0:T(8,128)S(1)}, u32[]{:S(2)}, u32[]{:S(2)}) %collective-permute-start.16) | collective-permute-done | bytes 8224 | tf_op jit(solution)/shard_map/ppermute | solution.py:460
  66.3 4.6 %collective-permute-start.1 = (f32[32,6,8,128]{3,2,1,0:T(8,128)S(1)}, f32[32,6,8,128]{3,2,1,0:T(8,128)S(1)}, u32[]{:S(2)}, u32[]{:S(2)}) collective-permute-start(f32[32,6,8,128]{3,2,1,0:T(8,128)S(1)} %get-tuple-element.34.lo_ref), channel_id=1, source_target_pairs={{8,0},{16,8},{24,16},{40,32},{48,40},{56,48},{72,64},{80,72},{88,8... | collective-permute-start | bytes 2359304 | tf_op jit(solution)/shard_map/ppermute | solution.py:433
  70.9 1.3 collective-permute-start.7
  72.2 1.3 collective-permute-start.4
  73.5 0.3 shard_map.77.refs_0_
  73.8 4.9 %collective-permute-start.17 = (f32[4,72,128]{2,1,0:T(8,128)S(1)}, f32[4,72,128]{2,1,0:T(8,128)S(1)}, u32[]{:S(2)}, u32[]{:S(2)}) collective-permute-start(f32[4,72,128]{2,1,0:T(8,128)S(1)} %shard_map.77.refs_0_), channel_id=1, source_target_pairs={{256,0},{384,128},{512,256},{640,384},{768,512},{896,640},{0,768},... | collective-permute-start | bytes 442376 | tf_op jit(solution)/shard_map/ppermute | solution.py:467
  78.7 10.2 %collective-permute-done.4 = f32[8,6,8,128]{3,2,1,0:T(8,128)S(1)} collective-permute-done((f32[8,6,8,128]{3,2,1,0:T(8,128)S(1)}, f32[8,6,8,128]{3,2,1,0:T(8,128)S(1)}, u32[]{:S(2)}, u32[]{:S(2)}) %collective-permute-start.4) | collective-permute-done | bytes 196640 | tf_op jit(solution)/shard_map/ppermute | solution.py:423
  88.9 4.1 %collective-permute-start.18 = (f32[4,72,128]{2,1,0:T(8,128)S(1)}, f32[4,72,128]{2,1,0:T(8,128)S(1)}, u32[]{:S(2)}, u32[]{:S(2)}) collective-permute-start(f32[4,72,128]{2,1,0:T(8,128)S(1)} %shard_map.77.refs_0_), channel_id=1, source_target_pairs={{768,0},{896,128},{0,256},{128,384},{256,512},{384,640},{512,768},... | collective-permute-start | bytes 442376 | tf_op jit(solution)/shard_map/ppermute | solution.py:467
  93.0 0.7 collective-permute-start.10
  93.7 4.8 %collective-permute-start.19 = (f32[4,72,128]{2,1,0:T(8,128)S(1)}, f32[4,72,128]{2,1,0:T(8,128)S(1)}, u32[]{:S(2)}, u32[]{:S(2)}) collective-permute-start(f32[4,72,128]{2,1,0:T(8,128)S(1)} %shard_map.77.refs_0_), channel_id=1, source_target_pairs={{512,0},{640,128},{768,256},{896,384},{0,512},{128,640},{256,768},... | collective-permute-start | bytes 442376 | tf_op jit(solution)/shard_map/ppermute | solution.py:467
  98.5 0.6 collective-permute-done.18.refs_2_
  99.1 0.7 collective-permute-start.5
  99.8 2.4 %collective-permute-done.19.refs_3_ = f32[4,72,128]{2,1,0:T(8,128)S(1)} collective-permute-done((f32[4,72,128]{2,1,0:T(8,128)S(1)}, f32[4,72,128]{2,1,0:T(8,128)S(1)}, u32[]{:S(2)}, u32[]{:S(2)}) %collective-permute-start.19) | collective-permute-done | bytes 147488 | tf_op jit(solution)/shard_map/ppermute | solution.py:467
  102.2 1.3 collective-permute-start.3
  103.5 1.3 collective-permute-start.8
  104.9 1.3 collective-permute-start.6
  106.2 4.9 %collective-permute-done.3.refs_0_ = f32[8,6,8,128]{3,2,1,0:T(8,128)S(1)} collective-permute-done((f32[8,6,8,128]{3,2,1,0:T(8,128)S(1)}, f32[8,6,8,128]{3,2,1,0:T(8,128)S(1)}, u32[]{:S(2)}, u32[]{:S(2)}) %collective-permute-start.3) | collective-permute-done | bytes 196640 | tf_op jit(solution)/shard_map/ppermute | solution.py:434
  111.0 1.3 collective-permute-start.11
  112.3 42.0 %collective-permute-done.8.refs_2_ = f32[9,6,8,128]{3,2,1,0:T(8,128)S(1)} collective-permute-done((f32[9,6,8,128]{3,2,1,0:T(8,128)S(1)}, f32[9,6,8,128]{3,2,1,0:T(8,128)S(1)}, u32[]{:S(2)}, u32[]{:S(2)}) %collective-permute-start.8) | collective-permute-done | bytes 221216 | tf_op jit(solution)/shard_map/ppermute | solution.py:428
  154.3 1.9 collective-permute-start.20
  156.3 2.4 %collective-permute-start.21 = (f32[4,72,128]{2,1,0:T(8,128)S(1)}, f32[4,72,128]{2,1,0:T(8,128)S(1)}, u32[]{:S(2)}, u32[]{:S(2)}) collective-permute-start(f32[4,72,128]{2,1,0:T(8,128)S(1)} %collective-permute-done.17.refs_1_), channel_id=1, source_target_pairs={{128,0},{0,128},{384,256},{256,384},{640,512},{512,640},{896,768},... | collective-permute-start | bytes 442376 | tf_op jit(solution)/shard_map/ppermute | solution.py:467
  158.7 1.9 collective-permute-start.22
  160.6 2.4 %collective-permute-start.23 = (f32[4,72,128]{2,1,0:T(8,128)S(1)}, f32[4,72,128]{2,1,0:T(8,128)S(1)}, u32[]{:S(2)}, u32[]{:S(2)}) collective-permute-start(f32[4,72,128]{2,1,0:T(8,128)S(1)} %collective-permute-done.19.refs_3_), channel_id=1, source_target_pairs={{128,0},{0,128},{384,256},{256,384},{640,512},{512,640},{896,768},... | collective-permute-start | bytes 442376 | tf_op jit(solution)/shard_map/ppermute | solution.py:467
  163.1 3.4 %shard_map.74 = (f32[32,20,8,128]{3,2,1,0:T(8,128)S(1)}, f32[32,8,128]{2,1,0:T(8,128)S(1)}, f32[32,8,128]{2,1,0:T(8,128)S(1)}) custom-call(s32[1]{0:T(128)} %bitcast.refs_0_.x_ref.refs_1_, f32[32,6,8,128]{3,2,1,0:T(8,128)S(1)} %get-tuple-element.33.hi_ref, f32[32,6,8,128]{3,2,1,0:T(8,128)S(1)} %get-tuple-element.34.lo_ref, ...), custom_call_target="tpu_custom_call" | custom-call | tf_op jit(solution)/shard_map/pallas_call | solution.py:63
  166.5 1.3 collective-permute-start.24
  167.8 1.3 collective-permute-start.25
  169.1 0.7 shard_map.78.coef_ref
  169.8 1.1 collective-permute-done.24.from_west_ref
  170.9 4.1 %collective-permute-done.25.from_east_ref = f32[32,8,128]{2,1,0:T(8,128)S(1)} collective-permute-done((f32[32,8,128]{2,1,0:T(8,128)S(1)}, f32[32,8,128]{2,1,0:T(8,128)S(1)}, u32[]{:S(2)}, u32[]{:S(2)}) %collective-permute-start.25) | collective-permute-done | bytes 131104 | tf_op jit(solution)/shard_map/ppermute | solution.py:479
  175.1 14.8 %shard_map.79 = (f32[32,14,8,128]{3,2,1,0:T(8,128)S(1)}, f32[32,8,128]{2,1,0:T(8,128)S(1)}, f32[32,8,128]{2,1,0:T(8,128)S(1)}) custom-call(f32[32,20,8,128]{3,2,1,0:T(8,128)S(1)} %get-tuple-element.43.q_ref, f32[32,168,128]{2,1,0:T(8,128)S(1)} %shard_map.78.coef_ref, f32[32,8,128]{2,1,0:T(8,128)S(1)} %get-tuple-element.56.east_ref, ...), custom_call_target="tpu_custom_call" | custom-call | tf_op jit(solution)/shard_map/pallas_call | solution.py:63
  189.8 1.4 collective-permute-start.26
  191.3 1.3 collective-permute-start.27
  192.6 1.2 collective-permute-done.26.from_west_ref
  193.8 4.4 %collective-permute-done.27.from_east_ref = f32[32,8,128]{2,1,0:T(8,128)S(1)} collective-permute-done((f32[32,8,128]{2,1,0:T(8,128)S(1)}, f32[32,8,128]{2,1,0:T(8,128)S(1)}, u32[]{:S(2)}, u32[]{:S(2)}) %collective-permute-start.27) | collective-permute-done | bytes 131104 | tf_op jit(solution)/shard_map/ppermute | solution.py:479
  198.2 7.3 %shard_map.80 = f32[2048,128]{1,0:T(8,128)} custom-call(f32[32,14,8,128]{3,2,1,0:T(8,128)S(1)} %get-tuple-element.58.q_ref, f32[32,168,128]{2,1,0:T(8,128)S(1)} %shard_map.78.coef_ref, f32[32,8,128]{2,1,0:T(8,128)S(1)} %get-tuple-element.59.east_ref, f32[32,8,128]{2,1,0:T(8,128)S(1)} %get-tuple-element.60.west_ref, ...), custom_call_target="tpu_custom_call" | custom-call | tf_op jit(solution)/shard_map/pallas_call | solution.py:63
  (20 shorter events, 0.1 us)
Async XLA Ops:
  3.0 70.8 %collective-permute-start.2 = (f32[8,6,8,128]{3,2,1,0:T(8,128)S(1)}, f32[8,6,8,128]{3,2,1,0:T(8,128)S(1)}, u32[]{:S(2)}, u32[]{:S(2)}) collective-permute-start(f32[8,6,8,128]{3,2,1,0:T(8,128)S(1)} %get-tuple-element.39), channel_id=1, source_target_pairs={{24,56},{56,88},{32,0},{88,120},{64,32},{96,64},{25,57},{57,89},{3... | collective-permute-start | bytes 589832 | tf_op jit(solution)/shard_map/ppermute | solution.py:426
  18.8 53.4 %collective-permute-start.9 = (f32[7,6,8,128]{3,2,1,0:T(8,128)S(1)}, f32[7,6,8,128]{3,2,1,0:T(8,128)S(1)}, u32[]{:S(2)}, u32[]{:S(2)}) collective-permute-start(f32[7,6,8,128]{3,2,1,0:T(8,128)S(1)} %get-tuple-element.42), channel_id=1, source_target_pairs={{24,8},{56,40},{32,48},{88,72},{64,80},{96,112},{25,9},{57,41},{33... | collective-permute-start | bytes 516104 | tf_op jit(solution)/shard_map/ppermute | solution.py:425
  22.6 14.0 %collective-permute-start.12 = (f32[9,8,128]{2,1,0:T(8,128)S(1)}, f32[9,8,128]{2,1,0:T(8,128)S(1)}, u32[]{:S(2)}, u32[]{:S(2)}) collective-permute-start(f32[9,8,128]{2,1,0:T(8,128)S(1)} %get-tuple-element.50), channel_id=1, source_target_pairs={{0,8},{8,16},{16,24},{32,40},{40,48},{48,56},{64,72},{72,80},{80,8... | collective-permute-start | bytes 110600 | tf_op jit(solution)/shard_map/ppermute | solution.py:447
  23.9 12.7 %collective-permute-start.13 = (f32[9,8,128]{2,1,0:T(8,128)S(1)}, f32[9,8,128]{2,1,0:T(8,128)S(1)}, u32[]{:S(2)}, u32[]{:S(2)}) collective-permute-start(f32[9,8,128]{2,1,0:T(8,128)S(1)} %get-tuple-element.51), channel_id=1, source_target_pairs={{8,0},{16,8},{24,16},{40,32},{48,40},{56,48},{72,64},{80,72},{88,8... | collective-permute-start | bytes 110600 | tf_op jit(solution)/shard_map/ppermute | solution.py:448
  28.5 29.6 %collective-permute-start.14 = (f32[9,8,128]{2,1,0:T(8,128)S(1)}, f32[9,8,128]{2,1,0:T(8,128)S(1)}, u32[]{:S(2)}, u32[]{:S(2)}) collective-permute-start(f32[9,8,128]{2,1,0:T(8,128)S(1)} %get-tuple-element.52), channel_id=1, source_target_pairs={{24,32},{56,64},{88,96},{32,24},{64,56},{96,88},{25,33},{57,65},{8... | collective-permute-start | bytes 110600 | tf_op jit(solution)/shard_map/ppermute | solution.py:450
  58.2 12.7 %collective-permute-start.15 = (f32[5,16,128]{2,1,0:T(8,128)S(1)}, f32[5,16,128]{2,1,0:T(8,128)S(1)}, u32[]{:S(2)}, u32[]{:S(2)}) collective-permute-start(f32[5,16,128]{2,1,0:T(8,128)S(1)} %get-tuple-element.54), channel_id=1, source_target_pairs={{0,1},{1,2},{2,3},{3,4},{4,5},{5,6},{6,7},{8,9},{9,10},{10,11},{11... | collective-permute-start | bytes 122888 | tf_op jit(solution)/shard_map/ppermute | solution.py:460
  59.4 101.2 %collective-permute-start = (f32[32,6,8,128]{3,2,1,0:T(8,128)S(1)}, f32[32,6,8,128]{3,2,1,0:T(8,128)S(1)}, u32[]{:S(2)}, u32[]{:S(2)}) collective-permute-start(f32[32,6,8,128]{3,2,1,0:T(8,128)S(1)} %get-tuple-element.33.hi_ref), channel_id=1, source_target_pairs={{0,8},{8,16},{16,24},{32,40},{40,48},{48,56},{64,72},{72,80},{80,8... | collective-permute-start | bytes 2359304 | tf_op jit(solution)/shard_map/ppermute | solution.py:432
  60.7 5.5 %collective-permute-start.16 = (f32[1,16,128]{2,1,0:T(8,128)S(1)}, f32[1,16,128]{2,1,0:T(8,128)S(1)}, u32[]{:S(2)}, u32[]{:S(2)}) collective-permute-start(f32[1,16,128]{2,1,0:T(8,128)S(1)} %get-tuple-element.55), channel_id=1, source_target_pairs={{1,0},{2,1},{3,2},{4,3},{5,4},{6,5},{7,6},{9,8},{10,9},{11,10},{12... | collective-permute-start | bytes 24584 | tf_op jit(solution)/shard_map/ppermute | solution.py:460
  66.3 96.8 %collective-permute-start.1 = (f32[32,6,8,128]{3,2,1,0:T(8,128)S(1)}, f32[32,6,8,128]{3,2,1,0:T(8,128)S(1)}, u32[]{:S(2)}, u32[]{:S(2)}) collective-permute-start(f32[32,6,8,128]{3,2,1,0:T(8,128)S(1)} %get-tuple-element.34.lo_ref), channel_id=1, source_target_pairs={{8,0},{16,8},{24,16},{40,32},{48,40},{56,48},{72,64},{80,72},{88,8... | collective-permute-start | bytes 2359304 | tf_op jit(solution)/shard_map/ppermute | solution.py:433
  70.9 22.1 %collective-permute-start.7 = (f32[9,6,8,128]{3,2,1,0:T(8,128)S(1)}, f32[9,6,8,128]{3,2,1,0:T(8,128)S(1)}, u32[]{:S(2)}, u32[]{:S(2)}) collective-permute-start(f32[9,6,8,128]{3,2,1,0:T(8,128)S(1)} %get-tuple-element.41), channel_id=1, source_target_pairs={{24,0},{56,32},{32,56},{88,64},{64,88},{96,120},{25,1},{57,33},{33... | collective-permute-start | bytes 663560 | tf_op jit(solution)/shard_map/ppermute | solution.py:424
  72.2 16.7 %collective-permute-start.4 = (f32[8,6,8,128]{3,2,1,0:T(8,128)S(1)}, f32[8,6,8,128]{3,2,1,0:T(8,128)S(1)}, u32[]{:S(2)}, u32[]{:S(2)}) collective-permute-start(f32[8,6,8,128]{3,2,1,0:T(8,128)S(1)} %get-tuple-element.40), channel_id=1, source_target_pairs={{24,16},{56,48},{32,40},{88,80},{64,72},{96,104},{25,17},{57,49},{... | collective-permute-start | bytes 589832 | tf_op jit(solution)/shard_map/ppermute | solution.py:423
  73.8 19.9 %collective-permute-start.17 = (f32[4,72,128]{2,1,0:T(8,128)S(1)}, f32[4,72,128]{2,1,0:T(8,128)S(1)}, u32[]{:S(2)}, u32[]{:S(2)}) collective-permute-start(f32[4,72,128]{2,1,0:T(8,128)S(1)} %shard_map.77.refs_0_), channel_id=1, source_target_pairs={{256,0},{384,128},{512,256},{640,384},{768,512},{896,640},{0,768},... | collective-permute-start | bytes 442376 | tf_op jit(solution)/shard_map/ppermute | solution.py:467
  88.9 10.2 %collective-permute-start.18 = (f32[4,72,128]{2,1,0:T(8,128)S(1)}, f32[4,72,128]{2,1,0:T(8,128)S(1)}, u32[]{:S(2)}, u32[]{:S(2)}) collective-permute-start(f32[4,72,128]{2,1,0:T(8,128)S(1)} %shard_map.77.refs_0_), channel_id=1, source_target_pairs={{768,0},{896,128},{0,256},{128,384},{256,512},{384,640},{512,768},... | collective-permute-start | bytes 442376 | tf_op jit(solution)/shard_map/ppermute | solution.py:467
  93.0 10.5 %collective-permute-start.10 = (f32[7,6,8,128]{3,2,1,0:T(8,128)S(1)}, f32[7,6,8,128]{3,2,1,0:T(8,128)S(1)}, u32[]{:S(2)}, u32[]{:S(2)}) collective-permute-start(f32[7,6,8,128]{3,2,1,0:T(8,128)S(1)} %collective-permute-done.9), channel_id=1, source_target_pairs={{8,40},{40,72},{48,16},{72,104},{80,48},{112,80},{9,41},{41,73},{4... | collective-permute-start | bytes 516104 | tf_op jit(solution)/shard_map/ppermute | solution.py:429
  93.7 8.5 %collective-permute-start.19 = (f32[4,72,128]{2,1,0:T(8,128)S(1)}, f32[4,72,128]{2,1,0:T(8,128)S(1)}, u32[]{:S(2)}, u32[]{:S(2)}) collective-permute-start(f32[4,72,128]{2,1,0:T(8,128)S(1)} %shard_map.77.refs_0_), channel_id=1, source_target_pairs={{512,0},{640,128},{768,256},{896,384},{0,512},{128,640},{256,768},... | collective-permute-start | bytes 442376 | tf_op jit(solution)/shard_map/ppermute | solution.py:467
  99.1 5.7 %collective-permute-start.5 = (f32[8,6,8,128]{3,2,1,0:T(8,128)S(1)}, f32[8,6,8,128]{3,2,1,0:T(8,128)S(1)}, u32[]{:S(2)}, u32[]{:S(2)}) collective-permute-start(f32[8,6,8,128]{3,2,1,0:T(8,128)S(1)} %collective-permute-done.4), channel_id=1, source_target_pairs={{16,48},{48,80},{40,8},{80,112},{72,40},{104,72},{17,49},{49,81},{... | collective-permute-start | bytes 589832 | tf_op jit(solution)/shard_map/ppermute | solution.py:427
  102.2 8.8 %collective-permute-start.3 = (f32[8,6,8,128]{3,2,1,0:T(8,128)S(1)}, f32[8,6,8,128]{3,2,1,0:T(8,128)S(1)}, u32[]{:S(2)}, u32[]{:S(2)}) collective-permute-start(f32[8,6,8,128]{3,2,1,0:T(8,128)S(1)} %collective-permute-done.2), channel_id=1, source_target_pairs={{0,24},{56,32},{32,56},{88,64},{64,88},{120,96},{1,25},{57,33},{33... | collective-permute-start | bytes 589832 | tf_op jit(solution)/shard_map/ppermute | solution.py:434
  103.5 50.8 %collective-permute-start.8 = (f32[9,6,8,128]{3,2,1,0:T(8,128)S(1)}, f32[9,6,8,128]{3,2,1,0:T(8,128)S(1)}, u32[]{:S(2)}, u32[]{:S(2)}) collective-permute-start(f32[9,6,8,128]{3,2,1,0:T(8,128)S(1)} %collective-permute-done.7), channel_id=1, source_target_pairs={{0,32},{32,64},{56,24},{64,96},{88,56},{120,88},{1,33},{33,65},{57... | collective-permute-start | bytes 663560 | tf_op jit(solution)/shard_map/ppermute | solution.py:428
  104.9 53.8 %collective-permute-start.6 = (f32[8,6,8,128]{3,2,1,0:T(8,128)S(1)}, f32[8,6,8,128]{3,2,1,0:T(8,128)S(1)}, u32[]{:S(2)}, u32[]{:S(2)}) collective-permute-start(f32[8,6,8,128]{3,2,1,0:T(8,128)S(1)} %collective-permute-done.5), channel_id=1, source_target_pairs={{8,24},{48,32},{40,56},{80,64},{72,88},{112,96},{9,25},{49,33},{41... | collective-permute-start | bytes 589832 | tf_op jit(solution)/shard_map/ppermute | solution.py:435
  111.0 45.3 %collective-permute-start.11 = (f32[7,6,8,128]{3,2,1,0:T(8,128)S(1)}, f32[7,6,8,128]{3,2,1,0:T(8,128)S(1)}, u32[]{:S(2)}, u32[]{:S(2)}) collective-permute-start(f32[7,6,8,128]{3,2,1,0:T(8,128)S(1)} %collective-permute-done.10), channel_id=1, source_target_pairs={{16,24},{40,32},{48,56},{72,64},{80,88},{104,96},{17,25},{41,33},{... | collective-permute-start | bytes 516104 | tf_op jit(solution)/shard_map/ppermute | solution.py:436
  154.3 13.4 %collective-permute-start.20 = (f32[4,72,128]{2,1,0:T(8,128)S(1)}, f32[4,72,128]{2,1,0:T(8,128)S(1)}, u32[]{:S(2)}, u32[]{:S(2)}) collective-permute-start(f32[4,72,128]{2,1,0:T(8,128)S(1)} %shard_map.77.refs_0_), channel_id=1, source_target_pairs={{128,0},{0,128},{384,256},{256,384},{640,512},{512,640},{896,768},... | collective-permute-start | bytes 442376 | tf_op jit(solution)/shard_map/ppermute | solution.py:467
  156.3 12.8 %collective-permute-start.21 = (f32[4,72,128]{2,1,0:T(8,128)S(1)}, f32[4,72,128]{2,1,0:T(8,128)S(1)}, u32[]{:S(2)}, u32[]{:S(2)}) collective-permute-start(f32[4,72,128]{2,1,0:T(8,128)S(1)} %collective-permute-done.17.refs_1_), channel_id=1, source_target_pairs={{128,0},{0,128},{384,256},{256,384},{640,512},{512,640},{896,768},... | collective-permute-start | bytes 442376 | tf_op jit(solution)/shard_map/ppermute | solution.py:467
  158.7 10.4 %collective-permute-start.22 = (f32[4,72,128]{2,1,0:T(8,128)S(1)}, f32[4,72,128]{2,1,0:T(8,128)S(1)}, u32[]{:S(2)}, u32[]{:S(2)}) collective-permute-start(f32[4,72,128]{2,1,0:T(8,128)S(1)} %collective-permute-done.18.refs_2_), channel_id=1, source_target_pairs={{128,0},{0,128},{384,256},{256,384},{640,512},{512,640},{896,768},... | collective-permute-start | bytes 442376 | tf_op jit(solution)/shard_map/ppermute | solution.py:467
  160.6 8.5 %collective-permute-start.23 = (f32[4,72,128]{2,1,0:T(8,128)S(1)}, f32[4,72,128]{2,1,0:T(8,128)S(1)}, u32[]{:S(2)}, u32[]{:S(2)}) collective-permute-start(f32[4,72,128]{2,1,0:T(8,128)S(1)} %collective-permute-done.19.refs_3_), channel_id=1, source_target_pairs={{128,0},{0,128},{384,256},{256,384},{640,512},{512,640},{896,768},... | collective-permute-start | bytes 442376 | tf_op jit(solution)/shard_map/ppermute | solution.py:467
  166.4 8.6 %copy-start = (f32[8,8]{1,0:T(8,128)S(1)}, f32[8,8]{1,0:T(8,128)}, u32[]{:S(2)}) copy-start(f32[8,8]{1,0:T(8,128)} %rates_ref.3) | copy-start | bytes 772
  166.5 4.5 %collective-permute-start.24 = (f32[32,8,128]{2,1,0:T(8,128)S(1)}, f32[32,8,128]{2,1,0:T(8,128)S(1)}, u32[]{:S(2)}, u32[]{:S(2)}) collective-permute-start(f32[32,8,128]{2,1,0:T(8,128)S(1)} %get-tuple-element.56.east_ref), channel_id=1, source_target_pairs={{0,1},{1,2},{2,3},{3,4},{4,5},{5,6},{6,7},{8,9},{9,10},{10,11},{11... | collective-permute-start | bytes 393224 | tf_op jit(solution)/shard_map/ppermute | solution.py:479
  167.8 7.3 %collective-permute-start.25 = (f32[32,8,128]{2,1,0:T(8,128)S(1)}, f32[32,8,128]{2,1,0:T(8,128)S(1)}, u32[]{:S(2)}, u32[]{:S(2)}) collective-permute-start(f32[32,8,128]{2,1,0:T(8,128)S(1)} %get-tuple-element.57.west_ref), channel_id=1, source_target_pairs={{1,0},{2,1},{3,2},{4,3},{5,4},{6,5},{7,6},{9,8},{10,9},{11,10},{12... | collective-permute-start | bytes 393224 | tf_op jit(solution)/shard_map/ppermute | solution.py:479
  189.8 4.0 %collective-permute-start.26 = (f32[32,8,128]{2,1,0:T(8,128)S(1)}, f32[32,8,128]{2,1,0:T(8,128)S(1)}, u32[]{:S(2)}, u32[]{:S(2)}) collective-permute-start(f32[32,8,128]{2,1,0:T(8,128)S(1)} %get-tuple-element.59.east_ref), channel_id=1, source_target_pairs={{0,1},{1,2},{2,3},{3,4},{4,5},{5,6},{6,7},{8,9},{9,10},{10,11},{11... | collective-permute-start | bytes 393224 | tf_op jit(solution)/shard_map/ppermute | solution.py:479
  191.3 6.9 %collective-permute-start.27 = (f32[32,8,128]{2,1,0:T(8,128)S(1)}, f32[32,8,128]{2,1,0:T(8,128)S(1)}, u32[]{:S(2)}, u32[]{:S(2)}) collective-permute-start(f32[32,8,128]{2,1,0:T(8,128)S(1)} %get-tuple-element.60.west_ref), channel_id=1, source_target_pairs={{1,0},{2,1},{3,2},{4,3},{5,4},{6,5},{7,6},{9,8},{10,9},{11,10},{12... | collective-permute-start | bytes 393224 | tf_op jit(solution)/shard_map/ppermute | solution.py:479

commit v3 on v2

--- a/solution.py
+++ b/solution.py
@@ -15,7 +15,7 @@
 HALO = 6
 VMEM_LIMIT = 24 << 20
 UNROLL = 2
-PIECES = {"O": (0, 8), "A": (8, 8), "B": (16, 9), "C": (25, 7)}
+PIECES = {"O": (0, 8), "A": (8, 10), "B": (18, 8), "C": (26, 6)}
 
 
 def spot(row):
@@ -120,10 +120,11 @@
             far_ref[...] = lo_ref[first : first + count]
 
 
-def pack(values, rows):
+def pack(values, rows, east=None, west=None):
     lane = lax.broadcasted_iota(jnp.int32, (TR, LANES), 1)
     slot = lane // 8
-    east = west = jnp.zeros((TR, LANES), jnp.float32)
+    if east is None:
+        east = west = jnp.zeros((TR, LANES), jnp.float32)
     for value, row in zip(values, rows):
         place = 8 * (row + 3)
         here = slot == row + 3
@@ -132,8 +133,36 @@
     return east, west
 
 
+HALF = NZ // 2
+
+
+def merge(message_ref, k, value, from_low):
+    place = lax.broadcasted_iota(jnp.int32, (TR, LANES), 1) % 8
+    mine = (place < 4) == from_low
+    slot = k % HALF
+    moved = pltpu.roll(value, 4 if from_low else LANES - 4, 1)
+    message_ref[slot] = jnp.where(k >= HALF, moved, jnp.where(mine, value, message_ref[slot]))
+
+
+def received(message_ref, k, from_low):
+    value = message_ref[k % HALF]
+    return jnp.where(k >= HALF, pltpu.roll(value, LANES - 4 if from_low else 4, 1), value)
+
+
+def ends_kernel(hi_ref, lo_ref, east_ref, west_ref):
+    def level(k, carry):
+        values = [lo_ref[k, row] for row in range(HALO)]
+        values += [hi_ref[k, row] for row in range(2 * HALO - 8, HALO)]
+        east_ref[k], west_ref[k] = pack(values, range(8))
+        return carry
+
+    lax.fori_loop(0, NZ, level, 0)
+
+
 def join_kernel(x_ref, hi_ref, lo_ref, west_ref, east_ref, *refs):
-    pieces, (all_ref, pack_east_ref, pack_west_ref) = refs[:4], refs[4:]
+    pieces, (coef_ref, own_east_ref, own_west_ref, all_ref, *pack_refs) = refs[:4], refs[4:]
+    pack_east_ref, pack_west_ref, send_east_ref, send_west_ref = pack_refs
+    place = lax.broadcasted_iota(jnp.int32, (TR, LANES), 1) % 8
     for near_ref, owner, base in ((west_ref, 0, 0), (east_ref, XS - 1, HALO + 8)):
 
         @pl.when(x_ref[0] == owner)
@@ -147,11 +176,20 @@
 
     all_ref[:, HALO : 2 * HALO] = lo_ref[...]
     all_ref[:, 2 * HALO : 2 * HALO + 2] = hi_ref[:, HALO - 2 : HALO]
-    rows = list(range(-3, 11))
-
-    def level(k, carry):
-        packed = pack([all_ref[k, row + HALO] for row in rows], rows)
-        pack_east_ref[k], pack_west_ref[k] = packed
+    rows = [-3, -2, -1, 8, 9, 10]
+
+    def level(step, carry):
+        k = NZ - 1 - step
+        east, west = pack(
+            [all_ref[k, row + HALO] for row in rows], rows, own_east_ref[k], own_west_ref[k]
+        )
+        pack_east_ref[k], pack_west_ref[k] = east, west
+        last_face = jnp.broadcast_to(coef_ref[k, pl.ds(ENDS + 1, 1)], (TR, LANES))
+        first_wet = jnp.broadcast_to(coef_ref[k, pl.ds(ENDS, 1)], (TR, LANES))
+        last_face = pltpu.roll(last_face, LANES - 1, 1)
+        first_wet = pltpu.roll(first_wet, 2, 1)
+        merge(send_east_ref, k, jnp.where(place < 3, east, last_face), True)
+        merge(send_west_ref, k, jnp.where(place < 5, first_wet, west), False)
         return carry
 
     lax.fori_loop(0, NZ, level, 0)
@@ -178,7 +216,8 @@
     far_ref[...] = jnp.where(x_ref[0] == XS - 1, high_ref[...], low_ref[...])
 
 
-def blocks_kernel(x_ref, own_ref, west_ref, east_ref, far_ref, blocks_ref, north_ref, south_ref):
+def table_kernel(group_ref, x_ref, own_ref, west_ref, east_ref, far_ref, table_ref, blocks_ref,
+                 next_ref):
     items = own_ref.shape[0]
     levels = items // 4
     blocks_ref[:, 0:8] = own_ref[...]
@@ -187,16 +226,6 @@
         far = far_ref[item // 2, place]
         blocks_ref[item, 8:12] = jnp.where(x_ref[0] == 0, far, west_ref[item // 2, place])
         blocks_ref[item, 12:16] = jnp.where(x_ref[0] == XS - 1, far, east_ref[item // 2, place])
-    for index, item in enumerate([*range(levels, 2 * levels), items - 1]):
-        north_ref[index] = jnp.broadcast_to(
-            blocks_ref[item][:, LANES - 1 : LANES], (16, LANES)
-        )
-    south_ref[0] = jnp.broadcast_to(blocks_ref[items - 1][:, 0:1], (16, LANES))
-
-
-def table_kernel(group_ref, blocks_ref, south_ref, north_ref, table_ref, next_ref):
-    items = blocks_ref.shape[0]
-    levels = items // 4
     lane = lax.broadcasted_iota(jnp.int32, (16, LANES), 1)
     slot = lax.broadcasted_iota(jnp.int32, (8, LANES), 1) // 8
     depth = blocks_ref[items - 1]
@@ -204,10 +233,10 @@
         next_ref[target : target + count] = blocks_ref[items - 1, source : source + count]
     next_ref[15:16] = jnp.zeros((1, LANES), jnp.float32)
     depth_x = jnp.minimum(depth, next_ref[...])
-    depth_y = jnp.minimum(
-        depth, jnp.where(lane == LANES - 1, north_ref[0], pltpu.roll(depth, LANES - 1, 1))
-    )
-    depth_south = jnp.minimum(south_ref[levels], jnp.broadcast_to(depth[:, 0:1], (16, LANES)))
+    depth_y = jnp.where(
+        lane == LANES - 1, depth, jnp.minimum(depth, pltpu.roll(depth, LANES - 1, 1))
+    )
+    depth_first = jnp.broadcast_to(depth[:, 0:1], (16, LANES))
     table_ref[...] = jnp.zeros_like(table_ref)
     for index in range(levels):
         level = (group_ref[0] * levels + index).astype(jnp.float32)
@@ -217,8 +246,8 @@
         wet_below = level + 1.0 < depth
         table_ref[index, 32:48] = jnp.where(wet_below, blocks_ref[2 * levels + index], 0.0)
         table_ref[index, 48:64] = jnp.where(wet_below, blocks_ref[3 * levels + index], 0.0)
-        south = jnp.where(level < depth_south, south_ref[index], 0.0)
-        next_ref[...] = jnp.where(lane == LANES - 1, south, courant_y)
+        wet_first = jnp.where(level < depth_first, 1.0, 0.0)
+        next_ref[...] = jnp.where(lane == LANES - 1, wet_first, courant_y)
         low = high = jnp.zeros((8, LANES), jnp.float32)
         for row in range(-3, 11):
             at = 8 * (row + 3)
@@ -297,9 +326,9 @@
 def step_kernel(low_row, high_row, base, last, q_ref, coef_ref, east_ref, west_ref,
                 from_west_ref, from_east_ref, rates_ref, *refs):
     if last:
-        out_ref, forward_ref, flux_ref = refs
+        ends_ref, out_ref, forward_ref, flux_ref = refs
     else:
-        out_ref, pack_east_ref, pack_west_ref, forward_ref, flux_ref = refs
+        out_ref, pack_east_ref, pack_west_ref, *message_refs, ends_ref, forward_ref, flux_ref = refs
     rows = list(range(low_row, high_row))
     rates = spun(rates_ref)
     lane = lax.broadcasted_iota(jnp.int32, (TR, LANES), 1)
@@ -308,8 +337,15 @@
     def coef(k, at, row):
         return jnp.broadcast_to(coef_ref[k, pl.ds(at + spot(row), 1), :], (TR, LANES))
 
-    def strip(k, at, value):
-        courant = jnp.broadcast_to(coef_ref[k, pl.ds(ENDS + at, 1), :], (TR, LANES))
+    def end_faces(k, from_west, from_east):
+        low = jnp.broadcast_to(coef_ref[k, pl.ds(ENDS, 1), :], (TR, LANES))
+        high = jnp.broadcast_to(coef_ref[k, pl.ds(ENDS + 1, 1), :], (TR, LANES))
+        low = jnp.where(place == 2, low * pltpu.roll(from_west, LANES - 1, 1), low)
+        high = jnp.where(place == 4, high * from_east, high)
+        ends_ref[k, 0], ends_ref[k, 1] = low, high
+        return low, high
+
+    def strip(courant, value):
         size = jnp.abs(courant)
         return along_y(value, courant, 0.5 * size, 1.0 - size * (2.0 / 3.0))
 
@@ -318,8 +354,14 @@
 
     def down(k):
         below = jnp.minimum(k + 1, NZ - 1)
-        strip_w = strip(k, 0, jnp.where(place < 3, from_west_ref[k], east_ref[k]))
-        strip_e = strip(k, 1, jnp.where(place < 5, west_ref[k], from_east_ref[k]))
+        from_west = received(from_west_ref, k, True)
+        from_east = received(from_east_ref, k, False)
+        if last:
+            low, high = ends_ref[k, 0], ends_ref[k, 1]
+        else:
+            low, high = end_faces(k, from_west, from_east)
+        strip_w = strip(low, jnp.where(place < 3, from_west, east_ref[k]))
+        strip_e = strip(high, jnp.where(place < 5, west_ref[k], from_east))
         edges, flux_x = {}, {}
 
         def q(row):
@@ -377,7 +419,10 @@
                 if 0 <= row < 8:
                     own[row] = value
         if not last:
-            pack_east_ref[k], pack_west_ref[k] = pack(own.values(), own.keys())
+            east, west = pack(own.values(), own.keys())
+            pack_east_ref[k], pack_west_ref[k] = east, west
+            merge(message_refs[0], k, east, True)
+            merge(message_refs[1], k, west, False)
 
     @pl.loop(0, NZ // UNROLL)
     def _(part):
@@ -448,17 +493,12 @@
     rim_east = lax.ppermute(rim_low, "dx", outside)
     swapped = [(i, i + 1) for i in range(count - 1) if i % XS == XS - 1]
     rim_far = lax.ppermute(rim_far, "dx", swapped + [(b, a) for a, b in swapped])
-    blocks, to_north, to_south = call(
-        blocks_kernel,
-        [shape_of(items, 16, LANES), shape_of(levels + 1, 16, LANES), shape_of(1, 16, LANES)],
-        [x_index], [own, rim_west, rim_east, rim_far],
-    )
     north = [(i, i + 1) for i in range(groups - 1)]
     south = [(b, a) for a, b in north]
     (table,) = call(
-        table_kernel, [shape_of(levels, 72, LANES)], [group],
-        [blocks, lax.ppermute(to_north, "dy", north), lax.ppermute(to_south, "dy", south)],
-        [pltpu.VMEM((16, LANES), jnp.float32)],
+        table_kernel, [shape_of(levels, 72, LANES)], [group, x_index],
+        [own, rim_west, rim_east, rim_far],
+        [pltpu.VMEM((items, 16, LANES), jnp.float32), pltpu.VMEM((16, LANES), jnp.float32)],
     )
     members = lax.axis_size("group")
 
@@ -479,9 +519,11 @@
         return lax.ppermute(east, "dy", north), lax.ppermute(west, "dy", south)
 
     packs = [shape_of(NZ, TR, LANES)] * 2
-    joined, east, west = call(
-        join_kernel, [shape_of(NZ, 20, TR, LANES)] + packs, [x_index],
-        [hi, lo, from_west, from_east] + [far[name] for name in PIECES],
+    messages = [shape_of(HALF, TR, LANES)] * 2
+    own_ends = call(ends_kernel, packs, [], [hi, lo])
+    joined, east, west, *sent = call(
+        join_kernel, [shape_of(NZ, 20, TR, LANES)] + packs + messages, [x_index],
+        [hi, lo, from_west, from_east] + [far[name] for name in PIECES] + [coefs, *own_ends],
     )
 
     def scratch(rows):
@@ -490,15 +532,16 @@
             pltpu.VMEM((rows, TR, LANES), jnp.float32),
         ]
 
-    middle, east2, west2 = call(
+    middle, east2, west2, *sent2, ends = call(
         functools.partial(step_kernel, -3, 11, HALO, False),
-        [shape_of(NZ, 14, TR, LANES)] + packs, [],
-        [joined, coefs, east, west, *swap(east, west), reaction], scratch(14),
+        [shape_of(NZ, 14, TR, LANES)] + packs + messages + [shape_of(NZ, 2, TR, LANES)],
+        [],
+        [joined, coefs, east, west, *swap(*sent), reaction], scratch(14),
     )
     (out,) = call(
         functools.partial(step_kernel, 0, 8, 3, True),
         [jax.ShapeDtypeStruct((TR * NZ * 8, LANES), jnp.float32)], [],
-        [middle, coefs, east2, west2, *swap(east2, west2), reaction], scratch(8),
+        [middle, coefs, east2, west2, *swap(*sent2), reaction, ends], scratch(8),
     )
     return out.reshape(TR, NZ, 8, LANES)
 

time: 206 us -> 204 us (level)
  the two profiles are of different devices: /device:TPU:6 before, /device:TPU:352 now
where the time goes in v3:
time: 204 us; the launch traced here: 203 us
  starting transfers between devices  89.6 us (44%)
  waiting for transfers between devices  74.1 us (36%)
  Pallas kernels  37.1 us (18%)
    pallas_call x8, Pallas kernels, call(): pl.pallas_call(fetched(body, len(scalars), len(arguments)), out_shape=out...  37.1 us
    ppermute x7, starting transfers between devices, gather(): return lax.ppermute(value, 'group', pairs)  20.3 us
    ppermute x1, waiting for transfers between devices, transport(): far['A'] = lax.ppermute(far['A'], 'dx', collect_pairs([(2, 0)], [(1, 3)]))  20.1 us
    ppermute x1, starting transfers between devices, transport(): far['B'] = lax.ppermute(far['B'], 'dx', dx_pairs([(3, 0, 0)], [(0, 3, 0)]))  18.9 us
    ppermute x4, waiting for transfers between devices, swap(): return (lax.ppermute(east, 'dy', north), lax.ppermute(west, 'dy', south))  16.8 us
    ppermute x4, starting transfers between devices, swap(): return (lax.ppermute(east, 'dy', north), lax.ppermute(west, 'dy', south))  15.8 us
    ppermute x1, waiting for transfers between devices, transport(): lax.ppermute(rim_far, 'dx', swapped + [(b, a) for a, b in swapped])  12.8 us
    ppermute x1, waiting for transfers between devices, transport(): far['B'] = lax.ppermute(far['B'], 'dx', dx_pairs([(0, 0, 1)], [(3, 3, 1)]))  12.3 us
  transfers between devices with their start and end apart: 26, of which 8 were waited for; matrix products, arithmetic and copies ran while one was open for 1% of the time, Pallas kernels for 2%

profile of v3, /device:TPU:352, one launch (start us, length us, event | category | flops | bytes accessed | tf_op | source)
XLA Modules:
  0.0 202.7 jit_solution(6680380679775396719)
XLA Ops:
  0.0 3.0 %shard_map.73 = (f32[32,6,8,128]{3,2,1,0:T(8,128)S(1)}, f32[32,6,8,128]{3,2,1,0:T(8,128)S(1)}, f32[8,6,8,128]{3,2,1,0:T(8,128)S(1)}, f32[10,6,8,128]{3,2,1,0:T(8...) custom-call(s32[1]{0:T(128)} %bitcast.refs_0_.refs_1_.x_ref, f32[2048,128]{1,0:T(8,128)} %bitcast.4, ...), custom_call_target="tpu_custom_call" | custom-call | tf_op jit(solution)/shard_map/pallas_call | solution.py:63
  3.0 4.9 %collective-permute-start.9 = (f32[6,6,8,128]{3,2,1,0:T(8,128)S(1)}, f32[6,6,8,128]{3,2,1,0:T(8,128)S(1)}, u32[]{:S(2)}, u32[]{:S(2)}) collective-permute-start(f32[6,6,8,128]{3,2,1,0:T(8,128)S(1)} %get-tuple-element.46), channel_id=1, source_target_pairs={{24,8},{56,40},{32,48},{88,72},{64,80},{96,112},{25,9},{57,41},{33... | collective-permute-start | bytes 442376 | tf_op jit(solution)/shard_map/ppermute | solution.py:470
  8.0 0.7 broadcast_multiply_fusion
  8.7 0.8 tanh_multiply_fusion.refs_5_
  9.5 1.0 shard_map.74
  10.5 1.3 collective-permute-start.12
  11.8 1.3 collective-permute-start.13
  13.1 2.7 %collective-permute-start.14 = (f32[9,8,128]{2,1,0:T(8,128)S(1)}, f32[9,8,128]{2,1,0:T(8,128)S(1)}, u32[]{:S(2)}, u32[]{:S(2)}) collective-permute-start(f32[9,8,128]{2,1,0:T(8,128)S(1)} %get-tuple-element.55), channel_id=1, source_target_pairs={{24,32},{56,64},{88,96},{32,24},{64,56},{96,88},{25,33},{57,65},{8... | collective-permute-start | bytes 110600 | tf_op jit(solution)/shard_map/ppermute | solution.py:495
  15.8 1.9 collective-permute-done.13.east_ref
  17.7 12.8 %collective-permute-done.14.far_ref = f32[9,8,128]{2,1,0:T(8,128)S(1)} collective-permute-done((f32[9,8,128]{2,1,0:T(8,128)S(1)}, f32[9,8,128]{2,1,0:T(8,128)S(1)}, u32[]{:S(2)}, u32[]{:S(2)}) %collective-permute-start.14) | collective-permute-done | bytes 36896 | tf_op jit(solution)/shard_map/ppermute | solution.py:495
  30.4 0.3 shard_map.75.refs_0_
  30.7 1.9 collective-permute-start.18
  32.6 5.1 %collective-permute-start.17 = (f32[4,72,128]{2,1,0:T(8,128)S(1)}, f32[4,72,128]{2,1,0:T(8,128)S(1)}, u32[]{:S(2)}, u32[]{:S(2)}) collective-permute-start(f32[4,72,128]{2,1,0:T(8,128)S(1)} %shard_map.75.refs_0_), channel_id=1, source_target_pairs={{512,0},{640,128},{768,256},{896,384},{0,512},{128,640},{256,768},... | collective-permute-start | bytes 442376 | tf_op jit(solution)/shard_map/ppermute | solution.py:507
  37.7 2.6 %collective-permute-start.16 = (f32[4,72,128]{2,1,0:T(8,128)S(1)}, f32[4,72,128]{2,1,0:T(8,128)S(1)}, u32[]{:S(2)}, u32[]{:S(2)}) collective-permute-start(f32[4,72,128]{2,1,0:T(8,128)S(1)} %shard_map.75.refs_0_), channel_id=1, source_target_pairs={{768,0},{896,128},{0,256},{128,384},{256,512},{384,640},{512,768},... | collective-permute-start | bytes 442376 | tf_op jit(solution)/shard_map/ppermute | solution.py:507
  40.3 4.5 %collective-permute-start.15 = (f32[4,72,128]{2,1,0:T(8,128)S(1)}, f32[4,72,128]{2,1,0:T(8,128)S(1)}, u32[]{:S(2)}, u32[]{:S(2)}) collective-permute-start(f32[4,72,128]{2,1,0:T(8,128)S(1)} %shard_map.75.refs_0_), channel_id=1, source_target_pairs={{256,0},{384,128},{512,256},{640,384},{768,512},{896,640},{0,768},... | collective-permute-start | bytes 442376 | tf_op jit(solution)/shard_map/ppermute | solution.py:507
  44.8 0.0 collective-permute-done.9
  44.8 1.9 collective-permute-start.2
  46.8 1.3 collective-permute-start
  48.1 0.0 collective-permute-done.17.refs_3_
  48.1 1.3 collective-permute-start.1
  49.4 4.6 %collective-permute-start.4 = (f32[10,6,8,128]{3,2,1,0:T(8,128)S(1)}, f32[10,6,8,128]{3,2,1,0:T(8,128)S(1)}, u32[]{:S(2)}, u32[]{:S(2)}) collective-permute-start(f32[10,6,8,128]{3,2,1,0:T(8,128)S(1)} %get-tuple-element.44), channel_id=1, source_target_pairs={{24,16},{56,48},{32,40},{88,80},{64,72},{96,104},{25,17},{57,49},{... | collective-permute-start | bytes 737288 | tf_op jit(solution)/shard_map/ppermute | solution.py:468
  54.0 0.0 collective-permute-done.15.refs_1_
  54.0 18.9 %collective-permute-start.7 = (f32[8,6,8,128]{3,2,1,0:T(8,128)S(1)}, f32[8,6,8,128]{3,2,1,0:T(8,128)S(1)}, u32[]{:S(2)}, u32[]{:S(2)}) collective-permute-start(f32[8,6,8,128]{3,2,1,0:T(8,128)S(1)} %get-tuple-element.45), channel_id=1, source_target_pairs={{24,0},{56,32},{32,56},{88,64},{64,88},{96,120},{25,1},{57,33},{33... | collective-permute-start | bytes 589832 | tf_op jit(solution)/shard_map/ppermute | solution.py:469
  72.9 10.1 %collective-permute-done.2 = f32[8,6,8,128]{3,2,1,0:T(8,128)S(1)} collective-permute-done((f32[8,6,8,128]{3,2,1,0:T(8,128)S(1)}, f32[8,6,8,128]{3,2,1,0:T(8,128)S(1)}, u32[]{:S(2)}, u32[]{:S(2)}) %collective-permute-start.2) | collective-permute-done | bytes 196640 | tf_op jit(solution)/shard_map/ppermute | solution.py:471
  83.0 0.7 collective-permute-start.10
  83.7 0.0 collective-permute-done.7
  83.7 1.9 collective-permute-start.21
  85.7 2.4 %collective-permute-start.20 = (f32[4,72,128]{2,1,0:T(8,128)S(1)}, f32[4,72,128]{2,1,0:T(8,128)S(1)}, u32[]{:S(2)}, u32[]{:S(2)}) collective-permute-start(f32[4,72,128]{2,1,0:T(8,128)S(1)} %collective-permute-done.16.refs_2_), channel_id=1, source_target_pairs={{128,0},{0,128},{384,256},{256,384},{640,512},{512,640},{896,768},... | collective-permute-start | bytes 442376 | tf_op jit(solution)/shard_map/ppermute | solution.py:507
  88.1 0.7 collective-permute-start.5
  88.8 1.9 collective-permute-start.19
  90.7 6.6 %collective-permute-start.3 = (f32[8,6,8,128]{3,2,1,0:T(8,128)S(1)}, f32[8,6,8,128]{3,2,1,0:T(8,128)S(1)}, u32[]{:S(2)}, u32[]{:S(2)}) collective-permute-start(f32[8,6,8,128]{3,2,1,0:T(8,128)S(1)} %collective-permute-done.2), channel_id=1, source_target_pairs={{0,24},{56,32},{32,56},{88,64},{64,88},{120,96},{1,25},{57,33},{33... | collective-permute-start | bytes 589832 | tf_op jit(solution)/shard_map/ppermute | solution.py:479
  97.3 1.3 collective-permute-start.6
  98.6 4.8 %collective-permute-start.8 = (f32[8,6,8,128]{3,2,1,0:T(8,128)S(1)}, f32[8,6,8,128]{3,2,1,0:T(8,128)S(1)}, u32[]{:S(2)}, u32[]{:S(2)}) collective-permute-start(f32[8,6,8,128]{3,2,1,0:T(8,128)S(1)} %collective-permute-done.7), channel_id=1, source_target_pairs={{0,32},{32,64},{56,24},{64,96},{88,56},{120,88},{1,33},{33,65},{57... | collective-permute-start | bytes 589832 | tf_op jit(solution)/shard_map/ppermute | solution.py:473
  103.4 1.3 collective-permute-start.11
  104.7 2.7 %shard_map.77 = (f32[32,8,128]{2,1,0:T(8,128)S(1)}, f32[32,8,128]{2,1,0:T(8,128)S(1)}) custom-call(f32[32,6,8,128]{3,2,1,0:T(8,128)S(1)} %get-tuple-element.37.hi_ref, f32[32,6,8,128]{3,2,1,0:T(8,128)S(1)} %get-tuple-element.38.lo_ref), custom_call_target="tpu_custom_call" | custom-call | tf_op jit(solution)/shard_map/pallas_call | solution.py:63
  107.4 0.7 shard_map.76.refs_4_.coef_ref
  108.2 12.3 %collective-permute-done.8.refs_2_ = f32[8,6,8,128]{3,2,1,0:T(8,128)S(1)} collective-permute-done((f32[8,6,8,128]{3,2,1,0:T(8,128)S(1)}, f32[8,6,8,128]{3,2,1,0:T(8,128)S(1)}, u32[]{:S(2)}, u32[]{:S(2)}) %collective-permute-start.8) | collective-permute-done | bytes 196640 | tf_op jit(solution)/shard_map/ppermute | solution.py:473
  120.5 20.1 %collective-permute-done.6.refs_1_ = f32[10,6,8,128]{3,2,1,0:T(8,128)S(1)} collective-permute-done((f32[10,6,8,128]{3,2,1,0:T(8,128)S(1)}, f32[10,6,8,128]{3,2,1,0:T(8,128)S(1)}, u32[]{:S(2)}, u32[]{:S(2)}) %collective-permute-start.6) | collective-permute-done | bytes 245792 | tf_op jit(solution)/shard_map/ppermute | solution.py:480
  140.6 5.1 %shard_map.78 = (f32[32,20,8,128]{3,2,1,0:T(8,128)S(1)}, f32[32,8,128]{2,1,0:T(8,128)S(1)}, f32[32,8,128]{2,1,0:T(8,128)S(1)}, f32[16,8,128]{2,1,0:T(8,128)S(1)}, f32[16,8,128]{2,1,0:T(8,128)S(1)}) custom-call(s32[1]{0:T(128)} %bitcast.refs_0_.refs_1_.x_ref, f32[32,6,8,128]{3,2,1,0:T(8,128)S(1)} %get-tuple-element.37.hi_ref, ...), custom_call_target="tpu_custom_call" | custom-call | tf_op jit(solution)/shard_map/pallas_call | solution.py:63
  145.7 1.9 collective-permute-start.22
  147.6 3.9 %collective-permute-start.23 = (f32[16,8,128]{2,1,0:T(8,128)S(1)}, f32[16,8,128]{2,1,0:T(8,128)S(1)}, u32[]{:S(2)}, u32[]{:S(2)}) collective-permute-start(f32[16,8,128]{2,1,0:T(8,128)S(1)} %get-tuple-element.62), channel_id=1, source_target_pairs={{1,0},{2,1},{3,2},{4,3},{5,4},{6,5},{7,6},{9,8},{10,9},{11,10},{12... | collective-permute-start | bytes 196616 | tf_op jit(solution)/shard_map/ppermute | solution.py:519
  151.5 0.3 collective-permute-done.22.from_west_ref
  151.8 8.1 %collective-permute-done.23.from_east_ref = f32[16,8,128]{2,1,0:T(8,128)S(1)} collective-permute-done((f32[16,8,128]{2,1,0:T(8,128)S(1)}, f32[16,8,128]{2,1,0:T(8,128)S(1)}, u32[]{:S(2)}, u32[]{:S(2)}) %collective-permute-start.23) | collective-permute-done | bytes 65568 | tf_op jit(solution)/shard_map/ppermute | solution.py:519
  160.0 15.8 %shard_map.79 = (f32[32,14,8,128]{3,2,1,0:T(8,128)S(1)}, f32[32,8,128]{2,1,0:T(8,128)S(1)}, f32[32,8,128]{2,1,0:T(8,128)S(1)}, f32[16,8,128]{2,1,0:T(8,128)S(1)}...) custom-call(f32[32,20,8,128]{3,2,1,0:T(8,128)S(1)} %get-tuple-element.58.q_ref, ...), custom_call_target="tpu_custom_call" | custom-call | tf_op jit(solution)/shard_map/pallas_call | solution.py:63
  175.8 8.1 %collective-permute-start.24 = (f32[16,8,128]{2,1,0:T(8,128)S(1)}, f32[16,8,128]{2,1,0:T(8,128)S(1)}, u32[]{:S(2)}, u32[]{:S(2)}) collective-permute-start(f32[16,8,128]{2,1,0:T(8,128)S(1)} %get-tuple-element.66), channel_id=1, source_target_pairs={{0,1},{1,2},{2,3},{3,4},{4,5},{5,6},{6,7},{8,9},{9,10},{10,11},{11... | collective-permute-start | bytes 196616 | tf_op jit(solution)/shard_map/ppermute | solution.py:519
  183.9 1.9 collective-permute-start.25
  185.8 8.4 %collective-permute-done.25.from_east_ref = f32[16,8,128]{2,1,0:T(8,128)S(1)} collective-permute-done((f32[16,8,128]{2,1,0:T(8,128)S(1)}, f32[16,8,128]{2,1,0:T(8,128)S(1)}, u32[]{:S(2)}, u32[]{:S(2)}) %collective-permute-start.25) | collective-permute-done | bytes 65568 | tf_op jit(solution)/shard_map/ppermute | solution.py:519
  194.2 8.5 %shard_map.80 = f32[2048,128]{1,0:T(8,128)} custom-call(f32[32,14,8,128]{3,2,1,0:T(8,128)S(1)} %get-tuple-element.63.q_ref, f32[32,168,128]{2,1,0:T(8,128)S(1)} %shard_map.76.refs_4_.coef_ref, f32[32,8,128]{2,1,0:T(8,128)S(1)} %get-tuple-element.64.east_ref, f32[32,8,128]{2,1,0:T(8,128)S(1)} %get-tuple-element.65.west_ref, ...), custom_call_target="tpu_custom_call" | custom-call | tf_op jit(solution)/shard_map/pallas_call | solution.py:63
  (16 shorter events, 0.0 us)
Async XLA Ops:
  3.0 41.8 %collective-permute-start.9 = (f32[6,6,8,128]{3,2,1,0:T(8,128)S(1)}, f32[6,6,8,128]{3,2,1,0:T(8,128)S(1)}, u32[]{:S(2)}, u32[]{:S(2)}) collective-permute-start(f32[6,6,8,128]{3,2,1,0:T(8,128)S(1)} %get-tuple-element.46), channel_id=1, source_target_pairs={{24,8},{56,40},{32,48},{88,72},{64,80},{96,112},{25,9},{57,41},{33... | collective-permute-start | bytes 442376 | tf_op jit(solution)/shard_map/ppermute | solution.py:470
  10.5 5.3 %collective-permute-start.12 = (f32[9,8,128]{2,1,0:T(8,128)S(1)}, f32[9,8,128]{2,1,0:T(8,128)S(1)}, u32[]{:S(2)}, u32[]{:S(2)}) collective-permute-start(f32[9,8,128]{2,1,0:T(8,128)S(1)} %get-tuple-element.53), channel_id=1, source_target_pairs={{0,8},{8,16},{16,24},{32,40},{40,48},{48,56},{64,72},{72,80},{80,8... | collective-permute-start | bytes 110600 | tf_op jit(solution)/shard_map/ppermute | solution.py:492
  11.8 5.9 %collective-permute-start.13 = (f32[9,8,128]{2,1,0:T(8,128)S(1)}, f32[9,8,128]{2,1,0:T(8,128)S(1)}, u32[]{:S(2)}, u32[]{:S(2)}) collective-permute-start(f32[9,8,128]{2,1,0:T(8,128)S(1)} %get-tuple-element.54), channel_id=1, source_target_pairs={{8,0},{16,8},{24,16},{40,32},{48,40},{56,48},{72,64},{80,72},{88,8... | collective-permute-start | bytes 110600 | tf_op jit(solution)/shard_map/ppermute | solution.py:493
  13.1 17.3 %collective-permute-start.14 = (f32[9,8,128]{2,1,0:T(8,128)S(1)}, f32[9,8,128]{2,1,0:T(8,128)S(1)}, u32[]{:S(2)}, u32[]{:S(2)}) collective-permute-start(f32[9,8,128]{2,1,0:T(8,128)S(1)} %get-tuple-element.55), channel_id=1, source_target_pairs={{24,32},{56,64},{88,96},{32,24},{64,56},{96,88},{25,33},{57,65},{8... | collective-permute-start | bytes 110600 | tf_op jit(solution)/shard_map/ppermute | solution.py:495
  30.7 16.0 %collective-permute-start.18 = (f32[4,72,128]{2,1,0:T(8,128)S(1)}, f32[4,72,128]{2,1,0:T(8,128)S(1)}, u32[]{:S(2)}, u32[]{:S(2)}) collective-permute-start(f32[4,72,128]{2,1,0:T(8,128)S(1)} %shard_map.75.refs_0_), channel_id=1, source_target_pairs={{128,0},{0,128},{384,256},{256,384},{640,512},{512,640},{896,768},... | collective-permute-start | bytes 442376 | tf_op jit(solution)/shard_map/ppermute | solution.py:507
  32.6 15.5 %collective-permute-start.17 = (f32[4,72,128]{2,1,0:T(8,128)S(1)}, f32[4,72,128]{2,1,0:T(8,128)S(1)}, u32[]{:S(2)}, u32[]{:S(2)}) collective-permute-start(f32[4,72,128]{2,1,0:T(8,128)S(1)} %shard_map.75.refs_0_), channel_id=1, source_target_pairs={{512,0},{640,128},{768,256},{896,384},{0,512},{128,640},{256,768},... | collective-permute-start | bytes 442376 | tf_op jit(solution)/shard_map/ppermute | solution.py:507
  37.7 11.7 %collective-permute-start.16 = (f32[4,72,128]{2,1,0:T(8,128)S(1)}, f32[4,72,128]{2,1,0:T(8,128)S(1)}, u32[]{:S(2)}, u32[]{:S(2)}) collective-permute-start(f32[4,72,128]{2,1,0:T(8,128)S(1)} %shard_map.75.refs_0_), channel_id=1, source_target_pairs={{768,0},{896,128},{0,256},{128,384},{256,512},{384,640},{512,768},... | collective-permute-start | bytes 442376 | tf_op jit(solution)/shard_map/ppermute | solution.py:507
  40.3 13.7 %collective-permute-start.15 = (f32[4,72,128]{2,1,0:T(8,128)S(1)}, f32[4,72,128]{2,1,0:T(8,128)S(1)}, u32[]{:S(2)}, u32[]{:S(2)}) collective-permute-start(f32[4,72,128]{2,1,0:T(8,128)S(1)} %shard_map.75.refs_0_), channel_id=1, source_target_pairs={{256,0},{384,128},{512,256},{640,384},{768,512},{896,640},{0,768},... | collective-permute-start | bytes 442376 | tf_op jit(solution)/shard_map/ppermute | solution.py:507
  44.8 38.2 %collective-permute-start.2 = (f32[8,6,8,128]{3,2,1,0:T(8,128)S(1)}, f32[8,6,8,128]{3,2,1,0:T(8,128)S(1)}, u32[]{:S(2)}, u32[]{:S(2)}) collective-permute-start(f32[8,6,8,128]{3,2,1,0:T(8,128)S(1)} %get-tuple-element.43), channel_id=1, source_target_pairs={{24,56},{56,88},{32,0},{88,120},{64,32},{96,64},{25,57},{57,89},{3... | collective-permute-start | bytes 589832 | tf_op jit(solution)/shard_map/ppermute | solution.py:471
  46.8 93.8 %collective-permute-start = (f32[32,6,8,128]{3,2,1,0:T(8,128)S(1)}, f32[32,6,8,128]{3,2,1,0:T(8,128)S(1)}, u32[]{:S(2)}, u32[]{:S(2)}) collective-permute-start(f32[32,6,8,128]{3,2,1,0:T(8,128)S(1)} %get-tuple-element.37.hi_ref), channel_id=1, source_target_pairs={{0,8},{8,16},{16,24},{32,40},{40,48},{48,56},{64,72},{72,80},{80,8... | collective-permute-start | bytes 2359304 | tf_op jit(solution)/shard_map/ppermute | solution.py:477
  48.1 92.5 %collective-permute-start.1 = (f32[32,6,8,128]{3,2,1,0:T(8,128)S(1)}, f32[32,6,8,128]{3,2,1,0:T(8,128)S(1)}, u32[]{:S(2)}, u32[]{:S(2)}) collective-permute-start(f32[32,6,8,128]{3,2,1,0:T(8,128)S(1)} %get-tuple-element.38.lo_ref), channel_id=1, source_target_pairs={{8,0},{16,8},{24,16},{40,32},{48,40},{56,48},{72,64},{80,72},{88,8... | collective-permute-start | bytes 2359304 | tf_op jit(solution)/shard_map/ppermute | solution.py:478
  49.4 36.2 %collective-permute-start.4 = (f32[10,6,8,128]{3,2,1,0:T(8,128)S(1)}, f32[10,6,8,128]{3,2,1,0:T(8,128)S(1)}, u32[]{:S(2)}, u32[]{:S(2)}) collective-permute-start(f32[10,6,8,128]{3,2,1,0:T(8,128)S(1)} %get-tuple-element.44), channel_id=1, source_target_pairs={{24,16},{56,48},{32,40},{88,80},{64,72},{96,104},{25,17},{57,49},{... | collective-permute-start | bytes 737288 | tf_op jit(solution)/shard_map/ppermute | solution.py:468
  54.0 29.7 %collective-permute-start.7 = (f32[8,6,8,128]{3,2,1,0:T(8,128)S(1)}, f32[8,6,8,128]{3,2,1,0:T(8,128)S(1)}, u32[]{:S(2)}, u32[]{:S(2)}) collective-permute-start(f32[8,6,8,128]{3,2,1,0:T(8,128)S(1)} %get-tuple-element.45), channel_id=1, source_target_pairs={{24,0},{56,32},{32,56},{88,64},{64,88},{96,120},{25,1},{57,33},{33... | collective-permute-start | bytes 589832 | tf_op jit(solution)/shard_map/ppermute | solution.py:469
  83.0 5.0 %collective-permute-start.10 = (f32[6,6,8,128]{3,2,1,0:T(8,128)S(1)}, f32[6,6,8,128]{3,2,1,0:T(8,128)S(1)}, u32[]{:S(2)}, u32[]{:S(2)}) collective-permute-start(f32[6,6,8,128]{3,2,1,0:T(8,128)S(1)} %collective-permute-done.9), channel_id=1, source_target_pairs={{8,40},{40,72},{48,16},{72,104},{80,48},{112,80},{9,41},{41,73},{4... | collective-permute-start | bytes 442376 | tf_op jit(solution)/shard_map/ppermute | solution.py:474
  83.7 5.1 %collective-permute-start.21 = (f32[4,72,128]{2,1,0:T(8,128)S(1)}, f32[4,72,128]{2,1,0:T(8,128)S(1)}, u32[]{:S(2)}, u32[]{:S(2)}) collective-permute-start(f32[4,72,128]{2,1,0:T(8,128)S(1)} %collective-permute-done.17.refs_3_), channel_id=1, source_target_pairs={{128,0},{0,128},{384,256},{256,384},{640,512},{512,640},{896,768},... | collective-permute-start | bytes 442376 | tf_op jit(solution)/shard_map/ppermute | solution.py:507
  85.7 5.1 %collective-permute-start.20 = (f32[4,72,128]{2,1,0:T(8,128)S(1)}, f32[4,72,128]{2,1,0:T(8,128)S(1)}, u32[]{:S(2)}, u32[]{:S(2)}) collective-permute-start(f32[4,72,128]{2,1,0:T(8,128)S(1)} %collective-permute-done.16.refs_2_), channel_id=1, source_target_pairs={{128,0},{0,128},{384,256},{256,384},{640,512},{512,640},{896,768},... | collective-permute-start | bytes 442376 | tf_op jit(solution)/shard_map/ppermute | solution.py:507
  88.1 9.2 %collective-permute-start.5 = (f32[10,6,8,128]{3,2,1,0:T(8,128)S(1)}, f32[10,6,8,128]{3,2,1,0:T(8,128)S(1)}, u32[]{:S(2)}, u32[]{:S(2)}) collective-permute-start(f32[10,6,8,128]{3,2,1,0:T(8,128)S(1)} %collective-permute-done.4), channel_id=1, source_target_pairs={{16,48},{48,80},{40,8},{80,112},{72,40},{104,72},{17,49},{49,81},{... | collective-permute-start | bytes 737288 | tf_op jit(solution)/shard_map/ppermute | solution.py:472
  88.8 9.8 %collective-permute-start.19 = (f32[4,72,128]{2,1,0:T(8,128)S(1)}, f32[4,72,128]{2,1,0:T(8,128)S(1)}, u32[]{:S(2)}, u32[]{:S(2)}) collective-permute-start(f32[4,72,128]{2,1,0:T(8,128)S(1)} %collective-permute-done.15.refs_1_), channel_id=1, source_target_pairs={{128,0},{0,128},{384,256},{256,384},{640,512},{512,640},{896,768},... | collective-permute-start | bytes 442376 | tf_op jit(solution)/shard_map/ppermute | solution.py:507
  90.7 12.7 %collective-permute-start.3 = (f32[8,6,8,128]{3,2,1,0:T(8,128)S(1)}, f32[8,6,8,128]{3,2,1,0:T(8,128)S(1)}, u32[]{:S(2)}, u32[]{:S(2)}) collective-permute-start(f32[8,6,8,128]{3,2,1,0:T(8,128)S(1)} %collective-permute-done.2), channel_id=1, source_target_pairs={{0,24},{56,32},{32,56},{88,64},{64,88},{120,96},{1,25},{57,33},{33... | collective-permute-start | bytes 589832 | tf_op jit(solution)/shard_map/ppermute | solution.py:479
  97.3 43.3 %collective-permute-start.6 = (f32[10,6,8,128]{3,2,1,0:T(8,128)S(1)}, f32[10,6,8,128]{3,2,1,0:T(8,128)S(1)}, u32[]{:S(2)}, u32[]{:S(2)}) collective-permute-start(f32[10,6,8,128]{3,2,1,0:T(8,128)S(1)} %collective-permute-done.5), channel_id=1, source_target_pairs={{8,24},{48,32},{40,56},{80,64},{72,88},{112,96},{9,25},{49,33},{41... | collective-permute-start | bytes 737288 | tf_op jit(solution)/shard_map/ppermute | solution.py:480
  98.6 21.8 %collective-permute-start.8 = (f32[8,6,8,128]{3,2,1,0:T(8,128)S(1)}, f32[8,6,8,128]{3,2,1,0:T(8,128)S(1)}, u32[]{:S(2)}, u32[]{:S(2)}) collective-permute-start(f32[8,6,8,128]{3,2,1,0:T(8,128)S(1)} %collective-permute-done.7), channel_id=1, source_target_pairs={{0,32},{32,64},{56,24},{64,96},{88,56},{120,88},{1,33},{33,65},{57... | collective-permute-start | bytes 589832 | tf_op jit(solution)/shard_map/ppermute | solution.py:473
  103.4 17.1 %collective-permute-start.11 = (f32[6,6,8,128]{3,2,1,0:T(8,128)S(1)}, f32[6,6,8,128]{3,2,1,0:T(8,128)S(1)}, u32[]{:S(2)}, u32[]{:S(2)}) collective-permute-start(f32[6,6,8,128]{3,2,1,0:T(8,128)S(1)} %collective-permute-done.10), channel_id=1, source_target_pairs={{16,24},{40,32},{48,56},{72,64},{80,88},{104,96},{17,25},{41,33},{... | collective-permute-start | bytes 442376 | tf_op jit(solution)/shard_map/ppermute | solution.py:481
  140.6 19.4 %copy-start = (f32[8,8]{1,0:T(8,128)S(1)}, f32[8,8]{1,0:T(8,128)}, u32[]{:S(2)}) copy-start(f32[8,8]{1,0:T(8,128)} %rates_ref.3) | copy-start | bytes 772
  145.7 6.2 %collective-permute-start.22 = (f32[16,8,128]{2,1,0:T(8,128)S(1)}, f32[16,8,128]{2,1,0:T(8,128)S(1)}, u32[]{:S(2)}, u32[]{:S(2)}) collective-permute-start(f32[16,8,128]{2,1,0:T(8,128)S(1)} %get-tuple-element.61), channel_id=1, source_target_pairs={{0,1},{1,2},{2,3},{3,4},{4,5},{5,6},{6,7},{8,9},{9,10},{10,11},{11... | collective-permute-start | bytes 196616 | tf_op jit(solution)/shard_map/ppermute | solution.py:519
  147.6 12.4 %collective-permute-start.23 = (f32[16,8,128]{2,1,0:T(8,128)S(1)}, f32[16,8,128]{2,1,0:T(8,128)S(1)}, u32[]{:S(2)}, u32[]{:S(2)}) collective-permute-start(f32[16,8,128]{2,1,0:T(8,128)S(1)} %get-tuple-element.62), channel_id=1, source_target_pairs={{1,0},{2,1},{3,2},{4,3},{5,4},{6,5},{7,6},{9,8},{10,9},{11,10},{12... | collective-permute-start | bytes 196616 | tf_op jit(solution)/shard_map/ppermute | solution.py:519
  175.8 10.0 %collective-permute-start.24 = (f32[16,8,128]{2,1,0:T(8,128)S(1)}, f32[16,8,128]{2,1,0:T(8,128)S(1)}, u32[]{:S(2)}, u32[]{:S(2)}) collective-permute-start(f32[16,8,128]{2,1,0:T(8,128)S(1)} %get-tuple-element.66), channel_id=1, source_target_pairs={{0,1},{1,2},{2,3},{3,4},{4,5},{5,6},{6,7},{8,9},{9,10},{10,11},{11... | collective-permute-start | bytes 196616 | tf_op jit(solution)/shard_map/ppermute | solution.py:519
  183.9 10.3 %collective-permute-start.25 = (f32[16,8,128]{2,1,0:T(8,128)S(1)}, f32[16,8,128]{2,1,0:T(8,128)S(1)}, u32[]{:S(2)}, u32[]{:S(2)}) collective-permute-start(f32[16,8,128]{2,1,0:T(8,128)S(1)} %get-tuple-element.67), channel_id=1, source_target_pairs={{1,0},{2,1},{3,2},{4,3},{5,4},{6,5},{7,6},{9,8},{10,9},{11,10},{12... | collective-permute-start | bytes 196616 | tf_op jit(solution)/shard_map/ppermute | solution.py:519

commit v4 on v3

--- a/solution.py
+++ b/solution.py
@@ -15,7 +15,7 @@
 HALO = 6
 VMEM_LIMIT = 24 << 20
 UNROLL = 2
-PIECES = {"O": (0, 8), "A": (8, 10), "B": (18, 8), "C": (26, 6)}
+PIECES = {"O": (0, 5), "A": (5, 12), "B": (17, 8), "C": (25, 7)}
 
 
 def spot(row):
@@ -133,22 +133,6 @@
     return east, west
 
 
-HALF = NZ // 2
-
-
-def merge(message_ref, k, value, from_low):
-    place = lax.broadcasted_iota(jnp.int32, (TR, LANES), 1) % 8
-    mine = (place < 4) == from_low
-    slot = k % HALF
-    moved = pltpu.roll(value, 4 if from_low else LANES - 4, 1)
-    message_ref[slot] = jnp.where(k >= HALF, moved, jnp.where(mine, value, message_ref[slot]))
-
-
-def received(message_ref, k, from_low):
-    value = message_ref[k % HALF]
-    return jnp.where(k >= HALF, pltpu.roll(value, LANES - 4 if from_low else 4, 1), value)
-
-
 def ends_kernel(hi_ref, lo_ref, east_ref, west_ref):
     def level(k, carry):
         values = [lo_ref[k, row] for row in range(HALO)]
@@ -178,8 +162,7 @@
     all_ref[:, 2 * HALO : 2 * HALO + 2] = hi_ref[:, HALO - 2 : HALO]
     rows = [-3, -2, -1, 8, 9, 10]
 
-    def level(step, carry):
-        k = NZ - 1 - step
+    def level(k, carry):
         east, west = pack(
             [all_ref[k, row + HALO] for row in rows], rows, own_east_ref[k], own_west_ref[k]
         )
@@ -188,8 +171,8 @@
         first_wet = jnp.broadcast_to(coef_ref[k, pl.ds(ENDS, 1)], (TR, LANES))
         last_face = pltpu.roll(last_face, LANES - 1, 1)
         first_wet = pltpu.roll(first_wet, 2, 1)
-        merge(send_east_ref, k, jnp.where(place < 3, east, last_face), True)
-        merge(send_west_ref, k, jnp.where(place < 5, first_wet, west), False)
+        send_east_ref[k] = jnp.where(place < 3, east, last_face)
+        send_west_ref[k] = jnp.where(place < 5, first_wet, west)
         return carry
 
     lax.fori_loop(0, NZ, level, 0)
@@ -328,7 +311,7 @@
     if last:
         ends_ref, out_ref, forward_ref, flux_ref = refs
     else:
-        out_ref, pack_east_ref, pack_west_ref, *message_refs, ends_ref, forward_ref, flux_ref = refs
+        out_ref, pack_east_ref, pack_west_ref, ends_ref, forward_ref, flux_ref = refs
     rows = list(range(low_row, high_row))
     rates = spun(rates_ref)
     lane = lax.broadcasted_iota(jnp.int32, (TR, LANES), 1)
@@ -354,8 +337,7 @@
 
     def down(k):
         below = jnp.minimum(k + 1, NZ - 1)
-        from_west = received(from_west_ref, k, True)
-        from_east = received(from_east_ref, k, False)
+        from_west, from_east = from_west_ref[k], from_east_ref[k]
         if last:
             low, high = ends_ref[k, 0], ends_ref[k, 1]
         else:
@@ -419,10 +401,7 @@
                 if 0 <= row < 8:
                     own[row] = value
         if not last:
-            east, west = pack(own.values(), own.keys())
-            pack_east_ref[k], pack_west_ref[k] = east, west
-            merge(message_refs[0], k, east, True)
-            merge(message_refs[1], k, west, False)
+            pack_east_ref[k], pack_west_ref[k] = pack(own.values(), own.keys())
 
     @pl.loop(0, NZ // UNROLL)
     def _(part):
@@ -519,10 +498,9 @@
         return lax.ppermute(east, "dy", north), lax.ppermute(west, "dy", south)
 
     packs = [shape_of(NZ, TR, LANES)] * 2
-    messages = [shape_of(HALF, TR, LANES)] * 2
     own_ends = call(ends_kernel, packs, [], [hi, lo])
     joined, east, west, *sent = call(
-        join_kernel, [shape_of(NZ, 20, TR, LANES)] + packs + messages, [x_index],
+        join_kernel, [shape_of(NZ, 20, TR, LANES)] + packs * 2, [x_index],
         [hi, lo, from_west, from_east] + [far[name] for name in PIECES] + [coefs, *own_ends],
     )
 
@@ -532,16 +510,15 @@
             pltpu.VMEM((rows, TR, LANES), jnp.float32),
         ]
 
-    middle, east2, west2, *sent2, ends = call(
+    middle, east2, west2, ends = call(
         functools.partial(step_kernel, -3, 11, HALO, False),
-        [shape_of(NZ, 14, TR, LANES)] + packs + messages + [shape_of(NZ, 2, TR, LANES)],
-        [],
+        [shape_of(NZ, 14, TR, LANES)] + packs + [shape_of(NZ, 2, TR, LANES)], [],
         [joined, coefs, east, west, *swap(*sent), reaction], scratch(14),
     )
     (out,) = call(
         functools.partial(step_kernel, 0, 8, 3, True),
         [jax.ShapeDtypeStruct((TR * NZ * 8, LANES), jnp.float32)], [],
-        [middle, coefs, east2, west2, *swap(*sent2), reaction, ends], scratch(8),
+        [middle, coefs, east2, west2, *swap(east2, west2), reaction, ends], scratch(8),
     )
     return out.reshape(TR, NZ, 8, LANES)
 

time: 204 us -> 191 us (0.936)
  the two profiles are of different devices: /device:TPU:352 before, /device:TPU:286 now
where the time goes in v4:
time: 191 us; the launch traced here: 190 us
  starting transfers between devices  88.5 us (46%)
  waiting for transfers between devices  66.6 us (35%)
  Pallas kernels  32.7 us (17%)
    ppermute x1, waiting for transfers between devices, transport(): far['B'] = lax.ppermute(far['B'], 'dx', dx_pairs([(0, 0, 1)], [(3, 3, 1)]))  45 us
    pallas_call x8, Pallas kernels, call(): pl.pallas_call(fetched(body, len(scalars), len(arguments)), out_shape=out...  32.7 us
    ppermute x7, starting transfers between devices, gather(): return lax.ppermute(value, 'group', pairs)  17.1 us
    ppermute x1, starting transfers between devices, transport(): lax.ppermute(rim_far, 'dx', swapped + [(b, a) for a, b in swapped])  14.5 us
    ppermute x4, starting transfers between devices, swap(): return (lax.ppermute(east, 'dy', north), lax.ppermute(west, 'dy', south))  14.2 us
    ppermute x1, starting transfers between devices, transport(): far['B'] = lax.ppermute(far['B'], 'dx', dx_pairs([(3, 0, 0)], [(0, 3, 0)]))  11.9 us
    ppermute x4, waiting for transfers between devices, swap(): return (lax.ppermute(east, 'dy', north), lax.ppermute(west, 'dy', south))  11.1 us
    ppermute x1, waiting for transfers between devices, transport(): far['C'] = lax.ppermute(far['C'], 'dx', collect_pairs([(1, 0)], [(2, 3)]))  7.86 us
  transfers between devices with their start and end apart: 26, of which 8 were waited for; matrix products, arithmetic and copies ran while one was open for 0% of the time, Pallas kernels for 2%

profile of v4, /device:TPU:286, one launch (start us, length us, event | category | flops | bytes accessed | tf_op | source)
XLA Modules:
  0.0 189.7 jit_solution(18173602703334485654)
XLA Ops:
  0.0 3.0 %shard_map.73 = (f32[32,6,8,128]{3,2,1,0:T(8,128)S(1)}, f32[32,6,8,128]{3,2,1,0:T(8,128)S(1)}, f32[5,6,8,128]{3,2,1,0:T(8,128)S(1)}, f32[12,6,8,128]{3,2,1,0:T(8...) custom-call(s32[1]{0:T(128)} %bitcast.refs_0_.refs_1_.x_ref, f32[2048,128]{1,0:T(8,128)} %bitcast.4, ...), custom_call_target="tpu_custom_call" | custom-call | tf_op jit(solution)/shard_map/pallas_call | solution.py:63
  3.0 0.7 broadcast_multiply_fusion
  3.7 0.8 tanh_multiply_fusion.refs_5_
  4.6 1.0 shard_map.74
  5.6 1.3 collective-permute-start.12
  6.9 4.5 %collective-permute-start.13 = (f32[9,8,128]{2,1,0:T(8,128)S(1)}, f32[9,8,128]{2,1,0:T(8,128)S(1)}, u32[]{:S(2)}, u32[]{:S(2)}) collective-permute-start(f32[9,8,128]{2,1,0:T(8,128)S(1)} %get-tuple-element.52), channel_id=1, source_target_pairs={{8,0},{16,8},{24,16},{40,32},{48,40},{56,48},{72,64},{80,72},{88,8... | collective-permute-start | bytes 110600 | tf_op jit(solution)/shard_map/ppermute | solution.py:472
  11.4 14.5 %collective-permute-start.14 = (f32[9,8,128]{2,1,0:T(8,128)S(1)}, f32[9,8,128]{2,1,0:T(8,128)S(1)}, u32[]{:S(2)}, u32[]{:S(2)}) collective-permute-start(f32[9,8,128]{2,1,0:T(8,128)S(1)} %get-tuple-element.53), channel_id=1, source_target_pairs={{24,32},{56,64},{88,96},{32,24},{64,56},{96,88},{25,33},{57,65},{8... | collective-permute-start | bytes 110600 | tf_op jit(solution)/shard_map/ppermute | solution.py:474
  25.9 6.1 %collective-permute-start.2 = (f32[5,6,8,128]{3,2,1,0:T(8,128)S(1)}, f32[5,6,8,128]{3,2,1,0:T(8,128)S(1)}, u32[]{:S(2)}, u32[]{:S(2)}) collective-permute-start(f32[5,6,8,128]{3,2,1,0:T(8,128)S(1)} %get-tuple-element.41), channel_id=1, source_target_pairs={{24,56},{56,88},{32,0},{88,120},{64,32},{96,64},{25,57},{57,89},{3... | collective-permute-start | bytes 368648 | tf_op jit(solution)/shard_map/ppermute | solution.py:450
  32.0 1.3 collective-permute-start.9
  33.3 0.0 collective-permute-done.13.east_ref
  33.4 0.3 shard_map.75.refs_0_
  33.6 1.9 %collective-permute-start.18 = (f32[4,72,128]{2,1,0:T(8,128)S(1)}, f32[4,72,128]{2,1,0:T(8,128)S(1)}, u32[]{:S(2)}, u32[]{:S(2)}) collective-permute-start(f32[4,72,128]{2,1,0:T(8,128)S(1)} %shard_map.75.refs_0_), channel_id=1, source_target_pairs={{128,0},{0,128},{384,256},{256,384},{640,512},{512,640},{896,768},... | collective-permute-start | bytes 442376 | tf_op jit(solution)/shard_map/ppermute | solution.py:486
  35.6 3.1 %collective-permute-start.17 = (f32[4,72,128]{2,1,0:T(8,128)S(1)}, f32[4,72,128]{2,1,0:T(8,128)S(1)}, u32[]{:S(2)}, u32[]{:S(2)}) collective-permute-start(f32[4,72,128]{2,1,0:T(8,128)S(1)} %shard_map.75.refs_0_), channel_id=1, source_target_pairs={{512,0},{640,128},{768,256},{896,384},{0,512},{128,640},{256,768},... | collective-permute-start | bytes 442376 | tf_op jit(solution)/shard_map/ppermute | solution.py:486
  38.7 1.3 collective-permute-start.4
  40.0 1.7 collective-permute-done.2
  41.8 2.4 %collective-permute-start.16 = (f32[4,72,128]{2,1,0:T(8,128)S(1)}, f32[4,72,128]{2,1,0:T(8,128)S(1)}, u32[]{:S(2)}, u32[]{:S(2)}) collective-permute-start(f32[4,72,128]{2,1,0:T(8,128)S(1)} %shard_map.75.refs_0_), channel_id=1, source_target_pairs={{768,0},{896,128},{0,256},{128,384},{256,512},{384,640},{512,768},... | collective-permute-start | bytes 442376 | tf_op jit(solution)/shard_map/ppermute | solution.py:486
  44.1 0.0 collective-permute-done.9
  44.2 1.3 collective-permute-start
  45.5 4.6 %collective-permute-start.1 = (f32[32,6,8,128]{3,2,1,0:T(8,128)S(1)}, f32[32,6,8,128]{3,2,1,0:T(8,128)S(1)}, u32[]{:S(2)}, u32[]{:S(2)}) collective-permute-start(f32[32,6,8,128]{3,2,1,0:T(8,128)S(1)} %get-tuple-element.36.lo_ref), channel_id=1, source_target_pairs={{8,0},{16,8},{24,16},{40,32},{48,40},{56,48},{72,64},{80,72},{88,8... | collective-permute-start | bytes 2359304 | tf_op jit(solution)/shard_map/ppermute | solution.py:457
  50.1 0.0 collective-permute-done.17.refs_3_
  50.1 3.5 %collective-permute-start.15 = (f32[4,72,128]{2,1,0:T(8,128)S(1)}, f32[4,72,128]{2,1,0:T(8,128)S(1)}, u32[]{:S(2)}, u32[]{:S(2)}) collective-permute-start(f32[4,72,128]{2,1,0:T(8,128)S(1)} %shard_map.75.refs_0_), channel_id=1, source_target_pairs={{256,0},{384,128},{512,256},{640,384},{768,512},{896,640},{0,768},... | collective-permute-start | bytes 442376 | tf_op jit(solution)/shard_map/ppermute | solution.py:486
  53.6 11.9 %collective-permute-start.7 = (f32[8,6,8,128]{3,2,1,0:T(8,128)S(1)}, f32[8,6,8,128]{3,2,1,0:T(8,128)S(1)}, u32[]{:S(2)}, u32[]{:S(2)}) collective-permute-start(f32[8,6,8,128]{3,2,1,0:T(8,128)S(1)} %get-tuple-element.43), channel_id=1, source_target_pairs={{24,0},{56,32},{32,56},{88,64},{64,88},{96,120},{25,1},{57,33},{33... | collective-permute-start | bytes 589832 | tf_op jit(solution)/shard_map/ppermute | solution.py:448
  65.5 4.5 %collective-permute-start.3 = (f32[5,6,8,128]{3,2,1,0:T(8,128)S(1)}, f32[5,6,8,128]{3,2,1,0:T(8,128)S(1)}, u32[]{:S(2)}, u32[]{:S(2)}) collective-permute-start(f32[5,6,8,128]{3,2,1,0:T(8,128)S(1)} %collective-permute-done.2), channel_id=1, source_target_pairs={{0,24},{56,32},{32,56},{88,64},{64,88},{120,96},{1,25},{57,33},{33... | collective-permute-start | bytes 368648 | tf_op jit(solution)/shard_map/ppermute | solution.py:458
  70.0 0.7 collective-permute-start.5
  70.7 1.9 %collective-permute-start.21 = (f32[4,72,128]{2,1,0:T(8,128)S(1)}, f32[4,72,128]{2,1,0:T(8,128)S(1)}, u32[]{:S(2)}, u32[]{:S(2)}) collective-permute-start(f32[4,72,128]{2,1,0:T(8,128)S(1)} %collective-permute-done.17.refs_3_), channel_id=1, source_target_pairs={{128,0},{0,128},{384,256},{256,384},{640,512},{512,640},{896,768},... | collective-permute-start | bytes 442376 | tf_op jit(solution)/shard_map/ppermute | solution.py:486
  72.6 0.8 collective-permute-done.3.refs_0_
  73.4 1.9 %collective-permute-start.20 = (f32[4,72,128]{2,1,0:T(8,128)S(1)}, f32[4,72,128]{2,1,0:T(8,128)S(1)}, u32[]{:S(2)}, u32[]{:S(2)}) collective-permute-start(f32[4,72,128]{2,1,0:T(8,128)S(1)} %collective-permute-done.16.refs_2_), channel_id=1, source_target_pairs={{128,0},{0,128},{384,256},{256,384},{640,512},{512,640},{896,768},... | collective-permute-start | bytes 442376 | tf_op jit(solution)/shard_map/ppermute | solution.py:486
  75.4 2.4 %collective-permute-start.19 = (f32[4,72,128]{2,1,0:T(8,128)S(1)}, f32[4,72,128]{2,1,0:T(8,128)S(1)}, u32[]{:S(2)}, u32[]{:S(2)}) collective-permute-start(f32[4,72,128]{2,1,0:T(8,128)S(1)} %collective-permute-done.15.refs_1_), channel_id=1, source_target_pairs={{128,0},{0,128},{384,256},{256,384},{640,512},{512,640},{896,768},... | collective-permute-start | bytes 442376 | tf_op jit(solution)/shard_map/ppermute | solution.py:486
  77.8 0.7 collective-permute-start.10
  78.5 1.3 collective-permute-start.6
  79.8 1.9 %collective-permute-start.8 = (f32[8,6,8,128]{3,2,1,0:T(8,128)S(1)}, f32[8,6,8,128]{3,2,1,0:T(8,128)S(1)}, u32[]{:S(2)}, u32[]{:S(2)}) collective-permute-start(f32[8,6,8,128]{3,2,1,0:T(8,128)S(1)} %collective-permute-done.7), channel_id=1, source_target_pairs={{0,32},{32,64},{56,24},{64,96},{88,56},{120,88},{1,33},{33,65},{57... | collective-permute-start | bytes 589832 | tf_op jit(solution)/shard_map/ppermute | solution.py:452
  81.7 1.3 collective-permute-start.11
  83.0 2.7 %shard_map.77 = (f32[32,8,128]{2,1,0:T(8,128)S(1)}, f32[32,8,128]{2,1,0:T(8,128)S(1)}) custom-call(f32[32,6,8,128]{3,2,1,0:T(8,128)S(1)} %get-tuple-element.35.hi_ref, f32[32,6,8,128]{3,2,1,0:T(8,128)S(1)} %get-tuple-element.36.lo_ref), custom_call_target="tpu_custom_call" | custom-call | tf_op jit(solution)/shard_map/pallas_call | solution.py:63
  85.8 0.7 shard_map.76.refs_4_.coef_ref
  86.5 45.0 %collective-permute-done.8.refs_2_ = f32[8,6,8,128]{3,2,1,0:T(8,128)S(1)} collective-permute-done((f32[8,6,8,128]{3,2,1,0:T(8,128)S(1)}, f32[8,6,8,128]{3,2,1,0:T(8,128)S(1)}, u32[]{:S(2)}, u32[]{:S(2)}) %collective-permute-start.8) | collective-permute-done | bytes 196640 | tf_op jit(solution)/shard_map/ppermute | solution.py:452
  131.5 7.9 %collective-permute-done.11.refs_3_ = f32[7,6,8,128]{3,2,1,0:T(8,128)S(1)} collective-permute-done((f32[7,6,8,128]{3,2,1,0:T(8,128)S(1)}, f32[7,6,8,128]{3,2,1,0:T(8,128)S(1)}, u32[]{:S(2)}, u32[]{:S(2)}) %collective-permute-start.11) | collective-permute-done | bytes 172064 | tf_op jit(solution)/shard_map/ppermute | solution.py:460
  139.3 0.0 copy-start
  139.4 2.9 %shard_map.78 = (f32[32,20,8,128]{3,2,1,0:T(8,128)S(1)}, f32[32,8,128]{2,1,0:T(8,128)S(1)}, f32[32,8,128]{2,1,0:T(8,128)S(1)}, f32[32,8,128]{2,1,0:T(8,128)S(1)}, f32[32,8,128]{2,1,0:T(8,128)S(1)}) custom-call(s32[1]{0:T(128)} %bitcast.refs_0_.refs_1_.x_ref, f32[32,6,8,128]{3,2,1,0:T(8,128)S(1)} %get-tuple-element.35.hi_ref, ...), custom_call_target="tpu_custom_call" | custom-call | tf_op jit(solution)/shard_map/pallas_call | solution.py:63
  142.3 9.7 %collective-permute-start.22 = (f32[32,8,128]{2,1,0:T(8,128)S(1)}, f32[32,8,128]{2,1,0:T(8,128)S(1)}, u32[]{:S(2)}, u32[]{:S(2)}) collective-permute-start(f32[32,8,128]{2,1,0:T(8,128)S(1)} %get-tuple-element.59), channel_id=1, source_target_pairs={{0,1},{1,2},{2,3},{3,4},{4,5},{5,6},{6,7},{8,9},{9,10},{10,11},{11... | collective-permute-start | bytes 393224 | tf_op jit(solution)/shard_map/ppermute | solution.py:498
  152.0 1.3 collective-permute-start.23
  153.3 1.2 collective-permute-done.22.from_west_ref
  154.5 4.4 %collective-permute-done.23.from_east_ref = f32[32,8,128]{2,1,0:T(8,128)S(1)} collective-permute-done((f32[32,8,128]{2,1,0:T(8,128)S(1)}, f32[32,8,128]{2,1,0:T(8,128)S(1)}, u32[]{:S(2)}, u32[]{:S(2)}) %collective-permute-start.23) | collective-permute-done | bytes 131104 | tf_op jit(solution)/shard_map/ppermute | solution.py:498
  158.8 14.8 %shard_map.79 = (f32[32,14,8,128]{3,2,1,0:T(8,128)S(1)}, f32[32,8,128]{2,1,0:T(8,128)S(1)}, f32[32,8,128]{2,1,0:T(8,128)S(1)}, f32[32,2,8,128]{3,2,1,0:T(8,128)S(1)}) custom-call(f32[32,20,8,128]{3,2,1,0:T(8,128)S(1)} %get-tuple-element.56.q_ref, f32[32,168,128]{2,1,0:T(8,128)S(1)} %shard_map.76.refs_4_.coef_ref, ...), custom_call_target="tpu_custom_call" | custom-call | tf_op jit(solution)/shard_map/pallas_call | solution.py:63
  173.6 1.9 %collective-permute-start.24 = (f32[32,8,128]{2,1,0:T(8,128)S(1)}, f32[32,8,128]{2,1,0:T(8,128)S(1)}, u32[]{:S(2)}, u32[]{:S(2)}) collective-permute-start(f32[32,8,128]{2,1,0:T(8,128)S(1)} %get-tuple-element.62.east_ref), channel_id=1, source_target_pairs={{0,1},{1,2},{2,3},{3,4},{4,5},{5,6},{6,7},{8,9},{9,10},{10,11},{11... | collective-permute-start | bytes 393224 | tf_op jit(solution)/shard_map/ppermute | solution.py:498
  175.5 1.3 collective-permute-start.25
  176.8 1.2 collective-permute-done.24.from_west_ref
  178.0 4.4 %collective-permute-done.25.from_east_ref = f32[32,8,128]{2,1,0:T(8,128)S(1)} collective-permute-done((f32[32,8,128]{2,1,0:T(8,128)S(1)}, f32[32,8,128]{2,1,0:T(8,128)S(1)}, u32[]{:S(2)}, u32[]{:S(2)}) %collective-permute-start.25) | collective-permute-done | bytes 131104 | tf_op jit(solution)/shard_map/ppermute | solution.py:498
  182.4 7.3 %shard_map.80 = f32[2048,128]{1,0:T(8,128)} custom-call(f32[32,14,8,128]{3,2,1,0:T(8,128)S(1)} %get-tuple-element.61.q_ref, f32[32,168,128]{2,1,0:T(8,128)S(1)} %shard_map.76.refs_4_.coef_ref, f32[32,8,128]{2,1,0:T(8,128)S(1)} %get-tuple-element.62.east_ref, f32[32,8,128]{2,1,0:T(8,128)S(1)} %get-tuple-element.63.west_ref, ...), custom_call_target="tpu_custom_call" | custom-call | tf_op jit(solution)/shard_map/pallas_call | solution.py:63
  (16 shorter events, 0.0 us)
Async XLA Ops:
  5.6 27.8 %collective-permute-start.12 = (f32[9,8,128]{2,1,0:T(8,128)S(1)}, f32[9,8,128]{2,1,0:T(8,128)S(1)}, u32[]{:S(2)}, u32[]{:S(2)}) collective-permute-start(f32[9,8,128]{2,1,0:T(8,128)S(1)} %get-tuple-element.51), channel_id=1, source_target_pairs={{0,8},{8,16},{16,24},{32,40},{40,48},{48,56},{64,72},{72,80},{80,8... | collective-permute-start | bytes 110600 | tf_op jit(solution)/shard_map/ppermute | solution.py:471
  6.9 26.5 %collective-permute-start.13 = (f32[9,8,128]{2,1,0:T(8,128)S(1)}, f32[9,8,128]{2,1,0:T(8,128)S(1)}, u32[]{:S(2)}, u32[]{:S(2)}) collective-permute-start(f32[9,8,128]{2,1,0:T(8,128)S(1)} %get-tuple-element.52), channel_id=1, source_target_pairs={{8,0},{16,8},{24,16},{40,32},{48,40},{56,48},{72,64},{80,72},{88,8... | collective-permute-start | bytes 110600 | tf_op jit(solution)/shard_map/ppermute | solution.py:472
  11.4 21.9 %collective-permute-start.14 = (f32[9,8,128]{2,1,0:T(8,128)S(1)}, f32[9,8,128]{2,1,0:T(8,128)S(1)}, u32[]{:S(2)}, u32[]{:S(2)}) collective-permute-start(f32[9,8,128]{2,1,0:T(8,128)S(1)} %get-tuple-element.53), channel_id=1, source_target_pairs={{24,32},{56,64},{88,96},{32,24},{64,56},{96,88},{25,33},{57,65},{8... | collective-permute-start | bytes 110600 | tf_op jit(solution)/shard_map/ppermute | solution.py:474
  25.9 15.9 %collective-permute-start.2 = (f32[5,6,8,128]{3,2,1,0:T(8,128)S(1)}, f32[5,6,8,128]{3,2,1,0:T(8,128)S(1)}, u32[]{:S(2)}, u32[]{:S(2)}) collective-permute-start(f32[5,6,8,128]{3,2,1,0:T(8,128)S(1)} %get-tuple-element.41), channel_id=1, source_target_pairs={{24,56},{56,88},{32,0},{88,120},{64,32},{96,64},{25,57},{57,89},{3... | collective-permute-start | bytes 368648 | tf_op jit(solution)/shard_map/ppermute | solution.py:450
  32.0 12.1 %collective-permute-start.9 = (f32[7,6,8,128]{3,2,1,0:T(8,128)S(1)}, f32[7,6,8,128]{3,2,1,0:T(8,128)S(1)}, u32[]{:S(2)}, u32[]{:S(2)}) collective-permute-start(f32[7,6,8,128]{3,2,1,0:T(8,128)S(1)} %get-tuple-element.44), channel_id=1, source_target_pairs={{24,8},{56,40},{32,48},{88,72},{64,80},{96,112},{25,9},{57,41},{33... | collective-permute-start | bytes 516104 | tf_op jit(solution)/shard_map/ppermute | solution.py:449
  33.6 11.8 %collective-permute-start.18 = (f32[4,72,128]{2,1,0:T(8,128)S(1)}, f32[4,72,128]{2,1,0:T(8,128)S(1)}, u32[]{:S(2)}, u32[]{:S(2)}) collective-permute-start(f32[4,72,128]{2,1,0:T(8,128)S(1)} %shard_map.75.refs_0_), channel_id=1, source_target_pairs={{128,0},{0,128},{384,256},{256,384},{640,512},{512,640},{896,768},... | collective-permute-start | bytes 442376 | tf_op jit(solution)/shard_map/ppermute | solution.py:486
  35.6 14.5 %collective-permute-start.17 = (f32[4,72,128]{2,1,0:T(8,128)S(1)}, f32[4,72,128]{2,1,0:T(8,128)S(1)}, u32[]{:S(2)}, u32[]{:S(2)}) collective-permute-start(f32[4,72,128]{2,1,0:T(8,128)S(1)} %shard_map.75.refs_0_), channel_id=1, source_target_pairs={{512,0},{640,128},{768,256},{896,384},{0,512},{128,640},{256,768},... | collective-permute-start | bytes 442376 | tf_op jit(solution)/shard_map/ppermute | solution.py:486
  38.7 31.3 %collective-permute-start.4 = (f32[12,6,8,128]{3,2,1,0:T(8,128)S(1)}, f32[12,6,8,128]{3,2,1,0:T(8,128)S(1)}, u32[]{:S(2)}, u32[]{:S(2)}) collective-permute-start(f32[12,6,8,128]{3,2,1,0:T(8,128)S(1)} %get-tuple-element.42), channel_id=1, source_target_pairs={{24,16},{56,48},{32,40},{88,80},{64,72},{96,104},{25,17},{57,49},{... | collective-permute-start | bytes 884744 | tf_op jit(solution)/shard_map/ppermute | solution.py:447
  41.8 11.8 %collective-permute-start.16 = (f32[4,72,128]{2,1,0:T(8,128)S(1)}, f32[4,72,128]{2,1,0:T(8,128)S(1)}, u32[]{:S(2)}, u32[]{:S(2)}) collective-permute-start(f32[4,72,128]{2,1,0:T(8,128)S(1)} %shard_map.75.refs_0_), channel_id=1, source_target_pairs={{768,0},{896,128},{0,256},{128,384},{256,512},{384,640},{512,768},... | collective-permute-start | bytes 442376 | tf_op jit(solution)/shard_map/ppermute | solution.py:486
  44.2 95.2 %collective-permute-start = (f32[32,6,8,128]{3,2,1,0:T(8,128)S(1)}, f32[32,6,8,128]{3,2,1,0:T(8,128)S(1)}, u32[]{:S(2)}, u32[]{:S(2)}) collective-permute-start(f32[32,6,8,128]{3,2,1,0:T(8,128)S(1)} %get-tuple-element.35.hi_ref), channel_id=1, source_target_pairs={{0,8},{8,16},{16,24},{32,40},{40,48},{48,56},{64,72},{72,80},{80,8... | collective-permute-start | bytes 2359304 | tf_op jit(solution)/shard_map/ppermute | solution.py:456
  45.5 93.9 %collective-permute-start.1 = (f32[32,6,8,128]{3,2,1,0:T(8,128)S(1)}, f32[32,6,8,128]{3,2,1,0:T(8,128)S(1)}, u32[]{:S(2)}, u32[]{:S(2)}) collective-permute-start(f32[32,6,8,128]{3,2,1,0:T(8,128)S(1)} %get-tuple-element.36.lo_ref), channel_id=1, source_target_pairs={{8,0},{16,8},{24,16},{40,32},{48,40},{56,48},{72,64},{80,72},{88,8... | collective-permute-start | bytes 2359304 | tf_op jit(solution)/shard_map/ppermute | solution.py:457
  50.1 15.4 %collective-permute-start.15 = (f32[4,72,128]{2,1,0:T(8,128)S(1)}, f32[4,72,128]{2,1,0:T(8,128)S(1)}, u32[]{:S(2)}, u32[]{:S(2)}) collective-permute-start(f32[4,72,128]{2,1,0:T(8,128)S(1)} %shard_map.75.refs_0_), channel_id=1, source_target_pairs={{256,0},{384,128},{512,256},{640,384},{768,512},{896,640},{0,768},... | collective-permute-start | bytes 442376 | tf_op jit(solution)/shard_map/ppermute | solution.py:486
  53.6 17.1 %collective-permute-start.7 = (f32[8,6,8,128]{3,2,1,0:T(8,128)S(1)}, f32[8,6,8,128]{3,2,1,0:T(8,128)S(1)}, u32[]{:S(2)}, u32[]{:S(2)}) collective-permute-start(f32[8,6,8,128]{3,2,1,0:T(8,128)S(1)} %get-tuple-element.43), channel_id=1, source_target_pairs={{24,0},{56,32},{32,56},{88,64},{64,88},{96,120},{25,1},{57,33},{33... | collective-permute-start | bytes 589832 | tf_op jit(solution)/shard_map/ppermute | solution.py:448
  65.5 8.0 %collective-permute-start.3 = (f32[5,6,8,128]{3,2,1,0:T(8,128)S(1)}, f32[5,6,8,128]{3,2,1,0:T(8,128)S(1)}, u32[]{:S(2)}, u32[]{:S(2)}) collective-permute-start(f32[5,6,8,128]{3,2,1,0:T(8,128)S(1)} %collective-permute-done.2), channel_id=1, source_target_pairs={{0,24},{56,32},{32,56},{88,64},{64,88},{120,96},{1,25},{57,33},{33... | collective-permute-start | bytes 368648 | tf_op jit(solution)/shard_map/ppermute | solution.py:458
  70.0 8.5 %collective-permute-start.5 = (f32[12,6,8,128]{3,2,1,0:T(8,128)S(1)}, f32[12,6,8,128]{3,2,1,0:T(8,128)S(1)}, u32[]{:S(2)}, u32[]{:S(2)}) collective-permute-start(f32[12,6,8,128]{3,2,1,0:T(8,128)S(1)} %collective-permute-done.4), channel_id=1, source_target_pairs={{16,48},{48,80},{40,8},{80,112},{72,40},{104,72},{17,49},{49,81},{... | collective-permute-start | bytes 884744 | tf_op jit(solution)/shard_map/ppermute | solution.py:451
  70.7 4.7 %collective-permute-start.21 = (f32[4,72,128]{2,1,0:T(8,128)S(1)}, f32[4,72,128]{2,1,0:T(8,128)S(1)}, u32[]{:S(2)}, u32[]{:S(2)}) collective-permute-start(f32[4,72,128]{2,1,0:T(8,128)S(1)} %collective-permute-done.17.refs_3_), channel_id=1, source_target_pairs={{128,0},{0,128},{384,256},{256,384},{640,512},{512,640},{896,768},... | collective-permute-start | bytes 442376 | tf_op jit(solution)/shard_map/ppermute | solution.py:486
  73.4 4.3 %collective-permute-start.20 = (f32[4,72,128]{2,1,0:T(8,128)S(1)}, f32[4,72,128]{2,1,0:T(8,128)S(1)}, u32[]{:S(2)}, u32[]{:S(2)}) collective-permute-start(f32[4,72,128]{2,1,0:T(8,128)S(1)} %collective-permute-done.16.refs_2_), channel_id=1, source_target_pairs={{128,0},{0,128},{384,256},{256,384},{640,512},{512,640},{896,768},... | collective-permute-start | bytes 442376 | tf_op jit(solution)/shard_map/ppermute | solution.py:486
  75.4 4.4 %collective-permute-start.19 = (f32[4,72,128]{2,1,0:T(8,128)S(1)}, f32[4,72,128]{2,1,0:T(8,128)S(1)}, u32[]{:S(2)}, u32[]{:S(2)}) collective-permute-start(f32[4,72,128]{2,1,0:T(8,128)S(1)} %collective-permute-done.15.refs_1_), channel_id=1, source_target_pairs={{128,0},{0,128},{384,256},{256,384},{640,512},{512,640},{896,768},... | collective-permute-start | bytes 442376 | tf_op jit(solution)/shard_map/ppermute | solution.py:486
  77.8 3.9 %collective-permute-start.10 = (f32[7,6,8,128]{3,2,1,0:T(8,128)S(1)}, f32[7,6,8,128]{3,2,1,0:T(8,128)S(1)}, u32[]{:S(2)}, u32[]{:S(2)}) collective-permute-start(f32[7,6,8,128]{3,2,1,0:T(8,128)S(1)} %collective-permute-done.9), channel_id=1, source_target_pairs={{8,40},{40,72},{48,16},{72,104},{80,48},{112,80},{9,41},{41,73},{4... | collective-permute-start | bytes 516104 | tf_op jit(solution)/shard_map/ppermute | solution.py:453
  78.5 60.9 %collective-permute-start.6 = (f32[12,6,8,128]{3,2,1,0:T(8,128)S(1)}, f32[12,6,8,128]{3,2,1,0:T(8,128)S(1)}, u32[]{:S(2)}, u32[]{:S(2)}) collective-permute-start(f32[12,6,8,128]{3,2,1,0:T(8,128)S(1)} %collective-permute-done.5), channel_id=1, source_target_pairs={{8,24},{48,32},{40,56},{80,64},{72,88},{112,96},{9,25},{49,33},{41... | collective-permute-start | bytes 884744 | tf_op jit(solution)/shard_map/ppermute | solution.py:459
  79.8 51.7 %collective-permute-start.8 = (f32[8,6,8,128]{3,2,1,0:T(8,128)S(1)}, f32[8,6,8,128]{3,2,1,0:T(8,128)S(1)}, u32[]{:S(2)}, u32[]{:S(2)}) collective-permute-start(f32[8,6,8,128]{3,2,1,0:T(8,128)S(1)} %collective-permute-done.7), channel_id=1, source_target_pairs={{0,32},{32,64},{56,24},{64,96},{88,56},{120,88},{1,33},{33,65},{57... | collective-permute-start | bytes 589832 | tf_op jit(solution)/shard_map/ppermute | solution.py:452
  81.7 57.6 %collective-permute-start.11 = (f32[7,6,8,128]{3,2,1,0:T(8,128)S(1)}, f32[7,6,8,128]{3,2,1,0:T(8,128)S(1)}, u32[]{:S(2)}, u32[]{:S(2)}) collective-permute-start(f32[7,6,8,128]{3,2,1,0:T(8,128)S(1)} %collective-permute-done.10), channel_id=1, source_target_pairs={{16,24},{40,32},{48,56},{72,64},{80,88},{104,96},{17,25},{41,33},{... | collective-permute-start | bytes 516104 | tf_op jit(solution)/shard_map/ppermute | solution.py:460
  139.3 19.5 %copy-start = (f32[8,8]{1,0:T(8,128)S(1)}, f32[8,8]{1,0:T(8,128)}, u32[]{:S(2)}) copy-start(f32[8,8]{1,0:T(8,128)} %rates_ref.3) | copy-start | bytes 772
  142.3 12.2 %collective-permute-start.22 = (f32[32,8,128]{2,1,0:T(8,128)S(1)}, f32[32,8,128]{2,1,0:T(8,128)S(1)}, u32[]{:S(2)}, u32[]{:S(2)}) collective-permute-start(f32[32,8,128]{2,1,0:T(8,128)S(1)} %get-tuple-element.59), channel_id=1, source_target_pairs={{0,1},{1,2},{2,3},{3,4},{4,5},{5,6},{6,7},{8,9},{9,10},{10,11},{11... | collective-permute-start | bytes 393224 | tf_op jit(solution)/shard_map/ppermute | solution.py:498
  152.0 6.9 %collective-permute-start.23 = (f32[32,8,128]{2,1,0:T(8,128)S(1)}, f32[32,8,128]{2,1,0:T(8,128)S(1)}, u32[]{:S(2)}, u32[]{:S(2)}) collective-permute-start(f32[32,8,128]{2,1,0:T(8,128)S(1)} %get-tuple-element.60), channel_id=1, source_target_pairs={{1,0},{2,1},{3,2},{4,3},{5,4},{6,5},{7,6},{9,8},{10,9},{11,10},{12... | collective-permute-start | bytes 393224 | tf_op jit(solution)/shard_map/ppermute | solution.py:498
  173.6 4.4 %collective-permute-start.24 = (f32[32,8,128]{2,1,0:T(8,128)S(1)}, f32[32,8,128]{2,1,0:T(8,128)S(1)}, u32[]{:S(2)}, u32[]{:S(2)}) collective-permute-start(f32[32,8,128]{2,1,0:T(8,128)S(1)} %get-tuple-element.62.east_ref), channel_id=1, source_target_pairs={{0,1},{1,2},{2,3},{3,4},{4,5},{5,6},{6,7},{8,9},{9,10},{10,11},{11... | collective-permute-start | bytes 393224 | tf_op jit(solution)/shard_map/ppermute | solution.py:498
  175.5 6.9 %collective-permute-start.25 = (f32[32,8,128]{2,1,0:T(8,128)S(1)}, f32[32,8,128]{2,1,0:T(8,128)S(1)}, u32[]{:S(2)}, u32[]{:S(2)}) collective-permute-start(f32[32,8,128]{2,1,0:T(8,128)S(1)} %get-tuple-element.63.west_ref), channel_id=1, source_target_pairs={{1,0},{2,1},{3,2},{4,3},{5,4},{6,5},{7,6},{9,8},{10,9},{11,10},{12... | collective-permute-start | bytes 393224 | tf_op jit(solution)/shard_map/ppermute | solution.py:498
